TPU v7x, 256 devices: a whole 4x4x8 slice. The times are simulated.
256 devices in a mesh: dp: 128 (over x, y, z), head: 2 (over core).
Axes of the slice: x: 4, y: 4, z: 8, core: 2. Of those that a mesh axis runs over, the one named last changes fastest.
Arguments:
- context: bfloat16 [49152, 2048], P('dp', 'head'), may hold values from -6 to 6
- residual: bfloat16 [49152, 2048], P('dp'), may hold values from -6 to 6
- bias_out: float32 [2048], replicated, may hold values from -3 to 3
- norm_gain: float32 [2048], replicated, may hold values from 0.1 to 1.9
- out_weight: bfloat16 [2048, 2048], P('head', 'dp'), may hold values from -0.125 to 0.125
- cotangent: bfloat16 [49152, 2048], P('dp'), may hold values from -6 to 6
- counts: int32 [128], P('dp'), may hold values from 96 to 384, as said below
- slot_codes: int32 [49152], P('dp'), may hold values from 0 to 383, as said below
Outputs:
- grad_resid: bfloat16 [49152, 2048], P('dp')
- grad_ctx: bfloat16 [49152, 2048], P('dp', 'head')
- grad_wout: float32 [2048, 2048], P('head', 'dp')
Inputs may be any that keep to these rules, and one draw needn't show every extreme that they name: `counts`: one dp index has 384 live rows, every other between 96 and 192. `slot_codes`: the codes of one device are distinct; code c names decoder owner c // 3 and slot c % 3; on every device the first 3 rows go to one owner.
All inputs are finite; a program needn't handle non-finite values.
Results may differ from a plain program's by a relative error of at most 0.0049.
Values may be sent and summed in bfloat16 or wider, within the bound.
No kernel may reach another device: no remote copies, remote signals or barrier semaphores. Data moves between devices by JAX's collectives and lax.ppermute only.
A program may use at most 64 MiB of HBM per device.

v0:
```python
import jax
import jax.numpy as jnp
from jax import lax
from jax.sharding import PartitionSpec as P


def whole_norm_back(projected, residual, bias_out, norm_gain, grad_out):
    summed_in = residual.astype(jnp.float32) + projected + bias_out
    mean_in = jnp.mean(summed_in, axis=-1, keepdims=True)
    centred = summed_in - mean_in
    variance = jnp.mean(centred * centred, axis=-1, keepdims=True)
    inv_std = lax.rsqrt(variance + 1e-05)
    normed = centred * inv_std
    grad_norm = grad_out.astype(jnp.float32) * norm_gain
    first_mean = jnp.mean(grad_norm, axis=-1, keepdims=True)
    second_mean = jnp.mean(grad_norm * normed, axis=-1, keepdims=True)
    return (inv_std * (grad_norm - first_mean - normed * second_mean)).astype(jnp.bfloat16)


def shards(context, residual, bias_out, norm_gain, out_weight, cotangent, counts, slot_codes):
    capacity = slot_codes.shape[0]
    live_mask = jnp.arange(capacity) < counts[0]
    returned = lax.all_to_all(cotangent, "dp", split_axis=0, concat_axis=0, tiled=True)
    picked = jnp.take(returned, slot_codes, axis=0)
    grad_out = jnp.where(live_mask[:, None], picked, jnp.zeros((), picked.dtype))
    whole_weight = lax.all_gather(out_weight, "dp", axis=1, tiled=True)
    partial_proj = jnp.dot(context, whole_weight, preferred_element_type=jnp.float32)
    projected = lax.psum(partial_proj, "head")
    grad_resid = whole_norm_back(projected, residual, bias_out, norm_gain, grad_out)
    grad_ctx_f = lax.dot_general(
        grad_resid, whole_weight, (((1,), (1,)), ((), ())), preferred_element_type=jnp.float32
    )
    grad_ctx = grad_ctx_f.astype(jnp.bfloat16)
    summed_grad = lax.psum_scatter(
        lax.dot_general(
            grad_resid, context, (((0,), (0,)), ((), ())), preferred_element_type=jnp.float32
        ),
        "dp",
        scatter_dimension=0,
        tiled=True,
    )
    grad_wout = (summed_grad / lax.axis_size("dp")).T
    return (grad_resid, grad_ctx, grad_wout)


def solution(mesh):
    return jax.shard_map(
        shards,
        mesh=mesh,
        in_specs=(
            P("dp", "head"),
            P("dp", None),
            P(),
            P(),
            P("head", "dp"),
            P("dp", None),
            P("dp"),
            P("dp"),
        ),
        out_specs=(P("dp", None), P("dp", "head"), P("head", "dp")),
        check_vma=False,
    )
```

profile of v0, /device:TPU:0, one launch (start us, length us, event | category | flops | bytes accessed | tf_op | source)
XLA Modules:
  0.0 932.8 jit_solution(7451474415759570714)
XLA Ops:
  7.2 0.0 copy-start
  7.2 0.0 all-gather.2.cloned.1.call-start
  7.2 0.7 all-gather.2.cloned.1.call-update
  7.9 0.0 all-reduce.2.cloned.1.call-start
  8.0 122.2 %all-gather.2.cloned.1.call-done = bf16[1024,2048]{0,1:T(8,128)(2,1)} async-done(((bf16[1024,16]{0,1:T(8,128)(2,1)}), bf16[1024,2048]{0,1:T(8,128)(2,1)}) %all-gather.2.cloned.1.call-update) | async-done | bytes 4194320 | tf_op jit(solution)/shard_map/all_gather | solution.py:26
  130.2 0.0 copy-done
  130.2 5.7 fusion.2
  135.9 0.0 all-reduce.2.cloned.1.call-update
  135.9 1.4 copy-done.6
  137.3 2.3 all_to_all.8
  139.6 10.0 %all-to-all-start = ((bf16[128,3,2048]{2,1,0:T(4,128)(2,1)}), bf16[128,3,2048]{2,1,0:T(4,128)(2,1)}, u32[]{:S(2)}, u32[]{:S(2)}) async-start(bf16[128,3,2048]{2,1,0:T(4,128)(2,1)} %all_to_all.8), calls=%async_computation | async-start | bytes 4194304 | tf_op jit(solution)/shard_map/all_to_all | solution.py:23
  149.6 0.2 reduce-scatter.2.cloned.1.call-start
  150.6 49.3 %all-to-all-done = bf16[128,3,2048]{2,1,0:T(4,128)(2,1)} async-done(((bf16[128,3,2048]{2,1,0:T(4,128)(2,1)}), bf16[128,3,2048]{2,1,0:T(4,128)(2,1)}, u32[]{:S(2)}, u32[]{:S(2)}) %all-to-all-start) | async-done | bytes 1572896 | tf_op jit(solution)/shard_map/all_to_all | solution.py:23
  199.9 3.9 all_to_all.10
  203.8 0.0 copy-start.7
  203.8 3.1 gather_fusion
  206.9 0.0 copy-done.7
  206.9 3.0 fusion.1
  209.9 0.0 copy-start.8
  210.0 0.7 copy-done.1
  210.7 0.7 multiply_reduce_fusion.1
  211.4 0.1 copy-done.3
  211.5 1.4 fusion
  213.0 1.8 multiply_convert_fusion
  214.7 0.0 copy-start.4
  214.7 1.1 copy-done.4
  215.9 5.6 fusion.3
  221.5 0.0 reduce-scatter.2.cloned.1.call-update
  221.5 1.4 copy-done.5
  222.9 4.9 convolution_convert_fusion
  227.8 697.1 %reduce-scatter.2.cloned.1.call-done = f32[16,1024]{1,0:T(8,128)} async-done(((f32[2048,1024]{1,0:T(8,128)}), f32[16,1024]{1,0:T(8,128)}) %reduce-scatter.2.cloned.1.call-update) | async-done | bytes 65552 | tf_op jit(solution)/shard_map/reduce_scatter | solution.py:34
  924.8 1.5 multiply_bitcast_fusion
  (17 shorter events, 0.1 us)
Async XLA Ops:
  7.2 123.0 %copy-start = (bf16[384,1024]{1,0:T(8,128)(2,1)S(1)}, bf16[384,1024]{1,0:T(8,128)(2,1)}, u32[]{:S(2)}) copy-start(bf16[384,1024]{1,0:T(8,128)(2,1)} %param.8) | copy-start | bytes 2359300
  7.2 123.0 %all-gather.2.cloned.1.call-start = ((), (), s32[]{:S(2)}) async-start(), calls=%async_computation.2 | async-start | bytes 4227072 | tf_op jit(solution)/shard_map/all_gather | solution.py:26
  7.9 199.0 %all-reduce.2.cloned.1.call-start = ((), (), s32[]{:S(2)}) async-start(), calls=%async_computation.3 | async-start | bytes 6291456 | tf_op jit(solution)/shard_map/psum | solution.py:28
  135.9 1.4 copy-start.6
  137.3 13.2 %copy-start.9 = (s32[384]{0:T(512)S(1)}, s32[384]{0:T(512)}, u32[]{:S(2)}) copy-start(s32[384]{0:T(512)} %param.15) | copy-start | bytes 4612
  139.6 60.2 %all-to-all-start = ((bf16[128,3,2048]{2,1,0:T(4,128)(2,1)}), bf16[128,3,2048]{2,1,0:T(4,128)(2,1)}, u32[]{:S(2)}, u32[]{:S(2)}) async-start(bf16[128,3,2048]{2,1,0:T(4,128)(2,1)} %all_to_all.8), calls=%async_computation | async-start | bytes 4194304 | tf_op jit(solution)/shard_map/all_to_all | solution.py:23
  149.6 775.2 %reduce-scatter.2.cloned.1.call-start = ((), (), s32[]{:S(2)}) async-start(), calls=%async_computation.4 | async-start | bytes 8454144 | tf_op jit(solution)/shard_map/reduce_scatter | solution.py:34
  203.8 3.1 copy-start.7
  206.9 3.1 copy-start.2
  206.9 3.8 copy-start.1
  209.9 1.6 copy-start.3
  209.9 1.6 copy-start.8
  214.7 1.1 copy-start.4
  221.5 1.4 copy-start.5
Sparse Core Ops, SparseCore 0:
  11.6 118.5 all-gather.1
  136.0 30.9 all-reduce.1
  221.6 703.1 reduce-scatter.1
where the time goes:
time: 933 us
  waiting for transfers between devices  869 us (93%)
  matrix products  16.2 us (2%)
  between operations  14.5 us (2%)
  local copies, waits for them, and re-layouts  14.1 us (2%)
  starting transfers between devices  10.3 us (1%)
    reduce_scatter x1, waiting for transfers between devices, shards(): lax.psum_scatter(lax.dot_general(grad_resid, context, (((0,), (0,)), ((),...  697 us
    all_gather x1, waiting for transfers between devices, shards(): whole_weight = lax.all_gather(out_weight, 'dp', axis=1, tiled=True)  122 us
    all_to_all x1, waiting for transfers between devices, shards(): lax.all_to_all(cotangent, 'dp', split_axis=0, concat_axis=0, tiled=True)  49.3 us
  transfers between devices with their start and end apart: 4, of which 3 were waited for; matrix products, arithmetic and copies ran while one was open for 1% of the time, Pallas kernels for 0%

commit v1 on v0

v1 whole, which is shorter than its diff:
```python
import jax
import jax.numpy as jnp
from jax import lax
from jax.sharding import Mesh, PartitionSpec as P

F32 = jnp.float32
BF16 = jnp.bfloat16


def norm_back(projected, residual, bias_out, norm_gain, grad_out):
    summed_in = residual.astype(F32) + projected + bias_out
    mean_in = jnp.mean(summed_in, axis=-1, keepdims=True)
    centred = summed_in - mean_in
    variance = jnp.mean(centred * centred, axis=-1, keepdims=True)
    inv_std = lax.rsqrt(variance + 1e-05)
    normed = centred * inv_std
    grad_norm = grad_out.astype(F32) * norm_gain
    first_mean = jnp.mean(grad_norm, axis=-1, keepdims=True)
    second_mean = jnp.mean(grad_norm * normed, axis=-1, keepdims=True)
    return (inv_std * (grad_norm - first_mean - normed * second_mean)).astype(BF16)


def shards(context, residual, bias_out, norm_gain, out_weight, cotangent, counts, slot_codes):
    capacity = slot_codes.shape[0]
    features = residual.shape[1]
    half = features // 2
    core = lax.axis_index("core")
    live_mask = jnp.arange(capacity) < counts[0]
    swap = [(0, 1), (1, 0)]

    mine = lax.dynamic_slice_in_dim(cotangent, core * half, half, axis=1)
    returned = lax.all_to_all(mine, ("x", "y", "z"), split_axis=0, concat_axis=0, tiled=True)
    picked = jnp.take(returned, slot_codes, axis=0)
    picked = jnp.where(live_mask[:, None], picked, jnp.zeros((), picked.dtype))
    other = lax.ppermute(picked, "core", swap)
    grad_out = jnp.where(
        core == 0,
        jnp.concatenate([picked, other], axis=1),
        jnp.concatenate([other, picked], axis=1),
    )

    weight_t = lax.all_gather(out_weight.T, "z", axis=0, tiled=True)
    weight_t = lax.all_gather(weight_t, ("x", "y"), axis=0, tiled=True)

    partial_proj = lax.dot_general(
        context, weight_t, (((1,), (1,)), ((), ())), preferred_element_type=F32
    )
    projected = partial_proj + lax.ppermute(partial_proj, "core", swap)
    grad_resid = norm_back(projected, residual, bias_out, norm_gain, grad_out)

    share = lax.dot_general(
        grad_resid, context, (((0,), (0,)), ((), ())), preferred_element_type=F32
    ).astype(BF16)
    grad_ctx = jnp.dot(grad_resid, weight_t, preferred_element_type=F32).astype(BF16)
    total = None
    for axis in ("x", "y", "z"):
        ways = lax.axis_size(axis)
        share = share.reshape(ways, -1, share.shape[-1])
        got = lax.all_to_all(share, axis, split_axis=0, concat_axis=0)
        total = jnp.sum(got.astype(F32), axis=0)
        share = total.astype(BF16)
    replicas = lax.axis_size("x") * lax.axis_size("y") * lax.axis_size("z")
    grad_wout = (total / replicas).T
    return (grad_resid, grad_ctx, grad_wout)


def solution(mesh):
    torus = Mesh(mesh.devices.reshape(4, 4, 8, 2), ("x", "y", "z", "core"))
    dp = ("x", "y", "z")
    return jax.shard_map(
        shards,
        mesh=torus,
        in_specs=(
            P(dp, "core"),
            P(dp, None),
            P(),
            P(),
            P("core", dp),
            P(dp, None),
            P(dp),
            P(dp),
        ),
        out_specs=(P(dp, None), P(dp, "core"), P("core", dp)),
        check_vma=False,
    )
```

time: 933 us -> 258 us (0.28)
  the two profiles are of different devices: /device:TPU:0 before, /device:TPU:24 now
where the time goes in v1:
time: 258 us; the launch traced here: 256 us
  blocking collectives  105 us (41%)
  waiting for transfers between devices  89.5 us (35%)
  starting transfers between devices  15.8 us (6%)
  between operations  14.9 us (6%)
  matrix products  13.7 us (5%)
  other arithmetic  13.2 us (5%)
  local copies, waits for them, and re-layouts  4.35 us (2%)
    all_to_all x2, blocking collectives, shards(): got = lax.all_to_all(share, axis, split_axis=0, concat_axis=0)  73.9 us
    all_gather x1, waiting for transfers between devices, shards(): weight_t = lax.all_gather(weight_t, ('x', 'y'), axis=0, tiled=True)  55.8 us
    all_gather x1, blocking collectives, shards(): weight_t = lax.all_gather(out_weight.T, 'z', axis=0, tiled=True)  30.8 us
    all_to_all x1, waiting for transfers between devices, shards(): lax.all_to_all(mine, ('x', 'y', 'z'), split_axis=0, concat_axis=0, tiled=...  28.3 us
    all_to_all x1, starting transfers between devices, shards(): lax.all_to_all(mine, ('x', 'y', 'z'), split_axis=0, concat_axis=0, tiled=...  12.3 us
    dot_general x1, matrix products, shards(): lax.dot_general(context, weight_t, (((1,), (1,)), ((), ())), preferred_el...  5.94 us
    reduce_sum x3, other arithmetic, shards(): total = jnp.sum(got.astype(F32), axis=0)  5.44 us
    all_to_all x1, waiting for transfers between devices, shards(): got = lax.all_to_all(share, axis, split_axis=0, concat_axis=0)  5.39 us
  transfers between devices with their start and end apart: 5, of which 3 were waited for; matrix products, arithmetic and copies ran while one was open for 5% of the time, Pallas kernels for 0%

profile of v1, /device:TPU:24, one launch (start us, length us, event | category | flops | bytes accessed | tf_op | source)
XLA Modules:
  0.0 256.2 jit_solution(9456713248749015484)
XLA Ops:
  7.2 0.0 copy-start
  7.2 0.0 all-gather.2.cloned.1.call-start
  7.2 30.8 %all_gather.6 = bf16[128,1024]{1,0:T(8,128)(2,1)} all-gather(bf16[16,1024]{1,0:T(8,128)(2,1)} %bitcast.16), channel_id=1, replica_groups=mesh['x'=4,'y'=4,'z'=8,'core'=2] {'z'}, dimensions={0}, use_global_device_ids=true | all-gather | bytes 294912 | tf_op jit(solution)/shard_map/all_gather | solution.py:42
  38.0 0.0 all-gather.2.cloned.1.call-update
  38.0 55.8 %all-gather.2.cloned.1.call-done = bf16[2048,1024]{1,0:T(8,128)(2,1)} async-done(((bf16[128,1024]{1,0:T(8,128)(2,1)}), bf16[2048,1024]{1,0:T(8,128)(2,1)}) %all-gather.2.cloned.1.call-update) | async-done | bytes 4194320 | tf_op jit(solution)/shard_map/all_gather | solution.py:43
  93.9 5.9 %fusion.2 = f32[384,2048]{1,0:T(8,128)} fusion(bf16[384,1024]{1,0:T(8,128)(2,1)} %param.8, bf16[2048,1024]{1,0:T(8,128)(2,1)} %all-gather.2.cloned.1.call-done), kind=kOutput, calls=%fused_computation.23 | convolution fusion | flops 1610612736 | bytes 8126464 | tf_op jit(solution)/shard_map/dot_general | solution.py:45
  99.8 0.0 collective-permute-start
  99.8 0.1 constant_dynamic-slice_fusion
  99.9 1.3 all_to_all.17
  101.2 12.3 %all-to-all-start = ((bf16[128,3,1024]{2,1,0:T(4,128)(2,1)}), bf16[128,3,1024]{2,1,0:T(4,128)(2,1)S(1)}, u32[]{:S(2)}, u32[]{:S(2)}) async-start(bf16[128,3,1024]{2,1,0:T(4,128)(2,1)} %all_to_all.17), calls=%async_computation | async-start | bytes 2097152 | tf_op jit(solution)/shard_map/all_to_all | solution.py:32
  114.1 28.3 %all-to-all-done = bf16[128,3,1024]{2,1,0:T(4,128)(2,1)S(1)} async-done(((bf16[128,3,1024]{2,1,0:T(4,128)(2,1)}), bf16[128,3,1024]{2,1,0:T(4,128)(2,1)S(1)}, u32[]{:S(2)}, u32[]{:S(2)}) %all-to-all-start) | async-done | bytes 786464 | tf_op jit(solution)/shard_map/all_to_all | solution.py:32
  142.4 0.7 all_to_all.19
  143.1 0.0 copy-start.4
  143.1 2.1 gather_fusion
  145.2 0.2 select_select_fusion
  145.4 0.1 collective-permute-start.1
  145.5 3.9 %fusion.1 = (f32[384]{0:T(512)S(1)}, f32[384,2048]{1,0:T(8,128)S(1)}) fusion(f32[2048]{0:T(1024)S(1)} %copy-done.4, f32[384,2048]{1,0:T(8,128)} %fusion.2, f32[384,2048]{1,0:T(8,128)} %collective-permute-done, bf16[384,2048]{1,0:T(8,128)(2,1)} %param.9), kind=kLoop, calls=%fused_computation.22 | loop fusion | flops 3931776 | bytes 11019776 | tf_op jit(solution)/shard_map/reduce_sum | solution.py:12
  149.4 0.5 multiply_reduce_fusion.1
  149.9 0.2 copy-done.2
  150.1 1.0 fusion
  151.1 0.0 copy-start.5
  151.1 1.6 multiply_convert_fusion
  152.7 0.0 copy-start.1
  152.8 2.4 convolution_convert_fusion
  155.2 53.3 %all_to_all.27 = bf16[4,512,1024]{2,1,0:T(8,128)(2,1)} all-to-all(bf16[4,512,1024]{2,1,0:T(8,128)(2,1)S(1)} %bitcast.14), channel_id=1, replica_groups=mesh['x'=4,'y'=4,'z'=8,'core'=2] {'x'}, dimensions={0} | all-to-all | bytes 8388608 | tf_op jit(solution)/shard_map/all_to_all | solution.py:59
  208.4 4.5 %reduce_sum.73 = bf16[512,1024]{1,0:T(8,128)(2,1)} reduce(bf16[4,512,1024]{2,1,0:T(8,128)(2,1)} %all_to_all.27, bf16[]{:T(256)} %constant.40.clone.1), dimensions={0}, to_apply=%region_4.5 | reduce | flops 1572864 | bytes 5242882 | tf_op jit(solution)/shard_map/reduce_sum | solution.py:60
  212.9 20.7 %all_to_all.28 = bf16[4,128,1024]{2,1,0:T(8,128)(2,1)S(1)} all-to-all(bf16[4,128,1024]{2,1,0:T(8,128)(2,1)} %bitcast.15), channel_id=1, replica_groups=mesh['x'=4,'y'=4,'z'=8,'core'=2] {'y'}, dimensions={0} | all-to-all | bytes 2097152 | tf_op jit(solution)/shard_map/all_to_all | solution.py:59
  233.6 0.9 reduce_sum.74
  234.5 3.4 %all-to-all-start.3 = ((bf16[8,16,1024]{2,1,0:T(8,128)(2,1)}), bf16[8,16,1024]{2,1,0:T(8,128)(2,1)S(1)}, u32[]{:S(2)}, u32[]{:S(2)}) async-start(bf16[8,16,1024]{2,1,0:T(8,128)(2,1)} %bitcast.4), calls=%async_computation.3 | async-start | bytes 524288 | tf_op jit(solution)/shard_map/all_to_all | solution.py:59
  237.9 5.3 %convolution_convert_fusion.1 = bf16[384,1024]{1,0:T(8,128)(2,1)} fusion(bf16[384,2048]{1,0:T(8,128)(2,1)} %copy-done.1, bf16[2048,1024]{1,0:T(8,128)(2,1)} %all-gather.2.cloned.1.call-done), kind=kOutput, calls=%fused_computation.9 | convolution fusion | flops 1611005952 | bytes 6553600 | tf_op jit(solution)/shard_map/dot_general | solution.py:54
  243.3 5.4 %all-to-all-done.3 = bf16[8,16,1024]{2,1,0:T(8,128)(2,1)S(1)} async-done(((bf16[8,16,1024]{2,1,0:T(8,128)(2,1)}), bf16[8,16,1024]{2,1,0:T(8,128)(2,1)S(1)}, u32[]{:S(2)}, u32[]{:S(2)}) %all-to-all-start.3) | async-done | bytes 262176 | tf_op jit(solution)/shard_map/all_to_all | solution.py:59
  248.7 0.6 multiply_bitcast_fusion
  (17 shorter events, 0.1 us)
Async XLA Ops:
  7.2 92.6 %copy-start = (bf16[384,2048]{1,0:T(8,128)(2,1)S(1)}, bf16[384,2048]{1,0:T(8,128)(2,1)}, u32[]{:S(2)}) copy-start(bf16[384,2048]{1,0:T(8,128)(2,1)} %param.13) | copy-start | bytes 4718596
  7.2 86.7 %all-gather.2.cloned.1.call-start = ((), (), s32[]{:S(2)}) async-start(), calls=%async_computation.4 | async-start | bytes 4456448 | tf_op jit(solution)/shard_map/all_gather | solution.py:43
  99.8 14.3 %copy-start.3 = (s32[384]{0:T(512)S(1)}, s32[384]{0:T(512)}, u32[]{:S(2)}) copy-start(s32[384]{0:T(512)} %param.15) | copy-start | bytes 4612
  99.8 45.7 %collective-permute-start = (f32[384,2048]{1,0:T(8,128)}, f32[384,2048]{1,0:T(8,128)}, u32[]{:S(2)}, u32[]{:S(2)}) collective-permute-start(f32[384,2048]{1,0:T(8,128)} %fusion.2), channel_id=1, source_target_pairs={{0,1},{1,0},{2,3},{3,2},{4,5},{5,4},{6,7},{7,6},{8,9},{9,8},{10,11... | collective-permute-start | bytes 9437192 | tf_op jit(solution)/shard_map/ppermute | solution.py:48
  101.2 41.3 %all-to-all-start = ((bf16[128,3,1024]{2,1,0:T(4,128)(2,1)}), bf16[128,3,1024]{2,1,0:T(4,128)(2,1)S(1)}, u32[]{:S(2)}, u32[]{:S(2)}) async-start(bf16[128,3,1024]{2,1,0:T(4,128)(2,1)} %all_to_all.17), calls=%async_computation | async-start | bytes 2097152 | tf_op jit(solution)/shard_map/all_to_all | solution.py:32
  143.1 2.4 copy-start.4
  145.4 4.5 %collective-permute-start.1 = (bf16[384,1024]{1,0:T(8,128)(2,1)S(1)}, bf16[384,1024]{1,0:T(8,128)(2,1)S(1)}, u32[]{:S(2)}, u32[]{:S(2)}) collective-permute-start(bf16[384,1024]{1,0:T(8,128)(2,1)S(1)} %select_select_fusion), channel_id=1, source_target_pairs={{0,1},{1,0},{2,3},{3,2},{4,5},{5,4},{6,7},{7,6},{8,9},{9,8},{10,11... | collective-permute-start | bytes 2359304 | tf_op jit(solution)/shard_map/ppermute | solution.py:35
  149.4 0.7 copy-start.2
  151.1 1.6 copy-start.5
  152.7 2.4 copy-start.1
  234.5 14.1 %all-to-all-start.3 = ((bf16[8,16,1024]{2,1,0:T(8,128)(2,1)}), bf16[8,16,1024]{2,1,0:T(8,128)(2,1)S(1)}, u32[]{:S(2)}, u32[]{:S(2)}) async-start(bf16[8,16,1024]{2,1,0:T(8,128)(2,1)} %bitcast.4), calls=%async_computation.3 | async-start | bytes 524288 | tf_op jit(solution)/shard_map/all_to_all | solution.py:59
Sparse Core Ops, SparseCore 0:
  38.1 55.6 all-gather.1

commit v2 on v1

v2 whole, which is shorter than its diff:
```python
import jax
import jax.numpy as jnp
from jax import lax
from jax.experimental import pallas as pl
from jax.experimental.pallas import tpu as pltpu
from jax.sharding import Mesh, PartitionSpec as P

F32 = jnp.float32
BF16 = jnp.bfloat16
RIGHT = [(i, (i + 1) % 4) for i in range(4)]
LEFT = [(i, (i - 1) % 4) for i in range(4)]


def norm_back(projected, residual, bias_out, norm_gain, grad_out):
    summed_in = residual.astype(F32) + projected + bias_out
    mean_in = jnp.mean(summed_in, axis=-1, keepdims=True)
    centred = summed_in - mean_in
    variance = jnp.mean(centred * centred, axis=-1, keepdims=True)
    inv_std = lax.rsqrt(variance + 1e-05)
    normed = centred * inv_std
    grad_norm = grad_out.astype(F32) * norm_gain
    first_mean = jnp.mean(grad_norm, axis=-1, keepdims=True)
    second_mean = jnp.mean(grad_norm * normed, axis=-1, keepdims=True)
    return (inv_std * (grad_norm - first_mean - normed * second_mean)).astype(BF16)


def ring_gather(piece, axis):
    mid = piece.shape[0] // 2
    before = lax.ppermute(piece, axis, RIGHT)
    after = lax.ppermute(piece, axis, LEFT)
    top = lax.ppermute(before[:mid], axis, RIGHT)
    bottom = lax.ppermute(after[mid:], axis, LEFT)
    return piece, after, top, bottom, before


def ring_reduce(chunk_of, axis):
    far = chunk_of(2).astype(BF16)
    mid = far.shape[0] // 2
    top = lax.ppermute(far[:mid], axis, RIGHT)
    bottom = lax.ppermute(far[mid:], axis, LEFT)
    ahead, behind = chunk_of(1), chunk_of(3)
    ahead = jnp.concatenate([ahead[:mid] + top.astype(F32), ahead[mid:]]).astype(BF16)
    behind = jnp.concatenate([behind[:mid], behind[mid:] + bottom.astype(F32)]).astype(BF16)
    from_before = lax.ppermute(ahead, axis, RIGHT)
    from_after = lax.ppermute(behind, axis, LEFT)
    return chunk_of(0) + from_before.astype(F32) + from_after.astype(F32)


def project_kernel(*refs):
    context_ref, a_refs, b_refs = refs[0], refs[1:6], refs[6:11]
    weight_ref, out_ref = refs[11], refs[12]
    ix, iy = lax.axis_index("x"), lax.axis_index("y")
    steps, lows = (0, 1, 2, 2, 3), (0, 0, 0, 2, 0)
    for ref, step, low in zip(a_refs, steps, lows):
        at = lax.rem(ix + step, 4)
        weight_ref[at, low:low + ref.shape[0], :, 0:512] = ref[...]
    for ref, step, low in zip(b_refs, steps, lows):
        at = lax.rem(iy + step, 4)
        for k in range(ref.shape[0]):
            weight_ref[low + k, at, :, 512:1024] = ref[k]
    for x in range(4):
        block = weight_ref[x].reshape(512, 1024)
        out_ref[:, x * 512:(x + 1) * 512] = lax.dot_general(
            context_ref[...], block, (((1,), (1,)), ((), ())), preferred_element_type=F32
        )


def project(context, a_pieces, b_pieces):
    rows = context.shape[0]
    return pl.pallas_call(
        project_kernel,
        out_shape=(
            jax.ShapeDtypeStruct((4, 4, 128, 1024), BF16),
            jax.ShapeDtypeStruct((rows, 2048), F32),
        ),
        compiler_params=pltpu.CompilerParams(vmem_limit_bytes=40 << 20),
        cost_estimate=pl.CostEstimate(
            flops=2 * rows * 1024 * 2048, bytes_accessed=16 << 20, transcendentals=0
        ),
        name="project",
    )(context, *a_pieces, *b_pieces)


def spread(piece, axes):
    return lax.all_to_all(
        jnp.broadcast_to(piece[None], (32,) + piece.shape), axes, split_axis=0, concat_axis=0
    )


def collect(total, axes):
    share = total.astype(BF16).reshape(32, 16, 512)
    got = lax.all_to_all(share, axes, split_axis=0, concat_axis=0)
    return jnp.sum(got.astype(F32), axis=0)


def shards(context, residual, bias_out, norm_gain, out_weight, cotangent, counts, slot_codes):
    capacity = slot_codes.shape[0]
    features = residual.shape[1]
    half = features // 2
    core = lax.axis_index("core")
    ix, iy = lax.axis_index("x"), lax.axis_index("y")
    live_mask = jnp.arange(capacity) < counts[0]
    swap = [(0, 1), (1, 0)]

    mine = lax.dynamic_slice_in_dim(cotangent, core * half, half, axis=1)
    weight_t = out_weight.T
    mine, weight_t = lax.optimization_barrier((mine, weight_t))
    returned = lax.all_to_all(mine, ("x", "y", "z"), split_axis=0, concat_axis=0, tiled=True)
    a_block = spread(weight_t[:, :512], ("y", "z")).reshape(4, 128, 512)
    b_block = spread(weight_t[:, 512:], ("x", "z")).reshape(4, 128, 512)
    a_pieces = ring_gather(a_block, "x")
    b_pieces = ring_gather(b_block, "y")
    a_pieces, b_pieces, returned = lax.optimization_barrier((a_pieces, b_pieces, returned))

    weight_t, partial_proj = project(context, a_pieces, b_pieces)
    weight_t = weight_t.reshape(2048, 1024)
    picked = returned.at[slot_codes].get(mode="promise_in_bounds")
    picked = jnp.where(live_mask[:, None], picked, jnp.zeros((), picked.dtype))
    other = lax.ppermute(picked, "core", swap)
    grad_out = jnp.where(
        core == 0,
        jnp.concatenate([picked, other], axis=1),
        jnp.concatenate([other, picked], axis=1),
    )
    projected = partial_proj + lax.ppermute(partial_proj, "core", swap)
    grad_resid = norm_back(projected, residual, bias_out, norm_gain, grad_out)

    def product(columns, left):
        return lax.dot_general(
            columns, left, (((0,), (0,)), ((), ())), preferred_element_type=F32
        )

    def a_chunk(step):
        at = lax.rem(ix + step, 4)
        return product(lax.dynamic_slice_in_dim(grad_resid, at * 512, 512, axis=1), context[:, :512])

    def b_chunk(step):
        at = lax.rem(iy + step, 4)
        strips = [
            lax.dynamic_slice_in_dim(grad_resid, (x * 4 + at) * 128, 128, axis=1) for x in range(4)
        ]
        return product(jnp.concatenate(strips, axis=1), context[:, 512:])

    a_sum = ring_reduce(a_chunk, "x")
    b_sum = ring_reduce(b_chunk, "y")

    total = jnp.concatenate(
        [collect(a_sum, ("y", "z")), collect(b_sum, ("x", "z"))], axis=1
    )
    replicas = lax.axis_size("x") * lax.axis_size("y") * lax.axis_size("z")
    grad_wout = (total / replicas).T
    grad_ctx = jnp.dot(grad_resid, weight_t, preferred_element_type=F32).astype(BF16)
    return (grad_resid, grad_ctx, grad_wout)


def solution(mesh):
    torus = Mesh(mesh.devices.reshape(4, 4, 8, 2), ("x", "y", "z", "core"))
    dp = ("x", "y", "z")
    return jax.shard_map(
        shards,
        mesh=torus,
        in_specs=(
            P(dp, "core"),
            P(dp, None),
            P(),
            P(),
            P("core", dp),
            P(dp, None),
            P(dp),
            P(dp),
        ),
        out_specs=(P(dp, None), P(dp, "core"), P("core", dp)),
        check_vma=False,
    )
```

time: 258 us -> 210 us (0.81)
  blocking collectives: 105 us -> 26.4 us
  starting transfers between devices: 15.8 us -> 58.4 us
  waiting for transfers between devices: 89.5 us -> 70.2 us
  local copies, waits for them, and re-layouts: 4.35 us -> 22.6 us
  between operations: 14.9 us -> 1.69 us
  Pallas kernels: 0 us -> 5.11 us
  matrix products: 13.7 us -> 10.1 us
    all_gather x1 -> x0, waiting for transfers between devices: 55.8 us -> none  [shards(): weight_t = lax.all_gather(weight_t, ('x', 'y'), axis=0, tiled=True)]
    all_to_all x2 -> x1, blocking collectives: 73.9 us -> 26.4 us  [spread(): lax.all_to_all(jnp.broadcast_to(piece[None], (32,) + piece.shape), axes,...]
    ppermute x0 -> x16, waiting for transfers between devices: none -> 44.9 us  [the longest x2 18 us: ring_gather(): before = lax.ppermute(piece, axis, RIGHT)]
    all_gather x1 -> x0, blocking collectives: 30.8 us -> none  [shards(): weight_t = lax.all_gather(out_weight.T, 'z', axis=0, tiled=True)]
    all_to_all x1, waiting for transfers between devices: 28.3 us -> 0.01 us  [shards(): lax.all_to_all(mine, ('x', 'y', 'z'), split_axis=0, concat_axis=0, tiled=...]
    all_to_all x1 -> x3, starting transfers between devices: 3.41 us -> 25.9 us  [the longest x2 18.8 us: collect(): got = lax.all_to_all(share, axes, split_axis=0, concat_axis=0)]
    ppermute x0 -> x16, starting transfers between devices: none -> 22.3 us  [the longest x2 5.38 us: ring_reduce(): bottom = lax.ppermute(far[mid:], axis, LEFT)]
    all_to_all x1 -> x3, waiting for transfers between devices: 5.39 us -> 24.8 us  [the longest x1 15.2 us: spread(): lax.all_to_all(jnp.broadcast_to(piece[None], (32,) + piece.shape), axes,...]
  transfers between devices with their start and end apart: 5 -> 22, of which waited for: 3 -> 9; matrix products, arithmetic and copies ran while one was open for 5% -> 14% of each run, Pallas kernels for 0% -> 0%
where the time goes in v2:
time: 210 us; the launch traced here: 208 us
  waiting for transfers between devices  70.2 us (33%)
  starting transfers between devices  58.4 us (28%)
  blocking collectives  26.4 us (13%)
  local copies, waits for them, and re-layouts  22.6 us (11%)
  other arithmetic  13.5 us (6%)
  matrix products  10.1 us (5%)
  Pallas kernels  5.11 us (2%)
    all_to_all x1, blocking collectives, spread(): lax.all_to_all(jnp.broadcast_to(piece[None], (32,) + piece.shape), axes,...  26.4 us
    all_to_all x2, starting transfers between devices, collect(): got = lax.all_to_all(share, axes, split_axis=0, concat_axis=0)  18.8 us
    ppermute x2, waiting for transfers between devices, ring_gather(): before = lax.ppermute(piece, axis, RIGHT)  18 us
    all_to_all x1, waiting for transfers between devices, spread(): lax.all_to_all(jnp.broadcast_to(piece[None], (32,) + piece.shape), axes,...  15.2 us
    ppermute x2, waiting for transfers between devices, ring_reduce(): from_after = lax.ppermute(behind, axis, LEFT)  15.1 us
    all_to_all x1, starting transfers between devices, shards(): lax.all_to_all(mine, ('x', 'y', 'z'), split_axis=0, concat_axis=0, tiled=...  9.68 us
    all_to_all x2, waiting for transfers between devices, collect(): got = lax.all_to_all(share, axes, split_axis=0, concat_axis=0)  9.62 us
    unnamed x32, local copies, waits for them, and re-layouts  7.9 us
  transfers between devices with their start and end apart: 22, of which 9 were waited for; matrix products, arithmetic and copies ran while one was open for 14% of the time, Pallas kernels for 0%

profile of v2, /device:TPU:24, one launch (start us, length us, event | category | flops | bytes accessed | tf_op | source)
XLA Modules:
  0.0 208.1 jit_solution(12996250674916001185)
XLA Ops:
  0.7 1.4 copy-done
  2.9 26.4 %all_to_all.32 = bf16[32,16,512]{2,1,0:T(8,128)(2,1)S(1)} all-to-all(bf16[32,16,512]{2,1,0:T(8,128)(2,1)S(1)} %broadcast_in_dim.18), channel_id=1, replica_groups=mesh['x'=4,'y'=4,'z'=8,'core'=2] {'y','z'}, dimensions={0} | all-to-all | bytes 1048576 | tf_op jit(solution)/shard_map/all_to_all | solution.py:85
  30.2 7.1 %all-to-all-start.1 = ((bf16[32,16,512]{2,1,0:T(8,128)(2,1)}), bf16[32,16,512]{2,1,0:T(8,128)(2,1)S(1)}, u32[]{:S(2)}, u32[]{:S(2)}) async-start(bf16[32,16,512]{2,1,0:T(8,128)(2,1)} %broadcast_in_dim.19), calls=%async_computation.1 | async-start | bytes 1048576 | tf_op jit(solution)/shard_map/all_to_all | solution.py:85
  37.3 1.3 all_to_all.22
  38.6 15.2 %all-to-all-done.1 = bf16[32,16,512]{2,1,0:T(8,128)(2,1)S(1)} async-done(((bf16[32,16,512]{2,1,0:T(8,128)(2,1)}), bf16[32,16,512]{2,1,0:T(8,128)(2,1)S(1)}, u32[]{:S(2)}, u32[]{:S(2)}) %all-to-all-start.1) | async-done | bytes 524320 | tf_op jit(solution)/shard_map/all_to_all | solution.py:85
  53.8 9.7 %all-to-all-start.2 = ((bf16[128,3,1024]{2,1,0:T(4,128)(2,1)}), bf16[128,3,1024]{2,1,0:T(4,128)(2,1)}, u32[]{:S(2)}, u32[]{:S(2)}) async-start(bf16[128,3,1024]{2,1,0:T(4,128)(2,1)} %all_to_all.22), calls=%async_computation.2 | async-start | bytes 2097152 | tf_op jit(solution)/shard_map/all_to_all | solution.py:108
  63.5 1.8 collective-permute-start.1
  65.3 1.7 collective-permute-start
  67.7 1.3 collective-permute-start.4
  69.0 18.0 %collective-permute-done.1.refs_5_ = bf16[4,128,512]{2,1,0:T(8,128)(2,1)S(1)} collective-permute-done((bf16[4,128,512]{2,1,0:T(8,128)(2,1)S(1)}, bf16[4,128,512]{2,1,0:T(8,128)(2,1)S(1)}, u32[]{:S(2)}, u32[]{:S(2)}) %collective-permute-start.1) | collective-permute-done | bytes 524320 | tf_op jit(solution)/shard_map/ppermute | solution.py:29
  88.5 3.2 %collective-permute-start.3 = (bf16[2,128,512]{2,1,0:T(8,128)(2,1)}, bf16[2,128,512]{2,1,0:T(8,128)(2,1)}, u32[]{:S(2)}, u32[]{:S(2)}) collective-permute-start(bf16[2,128,512]{2,1,0:T(8,128)(2,1)} %slice.93), channel_id=1, source_target_pairs={{0,192},{64,0},{128,64},{192,128},{1,193},{65,1},{129,65},{193,129... | collective-permute-start | bytes 786440 | tf_op jit(solution)/shard_map/ppermute | solution.py:32
  95.5 3.2 %all_to_all.24 = bf16[384,1024]{1,0:T(8,128)(2,1)} reshape(bf16[128,3,1024]{2,1,0:T(4,128)(2,1)} %all-to-all-done.2) | data formatting | bytes 1572864 | tf_op jit(solution)/shard_map/all_to_all | solution.py:108
  99.3 3.1 %collective-permute-done.7.refs_9_ = bf16[2,128,512]{2,1,0:T(8,128)(2,1)} collective-permute-done((bf16[2,128,512]{2,1,0:T(8,128)(2,1)}, bf16[2,128,512]{2,1,0:T(8,128)(2,1)}, u32[]{:S(2)}, u32[]{:S(2)}) %collective-permute-start.7) | collective-permute-done | bytes 262176 | tf_op jit(solution)/shard_map/ppermute | solution.py:32
  106.5 5.1 %project.1 = (bf16[4,4,128,1024]{3,2,1,0:T(8,128)(2,1)S(1)}, f32[384,2048]{1,0:T(8,128)}) custom-call(bf16[384,1024]{1,0:T(8,128)(2,1)S(1)} %copy-done.1, bf16[4,128,512]{2,1,0:T(8,128)(2,1)S(1)} %bitcast.14, bf16[4,128,512]{2,1,0:T(8,128)(2,1)S(1)} %copy-done.5, bf16[2,128,512]{2,1,0:T(8,128)(2,1)} %collective-permute-done.2.refs_3_, ...), custom_call_target="tpu_custom_call" | custom-call | flops 1610612736 | bytes 16777216 | tf_op jit(solution)/shard_map/project/pallas_call | solution.py:70
  111.6 2.0 copy-done.10
  114.3 4.0 %gather_fusion = bf16[384,1024]{1,0:T(8,128)(2,1)S(1)} fusion(bf16[384,1024]{1,0:T(8,128)(2,1)} %all_to_all.24, s32[1024]{0:T(1024)S(1)} %pad_clamp_fusion), kind=kCustom, calls=%fused_computation | custom fusion | bytes 1574400 | tf_op jit(solution)/shard_map/gather | solution.py:117
  119.6 3.9 %fusion.60 = (f32[384]{0:T(512)S(1)}, f32[384,2048]{1,0:T(8,128)S(1)}) fusion(f32[2048]{0:T(1024)S(1)} %copy-done.14, f32[384,2048]{1,0:T(8,128)} %get-tuple-element.30, f32[384,2048]{1,0:T(8,128)} %collective-permute-done.8, bf16[384,2048]{1,0:T(8,128)(2,1)} %param.9), kind=kLoop, calls=%fused_computation.112 | loop fusion | flops 3931776 | bytes 11019776 | tf_op jit(solution)/shard_map/reduce_sum | solution.py:16
  125.2 1.6 multiply_convert_fusion
  128.0 3.3 %collective-permute-start.12 = (bf16[256,512]{1,0:T(8,128)(2,1)S(1)}, bf16[256,512]{1,0:T(8,128)(2,1)S(1)}, u32[]{:S(2)}, u32[]{:S(2)}) collective-permute-start(bf16[256,512]{1,0:T(8,128)(2,1)S(1)} %get-tuple-element.54), channel_id=1, source_target_pairs={{0,192},{64,0},{128,64},{192,128},{1,193},{65,1},{129,65},{193,129... | collective-permute-start | bytes 786440 | tf_op jit(solution)/shard_map/ppermute | solution.py:40
  131.8 1.2 constant_dynamic-slice_fusion.11
  134.1 2.1 %collective-permute-start.16 = (bf16[256,512]{1,0:T(8,128)(2,1)S(1)}, bf16[256,512]{1,0:T(8,128)(2,1)}, u32[]{:S(2)}, u32[]{:S(2)}) collective-permute-start(bf16[256,512]{1,0:T(8,128)(2,1)S(1)} %get-tuple-element.56), channel_id=1, source_target_pairs={{0,48},{16,0},{32,16},{48,32},{1,49},{17,1},{33,17},{49,33},{2,50}... | collective-permute-start | bytes 786440 | tf_op jit(solution)/shard_map/ppermute | solution.py:40
  137.4 3.6 %collective-permute-start.13 = (bf16[512,512]{1,0:T(8,128)(2,1)S(1)}, bf16[512,512]{1,0:T(8,128)(2,1)S(1)}, u32[]{:S(2)}, u32[]{:S(2)}) collective-permute-start(bf16[512,512]{1,0:T(8,128)(2,1)S(1)} %pad_maximum_fusion.1), channel_id=1, source_target_pairs={{0,192},{64,0},{128,64},{192,128},{1,193},{65,1},{129,65},{193,129... | collective-permute-start | bytes 1572872 | tf_op jit(solution)/shard_map/ppermute | solution.py:45
  142.4 1.3 collective-permute-start.15
  143.8 7.8 %collective-permute-done.11 = bf16[512,512]{1,0:T(8,128)(2,1)S(1)} collective-permute-done((bf16[512,512]{1,0:T(8,128)(2,1)S(1)}, bf16[512,512]{1,0:T(8,128)(2,1)S(1)}, u32[]{:S(2)}, u32[]{:S(2)}) %collective-permute-start.11) | collective-permute-done | bytes 524320 | tf_op jit(solution)/shard_map/ppermute | solution.py:44
  152.7 9.6 %all-to-all-start.3 = ((bf16[32,16,512]{2,1,0:T(8,128)(2,1)}), bf16[32,16,512]{2,1,0:T(8,128)(2,1)S(1)}, u32[]{:S(2)}, u32[]{:S(2)}) async-start(bf16[32,16,512]{2,1,0:T(8,128)(2,1)} %bitcast.5), calls=%async_computation.3 | async-start | bytes 1048576 | tf_op jit(solution)/shard_map/all_to_all | solution.py:92
  162.3 1.2 fusion.1
  164.4 1.4 fusion.5
  165.8 15.1 %collective-permute-done.17 = bf16[512,512]{1,0:T(8,128)(2,1)S(1)} collective-permute-done((bf16[512,512]{1,0:T(8,128)(2,1)S(1)}, bf16[512,512]{1,0:T(8,128)(2,1)S(1)}, u32[]{:S(2)}, u32[]{:S(2)}) %collective-permute-start.17) | collective-permute-done | bytes 524320 | tf_op jit(solution)/shard_map/ppermute | solution.py:45
  181.0 2.1 add_convert_fusion
  183.1 9.2 %all-to-all-start.4 = ((bf16[32,16,512]{2,1,0:T(8,128)(2,1)}), bf16[32,16,512]{2,1,0:T(8,128)(2,1)S(1)}, u32[]{:S(2)}, u32[]{:S(2)}) async-start(bf16[32,16,512]{2,1,0:T(8,128)(2,1)} %bitcast.6), calls=%async_computation.4 | async-start | bytes 1048576 | tf_op jit(solution)/shard_map/all_to_all | solution.py:92
  192.3 5.3 %convolution_convert_fusion = bf16[384,1024]{1,0:T(8,128)(2,1)} fusion(bf16[384,2048]{1,0:T(8,128)(2,1)} %copy-done.11, bf16[2048,1024]{1,0:T(8,128)(2,1)} %bitcast.18), kind=kOutput, calls=%fused_computation.8 | convolution fusion | flops 1611005952 | bytes 6553600 | tf_op jit(solution)/shard_map/dot_general | solution.py:152
  197.7 9.6 %all-to-all-done.4 = bf16[32,16,512]{2,1,0:T(8,128)(2,1)S(1)} async-done(((bf16[32,16,512]{2,1,0:T(8,128)(2,1)}), bf16[32,16,512]{2,1,0:T(8,128)(2,1)S(1)}, u32[]{:S(2)}, u32[]{:S(2)}) %all-to-all-start.4) | async-done | bytes 524320 | tf_op jit(solution)/shard_map/all_to_all | solution.py:92
  (97 shorter events, 23.5 us)
Async XLA Ops:
  0.6 1.4 copy-start
  30.2 23.6 %all-to-all-start.1 = ((bf16[32,16,512]{2,1,0:T(8,128)(2,1)}), bf16[32,16,512]{2,1,0:T(8,128)(2,1)S(1)}, u32[]{:S(2)}, u32[]{:S(2)}) async-start(bf16[32,16,512]{2,1,0:T(8,128)(2,1)} %broadcast_in_dim.19), calls=%async_computation.1 | async-start | bytes 1048576 | tf_op jit(solution)/shard_map/all_to_all | solution.py:85
  38.6 63.8 %copy-start.1 = (bf16[384,1024]{1,0:T(8,128)(2,1)S(1)}, bf16[384,1024]{1,0:T(8,128)(2,1)}, u32[]{:S(2)}) copy-start(bf16[384,1024]{1,0:T(8,128)(2,1)} %refs_0_.1) | copy-start | bytes 2359300
  53.8 41.7 %all-to-all-start.2 = ((bf16[128,3,1024]{2,1,0:T(4,128)(2,1)}), bf16[128,3,1024]{2,1,0:T(4,128)(2,1)}, u32[]{:S(2)}, u32[]{:S(2)}) async-start(bf16[128,3,1024]{2,1,0:T(4,128)(2,1)} %all_to_all.22), calls=%async_computation.2 | async-start | bytes 2097152 | tf_op jit(solution)/shard_map/all_to_all | solution.py:108
  63.5 23.5 %collective-permute-start.1 = (bf16[4,128,512]{2,1,0:T(8,128)(2,1)S(1)}, bf16[4,128,512]{2,1,0:T(8,128)(2,1)S(1)}, u32[]{:S(2)}, u32[]{:S(2)}) collective-permute-start(bf16[4,128,512]{2,1,0:T(8,128)(2,1)S(1)} %bitcast.12), channel_id=1, source_target_pairs={{0,64},{64,128},{128,192},{192,0},{1,65},{65,129},{129,193},{193,1... | collective-permute-start | bytes 1572872 | tf_op jit(solution)/shard_map/ppermute | solution.py:29
  65.3 22.5 %collective-permute-start = (bf16[4,128,512]{2,1,0:T(8,128)(2,1)S(1)}, bf16[4,128,512]{2,1,0:T(8,128)(2,1)S(1)}, u32[]{:S(2)}, u32[]{:S(2)}) collective-permute-start(bf16[4,128,512]{2,1,0:T(8,128)(2,1)S(1)} %bitcast.13), channel_id=1, source_target_pairs={{0,192},{64,0},{128,64},{192,128},{1,193},{65,1},{129,65},{193,129... | collective-permute-start | bytes 1572872 | tf_op jit(solution)/shard_map/ppermute | solution.py:30
  67.0 24.8 %collective-permute-start.5 = (bf16[4,128,512]{2,1,0:T(8,128)(2,1)S(1)}, bf16[4,128,512]{2,1,0:T(8,128)(2,1)S(1)}, u32[]{:S(2)}, u32[]{:S(2)}) collective-permute-start(bf16[4,128,512]{2,1,0:T(8,128)(2,1)S(1)} %bitcast.15), channel_id=1, source_target_pairs={{0,16},{16,32},{32,48},{48,0},{1,17},{17,33},{33,49},{49,1},{2,18}... | collective-permute-start | bytes 1572872 | tf_op jit(solution)/shard_map/ppermute | solution.py:29
  67.7 25.8 %collective-permute-start.4 = (bf16[4,128,512]{2,1,0:T(8,128)(2,1)S(1)}, bf16[4,128,512]{2,1,0:T(8,128)(2,1)S(1)}, u32[]{:S(2)}, u32[]{:S(2)}) collective-permute-start(bf16[4,128,512]{2,1,0:T(8,128)(2,1)S(1)} %bitcast.16), channel_id=1, source_target_pairs={{0,48},{16,0},{32,16},{48,32},{1,49},{17,1},{33,17},{49,33},{2,50}... | collective-permute-start | bytes 1572872 | tf_op jit(solution)/shard_map/ppermute | solution.py:30
  87.0 6.6 %copy-start.2 = (bf16[4,128,512]{2,1,0:T(8,128)(2,1)}, bf16[4,128,512]{2,1,0:T(8,128)(2,1)S(1)}, u32[]{:S(2)}) copy-start(bf16[4,128,512]{2,1,0:T(8,128)(2,1)S(1)} %collective-permute-done.1.refs_5_) | copy-start | bytes 1572868
  87.7 11.0 %collective-permute-start.2 = (bf16[2,128,512]{2,1,0:T(8,128)(2,1)}, bf16[2,128,512]{2,1,0:T(8,128)(2,1)}, u32[]{:S(2)}, u32[]{:S(2)}) collective-permute-start(bf16[2,128,512]{2,1,0:T(8,128)(2,1)} %slice.92), channel_id=1, source_target_pairs={{0,64},{64,128},{128,192},{192,0},{1,65},{65,129},{129,193},{193,1... | collective-permute-start | bytes 786440 | tf_op jit(solution)/shard_map/ppermute | solution.py:31
  87.8 6.6 %copy-start.4 = (bf16[4,128,512]{2,1,0:T(8,128)(2,1)}, bf16[4,128,512]{2,1,0:T(8,128)(2,1)S(1)}, u32[]{:S(2)}) copy-start(bf16[4,128,512]{2,1,0:T(8,128)(2,1)S(1)} %collective-permute-done.refs_2_) | copy-start | bytes 1572868
  88.5 10.2 %collective-permute-start.3 = (bf16[2,128,512]{2,1,0:T(8,128)(2,1)}, bf16[2,128,512]{2,1,0:T(8,128)(2,1)}, u32[]{:S(2)}, u32[]{:S(2)}) collective-permute-start(bf16[2,128,512]{2,1,0:T(8,128)(2,1)} %slice.93), channel_id=1, source_target_pairs={{0,192},{64,0},{128,64},{192,128},{1,193},{65,1},{129,65},{193,129... | collective-permute-start | bytes 786440 | tf_op jit(solution)/shard_map/ppermute | solution.py:32
  91.8 2.6 %copy-start.6 = (bf16[4,128,512]{2,1,0:T(8,128)(2,1)}, bf16[4,128,512]{2,1,0:T(8,128)(2,1)S(1)}, u32[]{:S(2)}) copy-start(bf16[4,128,512]{2,1,0:T(8,128)(2,1)S(1)} %collective-permute-done.5.refs_10_) | copy-start | bytes 1572868
  92.6 6.7 %collective-permute-start.6 = (bf16[2,128,512]{2,1,0:T(8,128)(2,1)}, bf16[2,128,512]{2,1,0:T(8,128)(2,1)}, u32[]{:S(2)}, u32[]{:S(2)}) collective-permute-start(bf16[2,128,512]{2,1,0:T(8,128)(2,1)} %slice.94), channel_id=1, source_target_pairs={{0,16},{16,32},{32,48},{48,0},{1,17},{17,33},{33,49},{49,1},{2,18}... | collective-permute-start | bytes 786440 | tf_op jit(solution)/shard_map/ppermute | solution.py:31
  94.5 7.9 %collective-permute-start.7 = (bf16[2,128,512]{2,1,0:T(8,128)(2,1)}, bf16[2,128,512]{2,1,0:T(8,128)(2,1)}, u32[]{:S(2)}, u32[]{:S(2)}) collective-permute-start(bf16[2,128,512]{2,1,0:T(8,128)(2,1)} %slice.95), channel_id=1, source_target_pairs={{0,48},{16,0},{32,16},{48,32},{1,49},{17,1},{33,17},{49,33},{2,50}... | collective-permute-start | bytes 786440 | tf_op jit(solution)/shard_map/ppermute | solution.py:32
  95.5 18.8 %copy-start.15 = (s32[384]{0:T(512)S(1)}, s32[384]{0:T(512)}, u32[]{:S(2)}) copy-start(s32[384]{0:T(512)} %param.15) | copy-start | bytes 4612
  111.6 2.0 copy-start.10
  113.6 6.0 %collective-permute-start.8 = (f32[384,2048]{1,0:T(8,128)}, f32[384,2048]{1,0:T(8,128)}, u32[]{:S(2)}, u32[]{:S(2)}) collective-permute-start(f32[384,2048]{1,0:T(8,128)} %get-tuple-element.30), channel_id=1, source_target_pairs={{0,1},{1,0},{2,3},{3,2},{4,5},{5,4},{6,7},{7,6},{8,9},{9,8},{10,11... | collective-permute-start | bytes 9437192 | tf_op jit(solution)/shard_map/ppermute | solution.py:125
  114.3 5.3 %copy-start.14 = (f32[2048]{0:T(1024)S(1)}, f32[2048]{0:T(1024)}, u32[]{:S(2)}) copy-start(f32[2048]{0:T(1024)} %param.10) | copy-start | bytes 24580
  118.5 5.5 %collective-permute-start.9 = (bf16[384,1024]{1,0:T(8,128)(2,1)S(1)}, bf16[384,1024]{1,0:T(8,128)(2,1)S(1)}, u32[]{:S(2)}, u32[]{:S(2)}) collective-permute-start(bf16[384,1024]{1,0:T(8,128)(2,1)S(1)} %broadcast_select_fusion), channel_id=1, source_target_pairs={{0,1},{1,0},{2,3},{3,2},{4,5},{5,4},{6,7},{7,6},{8,9},{9,8},{10,11... | collective-permute-start | bytes 2359304 | tf_op jit(solution)/shard_map/ppermute | solution.py:119
  126.9 14.2 %copy-start.11 = (bf16[384,2048]{1,0:T(8,128)(2,1)}, bf16[384,2048]{1,0:T(8,128)(2,1)S(1)}, u32[]{:S(2)}) copy-start(bf16[384,2048]{1,0:T(8,128)(2,1)S(1)} %multiply_convert_fusion) | copy-start | bytes 4718596
  127.4 9.6 %collective-permute-start.10 = (bf16[256,512]{1,0:T(8,128)(2,1)S(1)}, bf16[256,512]{1,0:T(8,128)(2,1)S(1)}, u32[]{:S(2)}, u32[]{:S(2)}) collective-permute-start(bf16[256,512]{1,0:T(8,128)(2,1)S(1)} %get-tuple-element.53), channel_id=1, source_target_pairs={{0,64},{64,128},{128,192},{192,0},{1,65},{65,129},{129,193},{193,1... | collective-permute-start | bytes 786440 | tf_op jit(solution)/shard_map/ppermute | solution.py:39
  128.0 9.2 %collective-permute-start.12 = (bf16[256,512]{1,0:T(8,128)(2,1)S(1)}, bf16[256,512]{1,0:T(8,128)(2,1)S(1)}, u32[]{:S(2)}, u32[]{:S(2)}) collective-permute-start(bf16[256,512]{1,0:T(8,128)(2,1)S(1)} %get-tuple-element.54), channel_id=1, source_target_pairs={{0,192},{64,0},{128,64},{192,128},{1,193},{65,1},{129,65},{193,129... | collective-permute-start | bytes 786440 | tf_op jit(solution)/shard_map/ppermute | solution.py:40
  133.5 8.0 %collective-permute-start.14 = (bf16[256,512]{1,0:T(8,128)(2,1)S(1)}, bf16[256,512]{1,0:T(8,128)(2,1)S(1)}, u32[]{:S(2)}, u32[]{:S(2)}) collective-permute-start(bf16[256,512]{1,0:T(8,128)(2,1)S(1)} %get-tuple-element.55), channel_id=1, source_target_pairs={{0,16},{16,32},{32,48},{48,0},{1,17},{17,33},{33,49},{49,1},{2,18}... | collective-permute-start | bytes 786440 | tf_op jit(solution)/shard_map/ppermute | solution.py:39
  134.1 28.1 %collective-permute-start.16 = (bf16[256,512]{1,0:T(8,128)(2,1)S(1)}, bf16[256,512]{1,0:T(8,128)(2,1)}, u32[]{:S(2)}, u32[]{:S(2)}) collective-permute-start(bf16[256,512]{1,0:T(8,128)(2,1)S(1)} %get-tuple-element.56), channel_id=1, source_target_pairs={{0,48},{16,0},{32,16},{48,32},{1,49},{17,1},{33,17},{49,33},{2,50}... | collective-permute-start | bytes 786440 | tf_op jit(solution)/shard_map/ppermute | solution.py:40
  136.7 4.8 %copy-start.12 = (f32[512,512]{1,0:T(8,128)}, f32[512,512]{1,0:T(8,128)S(1)}, u32[]{:S(2)}) copy-start(f32[512,512]{1,0:T(8,128)S(1)} %fusion.28) | copy-start | bytes 3145732
  137.2 14.4 %collective-permute-start.11 = (bf16[512,512]{1,0:T(8,128)(2,1)S(1)}, bf16[512,512]{1,0:T(8,128)(2,1)S(1)}, u32[]{:S(2)}, u32[]{:S(2)}) collective-permute-start(bf16[512,512]{1,0:T(8,128)(2,1)S(1)} %pad_maximum_fusion), channel_id=1, source_target_pairs={{0,64},{64,128},{128,192},{192,0},{1,65},{65,129},{129,193},{193,1... | collective-permute-start | bytes 1572872 | tf_op jit(solution)/shard_map/ppermute | solution.py:44
  137.4 14.2 %collective-permute-start.13 = (bf16[512,512]{1,0:T(8,128)(2,1)S(1)}, bf16[512,512]{1,0:T(8,128)(2,1)S(1)}, u32[]{:S(2)}, u32[]{:S(2)}) collective-permute-start(bf16[512,512]{1,0:T(8,128)(2,1)S(1)} %pad_maximum_fusion.1), channel_id=1, source_target_pairs={{0,192},{64,0},{128,64},{192,128},{1,193},{65,1},{129,65},{193,129... | collective-permute-start | bytes 1572872 | tf_op jit(solution)/shard_map/ppermute | solution.py:45
  142.4 23.4 %collective-permute-start.15 = (bf16[512,512]{1,0:T(8,128)(2,1)}, bf16[512,512]{1,0:T(8,128)(2,1)}, u32[]{:S(2)}, u32[]{:S(2)}) collective-permute-start(bf16[512,512]{1,0:T(8,128)(2,1)} %pad_maximum_fusion.2), channel_id=1, source_target_pairs={{0,16},{16,32},{32,48},{48,0},{1,17},{17,33},{33,49},{49,1},{2,18}... | collective-permute-start | bytes 1572872 | tf_op jit(solution)/shard_map/ppermute | solution.py:44
  152.7 30.4 %all-to-all-start.3 = ((bf16[32,16,512]{2,1,0:T(8,128)(2,1)}), bf16[32,16,512]{2,1,0:T(8,128)(2,1)S(1)}, u32[]{:S(2)}, u32[]{:S(2)}) async-start(bf16[32,16,512]{2,1,0:T(8,128)(2,1)} %bitcast.5), calls=%async_computation.3 | async-start | bytes 1048576 | tf_op jit(solution)/shard_map/all_to_all | solution.py:92
  163.5 17.5 %collective-permute-start.17 = (bf16[512,512]{1,0:T(8,128)(2,1)S(1)}, bf16[512,512]{1,0:T(8,128)(2,1)S(1)}, u32[]{:S(2)}, u32[]{:S(2)}) collective-permute-start(bf16[512,512]{1,0:T(8,128)(2,1)S(1)} %pad_maximum_fusion.3), channel_id=1, source_target_pairs={{0,48},{16,0},{32,16},{48,32},{1,49},{17,1},{33,17},{49,33},{2,50}... | collective-permute-start | bytes 1572872 | tf_op jit(solution)/shard_map/ppermute | solution.py:45
  183.1 24.3 %all-to-all-start.4 = ((bf16[32,16,512]{2,1,0:T(8,128)(2,1)}), bf16[32,16,512]{2,1,0:T(8,128)(2,1)S(1)}, u32[]{:S(2)}, u32[]{:S(2)}) async-start(bf16[32,16,512]{2,1,0:T(8,128)(2,1)} %bitcast.6), calls=%async_computation.4 | async-start | bytes 1048576 | tf_op jit(solution)/shard_map/all_to_all | solution.py:92
  (6 other events, 5.8 us)

commit v3 on v2

v3 whole, which is shorter than its diff:
```python
import jax
import jax.numpy as jnp
from jax import lax
from jax.experimental import pallas as pl
from jax.experimental.pallas import tpu as pltpu
from jax.sharding import Mesh, PartitionSpec as P

F32 = jnp.float32
BF16 = jnp.bfloat16
RIGHT = [(i, (i + 1) % 4) for i in range(4)]
LEFT = [(i, (i - 1) % 4) for i in range(4)]


def norm_back(projected, residual, bias_out, norm_gain, grad_out):
    summed_in = residual.astype(F32) + projected + bias_out
    mean_in = jnp.mean(summed_in, axis=-1, keepdims=True)
    centred = summed_in - mean_in
    variance = jnp.mean(centred * centred, axis=-1, keepdims=True)
    inv_std = lax.rsqrt(variance + 1e-05)
    normed = centred * inv_std
    grad_norm = grad_out.astype(F32) * norm_gain
    first_mean = jnp.mean(grad_norm, axis=-1, keepdims=True)
    second_mean = jnp.mean(grad_norm * normed, axis=-1, keepdims=True)
    return (inv_std * (grad_norm - first_mean - normed * second_mean)).astype(BF16)


def ring_gather(piece, axis):
    mid = piece.shape[0] // 2
    before = lax.ppermute(piece, axis, RIGHT)
    after = lax.ppermute(piece, axis, LEFT)
    top = lax.ppermute(before[:mid], axis, RIGHT)
    bottom = lax.ppermute(after[mid:], axis, LEFT)
    return piece, after, top, bottom, before


def ring_columns(columns_of, axis):
    far = columns_of(2)
    rows = far.shape[0]
    mid = rows // 2
    right = jnp.concatenate([columns_of(1), far[:mid]])
    left = jnp.concatenate([columns_of(3), far[mid:]])
    before = lax.ppermute(right, axis, RIGHT)
    after = lax.ppermute(left, axis, LEFT)
    top = lax.ppermute(before[rows:], axis, RIGHT)
    bottom = lax.ppermute(after[rows:], axis, LEFT)
    return columns_of(0), after[:rows], top, bottom, before[:rows]


def project_kernel(*refs):
    context_ref, pieces = refs[0], refs[1:6]
    weight_ref, out_ref = refs[6], refs[7]
    iy = lax.axis_index("y")
    for ref, step, low in zip(pieces, (0, 1, 2, 2, 3), (0, 0, 0, 2, 0)):
        at = lax.rem(iy + step, 4)
        for k in range(ref.shape[0]):
            weight_ref[low + k, at] = ref[k]
    for x in range(4):
        block = weight_ref[x].reshape(512, 1024)
        out_ref[:, x * 512:(x + 1) * 512] = lax.dot_general(
            context_ref[...], block, (((1,), (1,)), ((), ())), preferred_element_type=F32
        )


def project(context, pieces):
    rows = context.shape[0]
    return pl.pallas_call(
        project_kernel,
        out_shape=(
            jax.ShapeDtypeStruct((4, 4, 128, 1024), BF16),
            jax.ShapeDtypeStruct((rows, 2048), F32),
        ),
        compiler_params=pltpu.CompilerParams(vmem_limit_bytes=40 << 20),
        cost_estimate=pl.CostEstimate(
            flops=2 * rows * 1024 * 2048, bytes_accessed=16 << 20, transcendentals=0
        ),
        name="project",
    )(context, *pieces)


def spread(piece, axes):
    return lax.all_to_all(
        jnp.broadcast_to(piece[None], (32,) + piece.shape), axes, split_axis=0, concat_axis=0
    )


def collect(total, axes):
    share = total.astype(BF16).reshape(32, 16, 1024)
    got = lax.all_to_all(share, axes, split_axis=0, concat_axis=0)
    return jnp.sum(got.astype(F32), axis=0)


def shards(context, residual, bias_out, norm_gain, out_weight, cotangent, counts, slot_codes):
    capacity = slot_codes.shape[0]
    features = residual.shape[1]
    half = features // 2
    core = lax.axis_index("core")
    ix = lax.axis_index("x")
    live_mask = jnp.arange(capacity) < counts[0]
    swap = [(0, 1), (1, 0)]

    mine = lax.dynamic_slice_in_dim(cotangent, core * half, half, axis=1)
    weight_t = out_weight.T
    mine, weight_t = lax.optimization_barrier((mine, weight_t))
    returned = lax.all_to_all(mine, ("x", "y", "z"), split_axis=0, concat_axis=0, tiled=True)
    block = spread(weight_t, ("x", "z")).reshape(4, 128, 1024)
    block, held = lax.optimization_barrier((block, context))
    context_pieces = ring_gather(held, "x")
    pieces = ring_gather(block, "y")
    pieces, returned = lax.optimization_barrier((pieces, returned))

    weight_t, partial_proj = project(context, pieces)
    weight_t = weight_t.reshape(2048, 1024)
    picked = returned.at[slot_codes].get(mode="promise_in_bounds")
    picked = jnp.where(live_mask[:, None], picked, jnp.zeros((), picked.dtype))
    other = lax.ppermute(picked, "core", swap)
    grad_out = jnp.where(
        core == 0,
        jnp.concatenate([picked, other], axis=1),
        jnp.concatenate([other, picked], axis=1),
    )
    projected = partial_proj + lax.ppermute(partial_proj, "core", swap)
    grad_resid = norm_back(projected, residual, bias_out, norm_gain, grad_out)

    def columns_of(step):
        at = lax.rem(ix + step, 4)
        return lax.dynamic_slice_in_dim(grad_resid, at * 512, 512, axis=1)

    share = jnp.zeros((), F32)
    for columns, rows in zip(ring_columns(columns_of, "x"), context_pieces):
        share = share + lax.dot_general(
            columns, rows, (((0,), (0,)), ((), ())), preferred_element_type=F32
        )
    total = collect(share, ("y", "z"))
    replicas = lax.axis_size("x") * lax.axis_size("y") * lax.axis_size("z")
    grad_wout = (total / replicas).T
    grad_ctx = jnp.dot(grad_resid, weight_t, preferred_element_type=F32).astype(BF16)
    return (grad_resid, grad_ctx, grad_wout)


def solution(mesh):
    torus = Mesh(mesh.devices.reshape(4, 4, 8, 2), ("x", "y", "z", "core"))
    dp = ("x", "y", "z")
    return jax.shard_map(
        shards,
        mesh=torus,
        in_specs=(
            P(dp, "core"),
            P(dp, None),
            P(),
            P(),
            P("core", dp),
            P(dp, None),
            P(dp),
            P(dp),
        ),
        out_specs=(P(dp, None), P(dp, "core"), P("core", dp)),
        check_vma=False,
    )
```

time: 210 us -> 190 us (0.905)
  starting transfers between devices: 58.4 us -> 33.7 us
  blocking collectives: 26.4 us -> 39.8 us
  waiting for transfers between devices: 70.2 us -> 63.8 us
  other arithmetic: 13.5 us -> 8.84 us
  matrix products: 10.1 us -> 13 us
    all_to_all x1 -> x0, waiting for transfers between devices: 15.2 us -> none  [spread(): lax.all_to_all(jnp.broadcast_to(piece[None], (32,) + piece.shape), axes,...]
    all_to_all x1, blocking collectives: 26.4 us -> 39.8 us  [spread(): lax.all_to_all(jnp.broadcast_to(piece[None], (32,) + piece.shape), axes,...]
    all_to_all x2 -> x1, waiting for transfers between devices: 9.62 us -> 20.8 us  [collect(): got = lax.all_to_all(share, axes, split_axis=0, concat_axis=0)]
    ppermute x8 -> x4, waiting for transfers between devices: 23.3 us -> 12.2 us  [the longest x1 6.58 us: ring_columns(): after = lax.ppermute(left, axis, LEFT)]
    ppermute x8 -> x4, starting transfers between devices: 11.5 us -> 3.56 us  [the longest x1 1.58 us: ring_columns(): after = lax.ppermute(left, axis, LEFT)]
    all_to_all x1 -> x0, starting transfers between devices: 7.06 us -> none  [spread(): lax.all_to_all(jnp.broadcast_to(piece[None], (32,) + piece.shape), axes,...]
    all_to_all x2 -> x1, starting transfers between devices: 18.8 us -> 12 us  [collect(): got = lax.all_to_all(share, axes, split_axis=0, concat_axis=0)]
    unnamed x32 -> x14, local copies, waits for them, and re-layouts: 7.9 us -> 4.69 us
  transfers between devices with their start and end apart: 22 -> 16, of which waited for: 9 -> 11; matrix products, arithmetic and copies ran while one was open for 14% -> 15% of each run, Pallas kernels for 0% -> 0%
where the time goes in v3:
time: 190 us; the launch traced here: 187 us
  waiting for transfers between devices  63.8 us (34%)
  blocking collectives  39.8 us (21%)
  starting transfers between devices  33.7 us (18%)
  local copies, waits for them, and re-layouts  20.9 us (11%)
  matrix products  13 us (7%)
  other arithmetic  8.84 us (5%)
  Pallas kernels  5.84 us (3%)
    all_to_all x1, blocking collectives, spread(): lax.all_to_all(jnp.broadcast_to(piece[None], (32,) + piece.shape), axes,...  39.8 us
    all_to_all x1, waiting for transfers between devices, collect(): got = lax.all_to_all(share, axes, split_axis=0, concat_axis=0)  20.8 us
    ppermute x2, waiting for transfers between devices, ring_gather(): before = lax.ppermute(piece, axis, RIGHT)  19.5 us
    all_to_all x1, starting transfers between devices, collect(): got = lax.all_to_all(share, axes, split_axis=0, concat_axis=0)  12 us
    all_to_all x1, starting transfers between devices, shards(): lax.all_to_all(mine, ('x', 'y', 'z'), split_axis=0, concat_axis=0, tiled=...  9.51 us
    dot_general x5, matrix products, shards(): lax.dot_general(columns, rows, (((0,), (0,)), ((), ())), preferred_elemen...  7.62 us
    ppermute x1, waiting for transfers between devices, ring_columns(): after = lax.ppermute(left, axis, LEFT)  6.58 us
    ppermute x2, waiting for transfers between devices, ring_gather(): bottom = lax.ppermute(after[mid:], axis, LEFT)  6.19 us
  transfers between devices with their start and end apart: 16, of which 11 were waited for; matrix products, arithmetic and copies ran while one was open for 15% of the time, Pallas kernels for 0%

profile of v3, /device:TPU:24, one launch (start us, length us, event | category | flops | bytes accessed | tf_op | source)
XLA Modules:
  0.0 187.4 jit_solution(18210527142038241474)
XLA Ops:
  0.7 1.4 copy-done
  3.0 39.8 %all_to_all.22 = bf16[32,16,1024]{2,1,0:T(8,128)(2,1)S(1)} all-to-all(bf16[32,16,1024]{2,1,0:T(8,128)(2,1)S(1)} %broadcast_in_dim.16), channel_id=1, replica_groups=mesh['x'=4,'y'=4,'z'=8,'core'=2] {'x','z'}, dimensions={0} | all-to-all | bytes 2097152 | tf_op jit(solution)/shard_map/all_to_all | solution.py:81
  43.0 1.8 collective-permute-start
  44.8 1.3 all_to_all.15
  46.1 9.5 %all-to-all-start.1 = ((bf16[128,3,1024]{2,1,0:T(4,128)(2,1)}), bf16[128,3,1024]{2,1,0:T(4,128)(2,1)}, u32[]{:S(2)}, u32[]{:S(2)}) async-start(bf16[128,3,1024]{2,1,0:T(4,128)(2,1)} %all_to_all.15), calls=%async_computation.1 | async-start | bytes 2097152 | tf_op jit(solution)/shard_map/all_to_all | solution.py:104
  55.6 19.5 %collective-permute-done.1.refs_5_ = bf16[4,128,1024]{2,1,0:T(8,128)(2,1)} collective-permute-done((bf16[4,128,1024]{2,1,0:T(8,128)(2,1)S(1)}, bf16[4,128,1024]{2,1,0:T(8,128)(2,1)}, u32[]{:S(2)}, u32[]{:S(2)}) %collective-permute-start.1) | collective-permute-done | bytes 1048608 | tf_op jit(solution)/shard_map/ppermute | solution.py:29
  75.1 1.9 %slice.42 = bf16[2,128,1024]{2,1,0:T(8,128)(2,1)} slice(bf16[4,128,1024]{2,1,0:T(8,128)(2,1)} %collective-permute-done.1.refs_5_), slice={[0:2], [0:128], [0:1024]} | slice | bytes 1048576 | tf_op jit(solution)/shard_map/slice | solution.py:31
  77.0 1.9 %slice.43 = bf16[2,128,1024]{2,1,0:T(8,128)(2,1)} slice(bf16[4,128,1024]{2,1,0:T(8,128)(2,1)} %collective-permute-done.refs_2_), slice={[2:4], [0:128], [0:1024]} | slice | bytes 1048576 | tf_op jit(solution)/shard_map/slice | solution.py:32
  78.9 2.0 %collective-permute-start.3 = (bf16[2,128,1024]{2,1,0:T(8,128)(2,1)}, bf16[2,128,1024]{2,1,0:T(8,128)(2,1)}, u32[]{:S(2)}, u32[]{:S(2)}) collective-permute-start(bf16[2,128,1024]{2,1,0:T(8,128)(2,1)} %slice.43), channel_id=1, source_target_pairs={{0,48},{16,0},{32,16},{48,32},{1,49},{17,1},{33,17},{49,33},{2,50}... | collective-permute-start | bytes 1572872 | tf_op jit(solution)/shard_map/ppermute | solution.py:32
  80.9 2.0 %all-to-all-done.1 = bf16[128,3,1024]{2,1,0:T(4,128)(2,1)} async-done(((bf16[128,3,1024]{2,1,0:T(4,128)(2,1)}), bf16[128,3,1024]{2,1,0:T(4,128)(2,1)}, u32[]{:S(2)}, u32[]{:S(2)}) %all-to-all-start.1) | async-done | bytes 786464 | tf_op jit(solution)/shard_map/all_to_all | solution.py:104
  82.8 3.2 %all_to_all.17 = bf16[384,1024]{1,0:T(8,128)(2,1)} reshape(bf16[128,3,1024]{2,1,0:T(4,128)(2,1)} %all-to-all-done.1) | data formatting | bytes 1572864 | tf_op jit(solution)/shard_map/all_to_all | solution.py:104
  86.7 2.8 %collective-permute-done.3.refs_4_ = bf16[2,128,1024]{2,1,0:T(8,128)(2,1)} collective-permute-done((bf16[2,128,1024]{2,1,0:T(8,128)(2,1)}, bf16[2,128,1024]{2,1,0:T(8,128)(2,1)}, u32[]{:S(2)}, u32[]{:S(2)}) %collective-permute-start.3) | collective-permute-done | bytes 524320 | tf_op jit(solution)/shard_map/ppermute | solution.py:32
  89.6 5.8 %project.1 = (bf16[4,4,128,1024]{3,2,1,0:T(8,128)(2,1)S(1)}, f32[384,2048]{1,0:T(8,128)}) custom-call(bf16[384,1024]{1,0:T(8,128)(2,1)S(1)} %copy-done.1, bf16[4,128,1024]{2,1,0:T(8,128)(2,1)S(1)} %bitcast.19, bf16[4,128,1024]{2,1,0:T(8,128)(2,1)} %collective-permute-done.refs_2_, bf16[2,128,1024]{2,1,0:T(8,128)(2,1)} %collective-permute-done.2.refs_3_, ...), custom_call_target="tpu_custom_call" | custom-call | flops 1610612736 | bytes 16777216 | tf_op jit(solution)/shard_map/project/pallas_call | solution.py:66
  95.4 2.0 %copy-done.2 = bf16[4,4,128,1024]{3,2,1,0:T(8,128)(2,1)} copy-done((bf16[4,4,128,1024]{3,2,1,0:T(8,128)(2,1)}, bf16[4,4,128,1024]{3,2,1,0:T(8,128)(2,1)S(1)}, u32[]{:S(2)}) %copy-start.2) | copy-done | bytes 4194328
  98.2 2.0 %collective-permute-start.10 = (bf16[384,1024]{1,0:T(8,128)(2,1)S(1)}, bf16[384,1024]{1,0:T(8,128)(2,1)}, u32[]{:S(2)}, u32[]{:S(2)}) collective-permute-start(bf16[384,1024]{1,0:T(8,128)(2,1)S(1)} %copy-done.1), channel_id=1, source_target_pairs={{0,64},{64,128},{128,192},{192,0},{1,65},{65,129},{129,193},{193,1... | collective-permute-start | bytes 2359304 | tf_op jit(solution)/shard_map/ppermute | solution.py:29
  100.2 4.0 %gather_fusion = bf16[384,1024]{1,0:T(8,128)(2,1)S(1)} fusion(bf16[384,1024]{1,0:T(8,128)(2,1)} %all_to_all.17, s32[1024]{0:T(1024)S(1)} %pad_clamp_fusion), kind=kCustom, calls=%fused_computation | custom fusion | bytes 1574400 | tf_op jit(solution)/shard_map/gather | solution.py:113
  104.7 3.9 %fusion.10 = (f32[384]{0:T(512)S(1)}, f32[384,2048]{1,0:T(8,128)S(1)}) fusion(f32[2048]{0:T(1024)S(1)} %copy-done.5, f32[384,2048]{1,0:T(8,128)} %get-tuple-element.23, f32[384,2048]{1,0:T(8,128)} %collective-permute-done.4, bf16[384,2048]{1,0:T(8,128)(2,1)} %param.9), kind=kLoop, calls=%fused_computation.33 | loop fusion | flops 3931776 | bytes 11019776 | tf_op jit(solution)/shard_map/reduce_sum | solution.py:16
  110.3 1.6 multiply_convert_fusion
  112.0 1.1 copy-done.3
  113.2 1.6 collective-permute-start.6
  116.1 2.5 %collective-permute-done.7 = bf16[384,1024]{1,0:T(8,128)(2,1)} collective-permute-done((bf16[384,1024]{1,0:T(8,128)(2,1)S(1)}, bf16[384,1024]{1,0:T(8,128)(2,1)}, u32[]{:S(2)}, u32[]{:S(2)}) %collective-permute-start.7) | collective-permute-done | bytes 786464 | tf_op jit(solution)/shard_map/ppermute | solution.py:30
  119.7 1.4 collective-permute-start.13
  122.9 1.7 fusion.7
  124.6 6.6 %collective-permute-done.6 = bf16[576,512]{1,0:T(8,128)(2,1)S(1)} collective-permute-done((bf16[576,512]{1,0:T(8,128)(2,1)S(1)}, bf16[576,512]{1,0:T(8,128)(2,1)S(1)}, u32[]{:S(2)}, u32[]{:S(2)}) %collective-permute-start.6) | collective-permute-done | bytes 589856 | tf_op jit(solution)/shard_map/ppermute | solution.py:43
  131.2 1.4 collective-permute-start.12
  134.4 1.9 fusion.5
  136.2 3.4 %collective-permute-done.13 = bf16[192,1024]{1,0:T(8,128)(2,1)S(1)} collective-permute-done((bf16[192,1024]{1,0:T(8,128)(2,1)S(1)}, bf16[192,1024]{1,0:T(8,128)(2,1)S(1)}, u32[]{:S(2)}, u32[]{:S(2)}) %collective-permute-start.13) | collective-permute-done | bytes 393248 | tf_op jit(solution)/shard_map/ppermute | solution.py:32
  139.6 3.8 %collective-permute-done.12 = bf16[192,512]{1,0:T(8,128)(2,1)S(1)} collective-permute-done((bf16[192,512]{1,0:T(8,128)(2,1)S(1)}, bf16[192,512]{1,0:T(8,128)(2,1)S(1)}, u32[]{:S(2)}, u32[]{:S(2)}) %collective-permute-start.12) | collective-permute-done | bytes 196640 | tf_op jit(solution)/shard_map/ppermute | solution.py:45
  145.4 3.1 %add_convert_fusion = bf16[512,1024]{1,0:T(8,128)(2,1)} fusion(f32[512,1024]{1,0:T(8,128)S(1)} %fusion.12, f32[512,1024]{1,0:T(8,128)S(1)} %fusion.11, f32[512,1024]{1,0:T(8,128)S(1)} %fusion.7, f32[512,1024]{1,0:T(8,128)S(1)} %fusion.5, bf16[384,1024]{1,0:T(8,128)(2,1)} %collective-permute-done.10, bf16[576,512]{1,0:T(8,128)(2,1)} %collective-permute-done.8), kind=kOutput, calls=%fused_computation.8 | convolution fusion | flops 405274624 | bytes 10616832 | tf_op jit(solution)/shard_map/dot_general | solution.py:130
  148.5 12.0 %all-to-all-start.2 = ((bf16[32,16,1024]{2,1,0:T(8,128)(2,1)}), bf16[32,16,1024]{2,1,0:T(8,128)(2,1)S(1)}, u32[]{:S(2)}, u32[]{:S(2)}) async-start(bf16[32,16,1024]{2,1,0:T(8,128)(2,1)} %bitcast.21), calls=%async_computation.2 | async-start | bytes 2097152 | tf_op jit(solution)/shard_map/all_to_all | solution.py:88
  160.5 5.3 %convolution_convert_fusion = bf16[384,1024]{1,0:T(8,128)(2,1)} fusion(bf16[384,2048]{1,0:T(8,128)(2,1)} %copy-done.3, bf16[2048,1024]{1,0:T(8,128)(2,1)} %bitcast.20), kind=kOutput, calls=%fused_computation.10 | convolution fusion | flops 1611005952 | bytes 6553600 | tf_op jit(solution)/shard_map/dot_general | solution.py:136
  165.8 20.8 %all-to-all-done.2 = bf16[32,16,1024]{2,1,0:T(8,128)(2,1)S(1)} async-done(((bf16[32,16,1024]{2,1,0:T(8,128)(2,1)}), bf16[32,16,1024]{2,1,0:T(8,128)(2,1)S(1)}, u32[]{:S(2)}, u32[]{:S(2)}) %all-to-all-start.2) | async-done | bytes 1048608 | tf_op jit(solution)/shard_map/all_to_all | solution.py:88
  (50 shorter events, 13.1 us)
Async XLA Ops:
  0.6 1.4 copy-start
  42.8 32.3 %collective-permute-start.1 = (bf16[4,128,1024]{2,1,0:T(8,128)(2,1)S(1)}, bf16[4,128,1024]{2,1,0:T(8,128)(2,1)}, u32[]{:S(2)}, u32[]{:S(2)}) collective-permute-start(bf16[4,128,1024]{2,1,0:T(8,128)(2,1)S(1)} %bitcast.17), channel_id=1, source_target_pairs={{0,16},{16,32},{32,48},{48,0},{1,17},{17,33},{33,49},{49,1},{2,18}... | collective-permute-start | bytes 3145736 | tf_op jit(solution)/shard_map/ppermute | solution.py:29
  43.0 34.0 %collective-permute-start = (bf16[4,128,1024]{2,1,0:T(8,128)(2,1)S(1)}, bf16[4,128,1024]{2,1,0:T(8,128)(2,1)}, u32[]{:S(2)}, u32[]{:S(2)}) collective-permute-start(bf16[4,128,1024]{2,1,0:T(8,128)(2,1)S(1)} %bitcast.18), channel_id=1, source_target_pairs={{0,48},{16,0},{32,16},{48,32},{1,49},{17,1},{33,17},{49,33},{2,50}... | collective-permute-start | bytes 3145736 | tf_op jit(solution)/shard_map/ppermute | solution.py:30
  46.0 43.5 %copy-start.1 = (bf16[384,1024]{1,0:T(8,128)(2,1)S(1)}, bf16[384,1024]{1,0:T(8,128)(2,1)}, u32[]{:S(2)}) copy-start(bf16[384,1024]{1,0:T(8,128)(2,1)} %refs_0_.1) | copy-start | bytes 2359300
  46.1 36.8 %all-to-all-start.1 = ((bf16[128,3,1024]{2,1,0:T(4,128)(2,1)}), bf16[128,3,1024]{2,1,0:T(4,128)(2,1)}, u32[]{:S(2)}, u32[]{:S(2)}) async-start(bf16[128,3,1024]{2,1,0:T(4,128)(2,1)} %all_to_all.15), calls=%async_computation.1 | async-start | bytes 2097152 | tf_op jit(solution)/shard_map/all_to_all | solution.py:104
  77.0 9.8 %collective-permute-start.2 = (bf16[2,128,1024]{2,1,0:T(8,128)(2,1)}, bf16[2,128,1024]{2,1,0:T(8,128)(2,1)}, u32[]{:S(2)}, u32[]{:S(2)}) collective-permute-start(bf16[2,128,1024]{2,1,0:T(8,128)(2,1)} %slice.42), channel_id=1, source_target_pairs={{0,16},{16,32},{32,48},{48,0},{1,17},{17,33},{33,49},{49,1},{2,18}... | collective-permute-start | bytes 1572872 | tf_op jit(solution)/shard_map/ppermute | solution.py:31
  78.9 10.7 %collective-permute-start.3 = (bf16[2,128,1024]{2,1,0:T(8,128)(2,1)}, bf16[2,128,1024]{2,1,0:T(8,128)(2,1)}, u32[]{:S(2)}, u32[]{:S(2)}) collective-permute-start(bf16[2,128,1024]{2,1,0:T(8,128)(2,1)} %slice.43), channel_id=1, source_target_pairs={{0,48},{16,0},{32,16},{48,32},{1,49},{17,1},{33,17},{49,33},{2,50}... | collective-permute-start | bytes 1572872 | tf_op jit(solution)/shard_map/ppermute | solution.py:32
  86.0 12.0 %copy-start.6 = (s32[384]{0:T(512)S(1)}, s32[384]{0:T(512)}, u32[]{:S(2)}) copy-start(s32[384]{0:T(512)} %param.15) | copy-start | bytes 4612
  95.4 2.0 %copy-start.2 = (bf16[4,4,128,1024]{3,2,1,0:T(8,128)(2,1)}, bf16[4,4,128,1024]{3,2,1,0:T(8,128)(2,1)S(1)}, u32[]{:S(2)}) copy-start(bf16[4,4,128,1024]{3,2,1,0:T(8,128)(2,1)S(1)} %get-tuple-element.25) | copy-start | bytes 12582916
  97.4 7.2 %collective-permute-start.4 = (f32[384,2048]{1,0:T(8,128)}, f32[384,2048]{1,0:T(8,128)}, u32[]{:S(2)}, u32[]{:S(2)}) collective-permute-start(f32[384,2048]{1,0:T(8,128)} %get-tuple-element.23), channel_id=1, source_target_pairs={{0,1},{1,0},{2,3},{3,2},{4,5},{5,4},{6,7},{7,6},{8,9},{9,8},{10,11... | collective-permute-start | bytes 9437192 | tf_op jit(solution)/shard_map/ppermute | solution.py:121
  98.1 6.5 %copy-start.5 = (f32[2048]{0:T(1024)S(1)}, f32[2048]{0:T(1024)}, u32[]{:S(2)}) copy-start(f32[2048]{0:T(1024)} %param.10) | copy-start | bytes 24580
  98.1 20.5 %collective-permute-start.7 = (bf16[384,1024]{1,0:T(8,128)(2,1)S(1)}, bf16[384,1024]{1,0:T(8,128)(2,1)}, u32[]{:S(2)}, u32[]{:S(2)}) collective-permute-start(bf16[384,1024]{1,0:T(8,128)(2,1)S(1)} %copy-done.1), channel_id=1, source_target_pairs={{0,192},{64,0},{128,64},{192,128},{1,193},{65,1},{129,65},{193,129... | collective-permute-start | bytes 2359304 | tf_op jit(solution)/shard_map/ppermute | solution.py:30
  98.2 22.8 %collective-permute-start.10 = (bf16[384,1024]{1,0:T(8,128)(2,1)S(1)}, bf16[384,1024]{1,0:T(8,128)(2,1)}, u32[]{:S(2)}, u32[]{:S(2)}) collective-permute-start(bf16[384,1024]{1,0:T(8,128)(2,1)S(1)} %copy-done.1), channel_id=1, source_target_pairs={{0,64},{64,128},{128,192},{192,0},{1,65},{65,129},{129,193},{193,1... | collective-permute-start | bytes 2359304 | tf_op jit(solution)/shard_map/ppermute | solution.py:29
  104.3 4.7 %collective-permute-start.5 = (bf16[384,1024]{1,0:T(8,128)(2,1)S(1)}, bf16[384,1024]{1,0:T(8,128)(2,1)S(1)}, u32[]{:S(2)}, u32[]{:S(2)}) collective-permute-start(bf16[384,1024]{1,0:T(8,128)(2,1)S(1)} %broadcast_select_fusion), channel_id=1, source_target_pairs={{0,1},{1,0},{2,3},{3,2},{4,5},{5,4},{6,7},{7,6},{8,9},{9,8},{10,11... | collective-permute-start | bytes 2359304 | tf_op jit(solution)/shard_map/ppermute | solution.py:115
  108.5 0.7 copy-start.4
  111.9 1.1 copy-start.3
  113.2 18.0 %collective-permute-start.6 = (bf16[576,512]{1,0:T(8,128)(2,1)S(1)}, bf16[576,512]{1,0:T(8,128)(2,1)S(1)}, u32[]{:S(2)}, u32[]{:S(2)}) collective-permute-start(bf16[576,512]{1,0:T(8,128)(2,1)S(1)} %pad_maximum_fusion), channel_id=1, source_target_pairs={{0,192},{64,0},{128,64},{192,128},{1,193},{65,1},{129,65},{193,129... | collective-permute-start | bytes 1769480 | tf_op jit(solution)/shard_map/ppermute | solution.py:43
  115.6 17.7 %collective-permute-start.8 = (bf16[576,512]{1,0:T(8,128)(2,1)}, bf16[576,512]{1,0:T(8,128)(2,1)}, u32[]{:S(2)}, u32[]{:S(2)}) collective-permute-start(bf16[576,512]{1,0:T(8,128)(2,1)} %pad_maximum_fusion.1), channel_id=1, source_target_pairs={{0,64},{64,128},{128,192},{192,0},{1,65},{65,129},{129,193},{193,1... | collective-permute-start | bytes 1769480 | tf_op jit(solution)/shard_map/ppermute | solution.py:42
  119.7 19.9 %collective-permute-start.13 = (bf16[192,1024]{1,0:T(8,128)(2,1)S(1)}, bf16[192,1024]{1,0:T(8,128)(2,1)S(1)}, u32[]{:S(2)}, u32[]{:S(2)}) collective-permute-start(bf16[192,1024]{1,0:T(8,128)(2,1)S(1)} %slice.48), channel_id=1, source_target_pairs={{0,192},{64,0},{128,64},{192,128},{1,193},{65,1},{129,65},{193,129... | collective-permute-start | bytes 1179656 | tf_op jit(solution)/shard_map/ppermute | solution.py:32
  122.1 21.8 %collective-permute-start.11 = (bf16[192,1024]{1,0:T(8,128)(2,1)S(1)}, bf16[192,1024]{1,0:T(8,128)(2,1)S(1)}, u32[]{:S(2)}, u32[]{:S(2)}) collective-permute-start(bf16[192,1024]{1,0:T(8,128)(2,1)S(1)} %slice.46), channel_id=1, source_target_pairs={{0,64},{64,128},{128,192},{192,0},{1,65},{65,129},{129,193},{193,1... | collective-permute-start | bytes 1179656 | tf_op jit(solution)/shard_map/ppermute | solution.py:31
  131.2 12.2 %collective-permute-start.12 = (bf16[192,512]{1,0:T(8,128)(2,1)S(1)}, bf16[192,512]{1,0:T(8,128)(2,1)S(1)}, u32[]{:S(2)}, u32[]{:S(2)}) collective-permute-start(bf16[192,512]{1,0:T(8,128)(2,1)S(1)} %slice.47), channel_id=1, source_target_pairs={{0,192},{64,0},{128,64},{192,128},{1,193},{65,1},{129,65},{193,129... | collective-permute-start | bytes 589832 | tf_op jit(solution)/shard_map/ppermute | solution.py:45
  134.3 10.6 %collective-permute-start.9 = (bf16[192,512]{1,0:T(8,128)(2,1)S(1)}, bf16[192,512]{1,0:T(8,128)(2,1)S(1)}, u32[]{:S(2)}, u32[]{:S(2)}) collective-permute-start(bf16[192,512]{1,0:T(8,128)(2,1)S(1)} %slice.45), channel_id=1, source_target_pairs={{0,64},{64,128},{128,192},{192,0},{1,65},{65,129},{129,193},{193,1... | collective-permute-start | bytes 589832 | tf_op jit(solution)/shard_map/ppermute | solution.py:44
  148.5 38.1 %all-to-all-start.2 = ((bf16[32,16,1024]{2,1,0:T(8,128)(2,1)}), bf16[32,16,1024]{2,1,0:T(8,128)(2,1)S(1)}, u32[]{:S(2)}, u32[]{:S(2)}) async-start(bf16[32,16,1024]{2,1,0:T(8,128)(2,1)} %bitcast.21), calls=%async_computation.2 | async-start | bytes 2097152 | tf_op jit(solution)/shard_map/all_to_all | solution.py:88

commit v4 on v3

--- a/solution.py
+++ b/solution.py
@@ -33,6 +33,19 @@
     return piece, after, top, bottom, before
 
 
+def ring_reduce(chunk_of, axis):
+    far = chunk_of(2).astype(BF16)
+    mid = far.shape[0] // 2
+    top = lax.ppermute(far[:mid], axis, RIGHT)
+    bottom = lax.ppermute(far[mid:], axis, LEFT)
+    ahead, behind = chunk_of(1), chunk_of(3)
+    ahead = jnp.concatenate([ahead[:mid] + top.astype(F32), ahead[mid:]]).astype(BF16)
+    behind = jnp.concatenate([behind[:mid], behind[mid:] + bottom.astype(F32)]).astype(BF16)
+    from_before = lax.ppermute(ahead, axis, RIGHT)
+    from_after = lax.ppermute(behind, axis, LEFT)
+    return chunk_of(0) + from_before.astype(F32) + from_after.astype(F32)
+
+
 def ring_columns(columns_of, axis):
     far = columns_of(2)
     rows = far.shape[0]
@@ -49,11 +62,11 @@
 def project_kernel(*refs):
     context_ref, pieces = refs[0], refs[1:6]
     weight_ref, out_ref = refs[6], refs[7]
-    iy = lax.axis_index("y")
+    ix, iy = lax.axis_index("x"), lax.axis_index("y")
     for ref, step, low in zip(pieces, (0, 1, 2, 2, 3), (0, 0, 0, 2, 0)):
         at = lax.rem(iy + step, 4)
         for k in range(ref.shape[0]):
-            weight_ref[low + k, at] = ref[k]
+            weight_ref[lax.rem(ix + low + k, 4), at] = ref[k]
     for x in range(4):
         block = weight_ref[x].reshape(512, 1024)
         out_ref[:, x * 512:(x + 1) * 512] = lax.dot_general(
@@ -77,15 +90,16 @@
     )(context, *pieces)
 
 
-def spread(piece, axes):
-    return lax.all_to_all(
-        jnp.broadcast_to(piece[None], (32,) + piece.shape), axes, split_axis=0, concat_axis=0
-    )
+def spread(piece, axis):
+    ways = lax.axis_size(axis)
+    whole = jnp.broadcast_to(piece[None], (ways,) + piece.shape)
+    return lax.all_to_all(whole, axis, split_axis=0, concat_axis=0)
 
 
-def collect(total, axes):
-    share = total.astype(BF16).reshape(32, 16, 1024)
-    got = lax.all_to_all(share, axes, split_axis=0, concat_axis=0)
+def collect(total, axis):
+    ways = lax.axis_size(axis)
+    share = total.astype(BF16).reshape(ways, -1, total.shape[1])
+    got = lax.all_to_all(share, axis, split_axis=0, concat_axis=0)
     return jnp.sum(got.astype(F32), axis=0)
 
 
@@ -94,7 +108,7 @@
     features = residual.shape[1]
     half = features // 2
     core = lax.axis_index("core")
-    ix = lax.axis_index("x")
+    ix, iy = lax.axis_index("x"), lax.axis_index("y")
     live_mask = jnp.arange(capacity) < counts[0]
     swap = [(0, 1), (1, 0)]
 
@@ -102,11 +116,19 @@
     weight_t = out_weight.T
     mine, weight_t = lax.optimization_barrier((mine, weight_t))
     returned = lax.all_to_all(mine, ("x", "y", "z"), split_axis=0, concat_axis=0, tiled=True)
-    block = spread(weight_t, ("x", "z")).reshape(4, 128, 1024)
-    block, held = lax.optimization_barrier((block, context))
-    context_pieces = ring_gather(held, "x")
+    block = spread(weight_t, "z").reshape(128, 1024)
+    context_before = lax.ppermute(context, "x", RIGHT)
+    context_after = lax.ppermute(context, "x", LEFT)
+    block, context_before, context_after = lax.optimization_barrier(
+        (block, context_before, context_after)
+    )
+    mid = capacity // 2
+    context_top = lax.ppermute(context_before[:mid], "x", RIGHT)
+    context_bottom = lax.ppermute(context_after[mid:], "x", LEFT)
+    context_pieces = (context, context_after, context_top, context_bottom, context_before)
+    block = jnp.concatenate(ring_gather(block, "x")).reshape(4, 128, 1024)
     pieces = ring_gather(block, "y")
-    pieces, returned = lax.optimization_barrier((pieces, returned))
+    pieces, returned, context_pieces = lax.optimization_barrier((pieces, returned, context_pieces))
 
     weight_t, partial_proj = project(context, pieces)
     weight_t = weight_t.reshape(2048, 1024)
@@ -130,7 +152,10 @@
         share = share + lax.dot_general(
             columns, rows, (((0,), (0,)), ((), ())), preferred_element_type=F32
         )
-    total = collect(share, ("y", "z"))
+    def strip_of(step):
+        return lax.dynamic_slice_in_dim(share, lax.rem(iy + step, 4) * 128, 128, axis=0)
+
+    total = collect(ring_reduce(strip_of, "y"), "z")
     replicas = lax.axis_size("x") * lax.axis_size("y") * lax.axis_size("z")
     grad_wout = (total / replicas).T
     grad_ctx = jnp.dot(grad_resid, weight_t, preferred_element_type=F32).astype(BF16)

time: 190 us -> 184 us (0.968)
  blocking collectives: 39.8 us -> 19.6 us
  starting transfers between devices: 33.7 us -> 50.8 us
  waiting for transfers between devices: 63.8 us -> 55.9 us
  other arithmetic: 8.84 us -> 13.9 us
  local copies, waits for them, and re-layouts: 20.9 us -> 23.7 us
    all_to_all x1, blocking collectives: 39.8 us -> 19.6 us  [spread(): return lax.all_to_all(whole, axis, split_axis=0, concat_axis=0)]
    all_to_all x1, waiting for transfers between devices: 20.8 us -> 5.62 us  [collect(): got = lax.all_to_all(share, axis, split_axis=0, concat_axis=0)]
    ppermute x0 -> x8, starting transfers between devices: none -> 13.4 us  [the longest x1 6.04 us: shards(): context_bottom = lax.ppermute(context_after[mid:], 'x', LEFT)]
    ppermute x0 -> x8, waiting for transfers between devices: none -> 13.2 us  [the longest x1 3.84 us: ring_reduce(): from_before = lax.ppermute(ahead, axis, RIGHT)]
    ppermute x1, waiting for transfers between devices: 0.78 us -> 11.6 us  [ring_columns(): before = lax.ppermute(right, axis, RIGHT)]
    ppermute x2, waiting for transfers between devices: 6.19 us -> 0.01 us  [ring_gather(): bottom = lax.ppermute(after[mid:], axis, LEFT)]
    ppermute x1, waiting for transfers between devices: 6.58 us -> 0.68 us  [ring_columns(): after = lax.ppermute(left, axis, LEFT)]
    all_to_all x1, starting transfers between devices: 12 us -> 6.76 us  [collect(): got = lax.all_to_all(share, axis, split_axis=0, concat_axis=0)]
  transfers between devices with their start and end apart: 16 -> 24, of which waited for: 11 -> 15; matrix products, arithmetic and copies ran while one was open for 15% -> 16% of each run, Pallas kernels for 0% -> 0%
where the time goes in v4:
time: 184 us; the launch traced here: 183 us
  waiting for transfers between devices  55.9 us (30%)
  starting transfers between devices  50.8 us (28%)
  local copies, waits for them, and re-layouts  23.7 us (13%)
  blocking collectives  19.6 us (11%)
  other arithmetic  13.9 us (8%)
  matrix products  12.2 us (7%)
  Pallas kernels  5.61 us (3%)
    all_to_all x1, blocking collectives, spread(): return lax.all_to_all(whole, axis, split_axis=0, concat_axis=0)  19.6 us
    ppermute x2, waiting for transfers between devices, ring_gather(): before = lax.ppermute(piece, axis, RIGHT)  19.2 us
    all_to_all x1, starting transfers between devices, shards(): lax.all_to_all(mine, ('x', 'y', 'z'), split_axis=0, concat_axis=0, tiled=...  13.7 us
    ppermute x1, waiting for transfers between devices, ring_columns(): before = lax.ppermute(right, axis, RIGHT)  11.6 us
    dot_general x5, matrix products, shards(): lax.dot_general(columns, rows, (((0,), (0,)), ((), ())), preferred_elemen...  7.31 us
    all_to_all x1, starting transfers between devices, collect(): got = lax.all_to_all(share, axis, split_axis=0, concat_axis=0)  6.76 us
    unnamed x30, local copies, waits for them, and re-layouts  6.51 us
    ppermute x1, starting transfers between devices, shards(): context_bottom = lax.ppermute(context_after[mid:], 'x', LEFT)  6.04 us
  transfers between devices with their start and end apart: 24, of which 15 were waited for; matrix products, arithmetic and copies ran while one was open for 16% of the time, Pallas kernels for 0%

profile of v4, /device:TPU:24, one launch (start us, length us, event | category | flops | bytes accessed | tf_op | source)
XLA Modules:
  0.0 183.3 jit_solution(11546744162301890373)
XLA Ops:
  2.2 1.7 collective-permute-start.1
  4.8 19.6 %all_to_all.22 = bf16[8,16,1024]{2,1,0:T(8,128)(2,1)S(1)} all-to-all(bf16[8,16,1024]{2,1,0:T(8,128)(2,1)S(1)} %broadcast_in_dim.16), channel_id=1, replica_groups=mesh['x'=4,'y'=4,'z'=8,'core'=2] {'z'}, dimensions={0} | all-to-all | bytes 524288 | tf_op jit(solution)/shard_map/all_to_all | solution.py:96
  24.8 3.0 %collective-permute-start.2 = (bf16[128,1024]{1,0:T(8,128)(2,1)S(1)}, bf16[128,1024]{1,0:T(8,128)(2,1)S(1)}, u32[]{:S(2)}, u32[]{:S(2)}) collective-permute-start(bf16[128,1024]{1,0:T(8,128)(2,1)S(1)} %bitcast.20), channel_id=1, source_target_pairs={{0,192},{64,0},{128,64},{192,128},{1,193},{65,1},{129,65},{193,129... | collective-permute-start | bytes 786440 | tf_op jit(solution)/shard_map/ppermute | solution.py:30
  27.7 4.3 %collective-permute-done.3 = bf16[128,1024]{1,0:T(8,128)(2,1)S(1)} collective-permute-done((bf16[128,1024]{1,0:T(8,128)(2,1)S(1)}, bf16[128,1024]{1,0:T(8,128)(2,1)S(1)}, u32[]{:S(2)}, u32[]{:S(2)}) %collective-permute-start.3) | collective-permute-done | bytes 262176 | tf_op jit(solution)/shard_map/ppermute | solution.py:29
  32.9 3.3 %collective-permute-start.5 = (bf16[64,1024]{1,0:T(8,128)(2,1)S(1)}, bf16[64,1024]{1,0:T(8,128)(2,1)S(1)}, u32[]{:S(2)}, u32[]{:S(2)}) collective-permute-start(bf16[64,1024]{1,0:T(8,128)(2,1)S(1)} %slice.77), channel_id=1, source_target_pairs={{0,192},{64,0},{128,64},{192,128},{1,193},{65,1},{129,65},{193,129... | collective-permute-start | bytes 393224 | tf_op jit(solution)/shard_map/ppermute | solution.py:32
  40.6 1.8 collective-permute-start.6
  43.7 13.7 %all-to-all-start.1 = ((bf16[128,3,1024]{2,1,0:T(4,128)(2,1)}), bf16[128,3,1024]{2,1,0:T(4,128)(2,1)}, u32[]{:S(2)}, u32[]{:S(2)}) async-start(bf16[128,3,1024]{2,1,0:T(4,128)(2,1)} %all_to_all.15), calls=%async_computation.1 | async-start | bytes 2097152 | tf_op jit(solution)/shard_map/all_to_all | solution.py:118
  57.4 14.9 %collective-permute-done.7.refs_5_ = bf16[4,128,1024]{2,1,0:T(8,128)(2,1)S(1)} collective-permute-done((bf16[4,128,1024]{2,1,0:T(8,128)(2,1)}, bf16[4,128,1024]{2,1,0:T(8,128)(2,1)S(1)}, u32[]{:S(2)}, u32[]{:S(2)}) %collective-permute-start.7) | collective-permute-done | bytes 1048608 | tf_op jit(solution)/shard_map/ppermute | solution.py:29
  74.7 1.9 %slice.79 = bf16[2,128,1024]{2,1,0:T(8,128)(2,1)} slice(bf16[4,128,1024]{2,1,0:T(8,128)(2,1)} %collective-permute-done.6.refs_2_), slice={[2:4], [0:128], [0:1024]} | slice | bytes 1048576 | tf_op jit(solution)/shard_map/slice | solution.py:32
  77.9 1.8 slice.61
  79.6 6.0 %collective-permute-start.11 = (bf16[192,1024]{1,0:T(8,128)(2,1)}, bf16[192,1024]{1,0:T(8,128)(2,1)}, u32[]{:S(2)}, u32[]{:S(2)}) collective-permute-start(bf16[192,1024]{1,0:T(8,128)(2,1)} %slice.61), channel_id=1, source_target_pairs={{0,192},{64,0},{128,64},{192,128},{1,193},{65,1},{129,65},{193,129... | collective-permute-start | bytes 1179656 | tf_op jit(solution)/shard_map/ppermute | solution.py:127
  85.7 3.2 %all_to_all.17 = bf16[384,1024]{1,0:T(8,128)(2,1)} reshape(bf16[128,3,1024]{2,1,0:T(4,128)(2,1)} %all-to-all-done.1) | data formatting | bytes 1572864 | tf_op jit(solution)/shard_map/all_to_all | solution.py:118
  91.3 5.6 %project.1 = (bf16[4,4,128,1024]{3,2,1,0:T(8,128)(2,1)S(1)}, f32[384,2048]{1,0:T(8,128)}) custom-call(bf16[384,1024]{1,0:T(8,128)(2,1)S(1)} %copy-done.1, bf16[4,128,1024]{2,1,0:T(8,128)(2,1)} %bitcast.2.refs_1_, bf16[4,128,1024]{2,1,0:T(8,128)(2,1)} %collective-permute-done.6.refs_2_, bf16[2,128,1024]{2,1,0:T(8,128)(2,1)} %collective-permute-done.8.refs_3_, ...), custom_call_target="tpu_custom_call" | custom-call | flops 1610612736 | bytes 16777216 | tf_op jit(solution)/shard_map/project/pallas_call | solution.py:79
  96.9 2.0 %copy-done.2 = bf16[4,4,128,1024]{3,2,1,0:T(8,128)(2,1)} copy-done((bf16[4,4,128,1024]{3,2,1,0:T(8,128)(2,1)}, bf16[4,4,128,1024]{3,2,1,0:T(8,128)(2,1)S(1)}, u32[]{:S(2)}) %copy-start.2) | copy-done | bytes 4194328
  99.6 4.0 %gather_fusion = bf16[384,1024]{1,0:T(8,128)(2,1)S(1)} fusion(bf16[384,1024]{1,0:T(8,128)(2,1)} %all_to_all.17, s32[1024]{0:T(1024)S(1)} %pad_clamp_fusion), kind=kCustom, calls=%fused_computation | custom fusion | bytes 1574400 | tf_op jit(solution)/shard_map/gather | solution.py:135
  105.0 3.6 %fusion.12 = (f32[384]{0:T(512)S(1)}, f32[384,2048]{1,0:T(8,128)S(1)}) fusion(f32[2048]{0:T(1024)S(1)} %copy-done.11, f32[384,2048]{1,0:T(8,128)} %get-tuple-element.31, f32[384,2048]{1,0:T(8,128)} %collective-permute-done.12, bf16[384,2048]{1,0:T(8,128)(2,1)S(1)} %copy-done.9), kind=kLoop, calls=%fused_computation.48 | loop fusion | flops 3931776 | bytes 11019776 | tf_op jit(solution)/shard_map/reduce_sum | solution.py:16
  113.1 1.9 %collective-permute-start.15 = (bf16[576,512]{1,0:T(8,128)(2,1)}, bf16[576,512]{1,0:T(8,128)(2,1)S(1)}, u32[]{:S(2)}, u32[]{:S(2)}) collective-permute-start(bf16[576,512]{1,0:T(8,128)(2,1)} %pad_maximum_fusion.1), channel_id=1, source_target_pairs={{0,64},{64,128},{128,192},{192,0},{1,65},{65,129},{129,193},{193,1... | collective-permute-start | bytes 1769480 | tf_op jit(solution)/shard_map/ppermute | solution.py:55
  115.9 1.8 collective-permute-start.14
  117.7 1.7 fusion.7
  119.4 11.6 %collective-permute-done.15 = bf16[576,512]{1,0:T(8,128)(2,1)S(1)} collective-permute-done((bf16[576,512]{1,0:T(8,128)(2,1)}, bf16[576,512]{1,0:T(8,128)(2,1)S(1)}, u32[]{:S(2)}, u32[]{:S(2)}) %collective-permute-start.15) | collective-permute-done | bytes 589856 | tf_op jit(solution)/shard_map/ppermute | solution.py:55
  131.8 3.3 %collective-permute-start.17 = (bf16[192,512]{1,0:T(8,128)(2,1)S(1)}, bf16[192,512]{1,0:T(8,128)(2,1)S(1)}, u32[]{:S(2)}, u32[]{:S(2)}) collective-permute-start(bf16[192,512]{1,0:T(8,128)(2,1)S(1)} %slice.82), channel_id=1, source_target_pairs={{0,192},{64,0},{128,64},{192,128},{1,193},{65,1},{129,65},{193,129... | collective-permute-start | bytes 589832 | tf_op jit(solution)/shard_map/ppermute | solution.py:58
  135.2 1.9 %fusion.5 = f32[512,1024]{1,0:T(8,128)S(1)} fusion(bf16[384,1024]{1,0:T(8,128)(2,1)} %collective-permute-done.1, bf16[576,512]{1,0:T(8,128)(2,1)S(1)} %collective-permute-done.14), kind=kOutput, calls=%fused_computation.18 | convolution fusion | flops 402653184 | bytes 3276800 | tf_op jit(solution)/shard_map/dot_general | solution.py:152
  137.0 2.0 %collective-permute-done.16 = bf16[192,512]{1,0:T(8,128)(2,1)S(1)} collective-permute-done((bf16[192,512]{1,0:T(8,128)(2,1)S(1)}, bf16[192,512]{1,0:T(8,128)(2,1)S(1)}, u32[]{:S(2)}, u32[]{:S(2)}) %collective-permute-start.16) | collective-permute-done | bytes 196640 | tf_op jit(solution)/shard_map/ppermute | solution.py:57
  148.0 2.1 %collective-permute-done.18 = bf16[64,1024]{1,0:T(8,128)(2,1)S(1)} collective-permute-done((bf16[64,1024]{1,0:T(8,128)(2,1)}, bf16[64,1024]{1,0:T(8,128)(2,1)S(1)}, u32[]{:S(2)}, u32[]{:S(2)}) %collective-permute-start.18) | collective-permute-done | bytes 131104 | tf_op jit(solution)/shard_map/ppermute | solution.py:39
  150.1 2.6 %collective-permute-done.20 = bf16[64,1024]{1,0:T(8,128)(2,1)S(1)} collective-permute-done((bf16[64,1024]{1,0:T(8,128)(2,1)S(1)}, bf16[64,1024]{1,0:T(8,128)(2,1)S(1)}, u32[]{:S(2)}, u32[]{:S(2)}) %collective-permute-start.20) | collective-permute-done | bytes 131104 | tf_op jit(solution)/shard_map/ppermute | solution.py:40
  155.5 1.8 collective-permute-start.21
  157.3 3.8 %collective-permute-done.19 = bf16[128,1024]{1,0:T(8,128)(2,1)S(1)} collective-permute-done((bf16[128,1024]{1,0:T(8,128)(2,1)}, bf16[128,1024]{1,0:T(8,128)(2,1)S(1)}, u32[]{:S(2)}, u32[]{:S(2)}) %collective-permute-start.19) | collective-permute-done | bytes 262176 | tf_op jit(solution)/shard_map/ppermute | solution.py:44
  161.1 2.3 %collective-permute-done.21 = bf16[128,1024]{1,0:T(8,128)(2,1)} collective-permute-done((bf16[128,1024]{1,0:T(8,128)(2,1)}, bf16[128,1024]{1,0:T(8,128)(2,1)}, u32[]{:S(2)}, u32[]{:S(2)}) %collective-permute-start.21) | collective-permute-done | bytes 262176 | tf_op jit(solution)/shard_map/ppermute | solution.py:45
  163.4 1.9 %add_convert_fusion = bf16[128,1024]{1,0:T(8,128)(2,1)} fusion(bf16[128,1024]{1,0:T(8,128)(2,1)} %collective-permute-done.21, bf16[128,1024]{1,0:T(8,128)(2,1)S(1)} %collective-permute-done.19, f32[512,1024]{1,0:T(8,128)} %copy-done.3, s32[]{:T(128)S(6)} %select_n.51), kind=kLoop, calls=%fused_computation.14 | loop fusion | flops 655360 | bytes 1310724 | tf_op jit(solution)/shard_map/convert_element_type | solution.py:101
  165.3 6.8 %all-to-all-start.2 = ((bf16[8,16,1024]{2,1,0:T(8,128)(2,1)}), bf16[8,16,1024]{2,1,0:T(8,128)(2,1)S(1)}, u32[]{:S(2)}, u32[]{:S(2)}) async-start(bf16[8,16,1024]{2,1,0:T(8,128)(2,1)} %bitcast.5), calls=%async_computation.2 | async-start | bytes 524288 | tf_op jit(solution)/shard_map/all_to_all | solution.py:102
  172.1 4.9 %convolution_convert_fusion = bf16[384,1024]{1,0:T(8,128)(2,1)} fusion(bf16[384,2048]{1,0:T(8,128)(2,1)S(1)} %copy-done.5, bf16[2048,1024]{1,0:T(8,128)(2,1)} %bitcast.18), kind=kOutput, calls=%fused_computation.9 | convolution fusion | flops 1611005952 | bytes 6553600 | tf_op jit(solution)/shard_map/dot_general | solution.py:161
  177.0 5.6 %all-to-all-done.2 = bf16[8,16,1024]{2,1,0:T(8,128)(2,1)S(1)} async-done(((bf16[8,16,1024]{2,1,0:T(8,128)(2,1)}), bf16[8,16,1024]{2,1,0:T(8,128)(2,1)S(1)}, u32[]{:S(2)}, u32[]{:S(2)}) %all-to-all-start.2) | async-done | bytes 262176 | tf_op jit(solution)/shard_map/all_to_all | solution.py:102
  (92 shorter events, 35.3 us)
Async XLA Ops:
  0.6 23.8 %collective-permute-start = (bf16[384,1024]{1,0:T(8,128)(2,1)}, bf16[384,1024]{1,0:T(8,128)(2,1)S(1)}, u32[]{:S(2)}, u32[]{:S(2)}) collective-permute-start(bf16[384,1024]{1,0:T(8,128)(2,1)} %refs_0_.1), channel_id=1, source_target_pairs={{0,64},{64,128},{128,192},{192,0},{1,65},{65,129},{129,193},{193,1... | collective-permute-start | bytes 2359304 | tf_op jit(solution)/shard_map/ppermute | solution.py:120
  2.2 22.2 %collective-permute-start.1 = (bf16[384,1024]{1,0:T(8,128)(2,1)}, bf16[384,1024]{1,0:T(8,128)(2,1)}, u32[]{:S(2)}, u32[]{:S(2)}) collective-permute-start(bf16[384,1024]{1,0:T(8,128)(2,1)} %refs_0_.1), channel_id=1, source_target_pairs={{0,192},{64,0},{128,64},{192,128},{1,193},{65,1},{129,65},{193,129... | collective-permute-start | bytes 2359304 | tf_op jit(solution)/shard_map/ppermute | solution.py:121
  24.4 16.0 %copy-start.6 = (bf16[384,1024]{1,0:T(8,128)(2,1)}, bf16[384,1024]{1,0:T(8,128)(2,1)S(1)}, u32[]{:S(2)}) copy-start(bf16[384,1024]{1,0:T(8,128)(2,1)S(1)} %collective-permute-done) | copy-start | bytes 2359300
  24.4 7.7 %collective-permute-start.3 = (bf16[128,1024]{1,0:T(8,128)(2,1)S(1)}, bf16[128,1024]{1,0:T(8,128)(2,1)S(1)}, u32[]{:S(2)}, u32[]{:S(2)}) collective-permute-start(bf16[128,1024]{1,0:T(8,128)(2,1)S(1)} %bitcast.19), channel_id=1, source_target_pairs={{0,64},{64,128},{128,192},{192,0},{1,65},{65,129},{129,193},{193,1... | collective-permute-start | bytes 786440 | tf_op jit(solution)/shard_map/ppermute | solution.py:29
  24.8 8.1 %collective-permute-start.2 = (bf16[128,1024]{1,0:T(8,128)(2,1)S(1)}, bf16[128,1024]{1,0:T(8,128)(2,1)S(1)}, u32[]{:S(2)}, u32[]{:S(2)}) collective-permute-start(bf16[128,1024]{1,0:T(8,128)(2,1)S(1)} %bitcast.20), channel_id=1, source_target_pairs={{0,192},{64,0},{128,64},{192,128},{1,193},{65,1},{129,65},{193,129... | collective-permute-start | bytes 786440 | tf_op jit(solution)/shard_map/ppermute | solution.py:30
  32.1 6.3 %collective-permute-start.4 = (bf16[64,1024]{1,0:T(8,128)(2,1)S(1)}, bf16[64,1024]{1,0:T(8,128)(2,1)S(1)}, u32[]{:S(2)}, u32[]{:S(2)}) collective-permute-start(bf16[64,1024]{1,0:T(8,128)(2,1)S(1)} %slice.76), channel_id=1, source_target_pairs={{0,64},{64,128},{128,192},{192,0},{1,65},{65,129},{129,193},{193,1... | collective-permute-start | bytes 393224 | tf_op jit(solution)/shard_map/ppermute | solution.py:31
  32.9 6.1 %collective-permute-start.5 = (bf16[64,1024]{1,0:T(8,128)(2,1)S(1)}, bf16[64,1024]{1,0:T(8,128)(2,1)S(1)}, u32[]{:S(2)}, u32[]{:S(2)}) collective-permute-start(bf16[64,1024]{1,0:T(8,128)(2,1)S(1)} %slice.77), channel_id=1, source_target_pairs={{0,192},{64,0},{128,64},{192,128},{1,193},{65,1},{129,65},{193,129... | collective-permute-start | bytes 393224 | tf_op jit(solution)/shard_map/ppermute | solution.py:32
  40.4 31.9 %collective-permute-start.7 = (bf16[4,128,1024]{2,1,0:T(8,128)(2,1)}, bf16[4,128,1024]{2,1,0:T(8,128)(2,1)S(1)}, u32[]{:S(2)}, u32[]{:S(2)}) collective-permute-start(bf16[4,128,1024]{2,1,0:T(8,128)(2,1)} %bitcast.2.refs_1_), channel_id=1, source_target_pairs={{0,16},{16,32},{32,48},{48,0},{1,17},{17,33},{33,49},{49,1},{2,18}... | collective-permute-start | bytes 3145736 | tf_op jit(solution)/shard_map/ppermute | solution.py:29
  40.6 34.1 %collective-permute-start.6 = (bf16[4,128,1024]{2,1,0:T(8,128)(2,1)}, bf16[4,128,1024]{2,1,0:T(8,128)(2,1)}, u32[]{:S(2)}, u32[]{:S(2)}) collective-permute-start(bf16[4,128,1024]{2,1,0:T(8,128)(2,1)} %bitcast.2.refs_1_), channel_id=1, source_target_pairs={{0,48},{16,0},{32,16},{48,32},{1,49},{17,1},{33,17},{49,33},{2,50}... | collective-permute-start | bytes 3145736 | tf_op jit(solution)/shard_map/ppermute | solution.py:30
  43.7 42.0 %all-to-all-start.1 = ((bf16[128,3,1024]{2,1,0:T(4,128)(2,1)}), bf16[128,3,1024]{2,1,0:T(4,128)(2,1)}, u32[]{:S(2)}, u32[]{:S(2)}) async-start(bf16[128,3,1024]{2,1,0:T(4,128)(2,1)} %all_to_all.15), calls=%async_computation.1 | async-start | bytes 2097152 | tf_op jit(solution)/shard_map/all_to_all | solution.py:118
  57.4 19.7 %copy-start.7 = (bf16[384,1024]{1,0:T(8,128)(2,1)S(1)}, bf16[384,1024]{1,0:T(8,128)(2,1)}, u32[]{:S(2)}) copy-start(bf16[384,1024]{1,0:T(8,128)(2,1)} %copy-done.6) | copy-start | bytes 2359300
  73.2 18.1 %copy-start.1 = (bf16[384,1024]{1,0:T(8,128)(2,1)S(1)}, bf16[384,1024]{1,0:T(8,128)(2,1)}, u32[]{:S(2)}) copy-start(bf16[384,1024]{1,0:T(8,128)(2,1)} %refs_0_.1) | copy-start | bytes 2359300
  73.2 18.1 %collective-permute-start.8 = (bf16[2,128,1024]{2,1,0:T(8,128)(2,1)}, bf16[2,128,1024]{2,1,0:T(8,128)(2,1)}, u32[]{:S(2)}, u32[]{:S(2)}) collective-permute-start(bf16[2,128,1024]{2,1,0:T(8,128)(2,1)} %slice.78), channel_id=1, source_target_pairs={{0,16},{16,32},{32,48},{48,0},{1,17},{17,33},{33,49},{49,1},{2,18}... | collective-permute-start | bytes 1572872 | tf_op jit(solution)/shard_map/ppermute | solution.py:31
  76.6 14.7 %collective-permute-start.9 = (bf16[2,128,1024]{2,1,0:T(8,128)(2,1)}, bf16[2,128,1024]{2,1,0:T(8,128)(2,1)}, u32[]{:S(2)}, u32[]{:S(2)}) collective-permute-start(bf16[2,128,1024]{2,1,0:T(8,128)(2,1)} %slice.79), channel_id=1, source_target_pairs={{0,48},{16,0},{32,16},{48,32},{1,49},{17,1},{33,17},{49,33},{2,50}... | collective-permute-start | bytes 1572872 | tf_op jit(solution)/shard_map/ppermute | solution.py:32
  77.9 12.1 %collective-permute-start.10 = (bf16[192,1024]{1,0:T(8,128)(2,1)}, bf16[192,1024]{1,0:T(8,128)(2,1)}, u32[]{:S(2)}, u32[]{:S(2)}) collective-permute-start(bf16[192,1024]{1,0:T(8,128)(2,1)} %slice.60), channel_id=1, source_target_pairs={{0,64},{64,128},{128,192},{192,0},{1,65},{65,129},{129,193},{193,1... | collective-permute-start | bytes 1179656 | tf_op jit(solution)/shard_map/ppermute | solution.py:126
  79.6 11.7 %collective-permute-start.11 = (bf16[192,1024]{1,0:T(8,128)(2,1)}, bf16[192,1024]{1,0:T(8,128)(2,1)}, u32[]{:S(2)}, u32[]{:S(2)}) collective-permute-start(bf16[192,1024]{1,0:T(8,128)(2,1)} %slice.61), channel_id=1, source_target_pairs={{0,192},{64,0},{128,64},{192,128},{1,193},{65,1},{129,65},{193,129... | collective-permute-start | bytes 1179656 | tf_op jit(solution)/shard_map/ppermute | solution.py:127
  88.9 10.7 %copy-start.12 = (s32[384]{0:T(512)S(1)}, s32[384]{0:T(512)}, u32[]{:S(2)}) copy-start(s32[384]{0:T(512)} %param.15) | copy-start | bytes 4612
  98.9 6.0 %collective-permute-start.12 = (f32[384,2048]{1,0:T(8,128)}, f32[384,2048]{1,0:T(8,128)}, u32[]{:S(2)}, u32[]{:S(2)}) collective-permute-start(f32[384,2048]{1,0:T(8,128)} %get-tuple-element.31), channel_id=1, source_target_pairs={{0,1},{1,0},{2,3},{3,2},{4,5},{5,4},{6,7},{7,6},{8,9},{9,8},{10,11... | collective-permute-start | bytes 9437192 | tf_op jit(solution)/shard_map/ppermute | solution.py:143
  99.6 5.3 %copy-start.11 = (f32[2048]{0:T(1024)S(1)}, f32[2048]{0:T(1024)}, u32[]{:S(2)}) copy-start(f32[2048]{0:T(1024)} %param.10) | copy-start | bytes 24580
  103.7 5.3 %collective-permute-start.13 = (bf16[384,1024]{1,0:T(8,128)(2,1)S(1)}, bf16[384,1024]{1,0:T(8,128)(2,1)S(1)}, u32[]{:S(2)}, u32[]{:S(2)}) collective-permute-start(bf16[384,1024]{1,0:T(8,128)(2,1)S(1)} %broadcast_select_fusion), channel_id=1, source_target_pairs={{0,1},{1,0},{2,3},{3,2},{4,5},{5,4},{6,7},{7,6},{8,9},{9,8},{10,11... | collective-permute-start | bytes 2359304 | tf_op jit(solution)/shard_map/ppermute | solution.py:137
  111.9 3.9 %copy-start.4 = (bf16[384,2048]{1,0:T(8,128)(2,1)}, bf16[384,2048]{1,0:T(8,128)(2,1)S(1)}, u32[]{:S(2)}) copy-start(bf16[384,2048]{1,0:T(8,128)(2,1)S(1)} %multiply_convert_fusion) | copy-start | bytes 4718596
  113.1 17.9 %collective-permute-start.15 = (bf16[576,512]{1,0:T(8,128)(2,1)}, bf16[576,512]{1,0:T(8,128)(2,1)S(1)}, u32[]{:S(2)}, u32[]{:S(2)}) collective-permute-start(bf16[576,512]{1,0:T(8,128)(2,1)} %pad_maximum_fusion.1), channel_id=1, source_target_pairs={{0,64},{64,128},{128,192},{192,0},{1,65},{65,129},{129,193},{193,1... | collective-permute-start | bytes 1769480 | tf_op jit(solution)/shard_map/ppermute | solution.py:55
  115.9 16.0 %collective-permute-start.14 = (bf16[576,512]{1,0:T(8,128)(2,1)}, bf16[576,512]{1,0:T(8,128)(2,1)S(1)}, u32[]{:S(2)}, u32[]{:S(2)}) collective-permute-start(bf16[576,512]{1,0:T(8,128)(2,1)} %pad_maximum_fusion), channel_id=1, source_target_pairs={{0,192},{64,0},{128,64},{192,128},{1,193},{65,1},{129,65},{193,129... | collective-permute-start | bytes 1769480 | tf_op jit(solution)/shard_map/ppermute | solution.py:56
  131.0 8.0 %collective-permute-start.16 = (bf16[192,512]{1,0:T(8,128)(2,1)S(1)}, bf16[192,512]{1,0:T(8,128)(2,1)S(1)}, u32[]{:S(2)}, u32[]{:S(2)}) collective-permute-start(bf16[192,512]{1,0:T(8,128)(2,1)S(1)} %slice.81), channel_id=1, source_target_pairs={{0,64},{64,128},{128,192},{192,0},{1,65},{65,129},{129,193},{193,1... | collective-permute-start | bytes 589832 | tf_op jit(solution)/shard_map/ppermute | solution.py:57
  131.8 8.7 %collective-permute-start.17 = (bf16[192,512]{1,0:T(8,128)(2,1)S(1)}, bf16[192,512]{1,0:T(8,128)(2,1)S(1)}, u32[]{:S(2)}, u32[]{:S(2)}) collective-permute-start(bf16[192,512]{1,0:T(8,128)(2,1)S(1)} %slice.82), channel_id=1, source_target_pairs={{0,192},{64,0},{128,64},{192,128},{1,193},{65,1},{129,65},{193,129... | collective-permute-start | bytes 589832 | tf_op jit(solution)/shard_map/ppermute | solution.py:58
  137.0 5.0 %copy-start.8 = (bf16[384,1024]{1,0:T(8,128)(2,1)S(1)}, bf16[384,1024]{1,0:T(8,128)(2,1)}, u32[]{:S(2)}) copy-start(bf16[384,1024]{1,0:T(8,128)(2,1)} %copy-done.6) | copy-start | bytes 2359300
  144.9 5.2 %collective-permute-start.18 = (bf16[64,1024]{1,0:T(8,128)(2,1)}, bf16[64,1024]{1,0:T(8,128)(2,1)S(1)}, u32[]{:S(2)}, u32[]{:S(2)}) collective-permute-start(bf16[64,1024]{1,0:T(8,128)(2,1)} %get-tuple-element.51), channel_id=1, source_target_pairs={{0,16},{16,32},{32,48},{48,0},{1,17},{17,33},{33,49},{49,1},{2,18}... | collective-permute-start | bytes 393224 | tf_op jit(solution)/shard_map/ppermute | solution.py:39
  146.5 6.2 %collective-permute-start.20 = (bf16[64,1024]{1,0:T(8,128)(2,1)S(1)}, bf16[64,1024]{1,0:T(8,128)(2,1)S(1)}, u32[]{:S(2)}, u32[]{:S(2)}) collective-permute-start(bf16[64,1024]{1,0:T(8,128)(2,1)S(1)} %get-tuple-element.52), channel_id=1, source_target_pairs={{0,48},{16,0},{32,16},{48,32},{1,49},{17,1},{33,17},{49,33},{2,50}... | collective-permute-start | bytes 393224 | tf_op jit(solution)/shard_map/ppermute | solution.py:40
  148.0 24.1 %copy-start.5 = (bf16[384,2048]{1,0:T(8,128)(2,1)S(1)}, bf16[384,2048]{1,0:T(8,128)(2,1)}, u32[]{:S(2)}) copy-start(bf16[384,2048]{1,0:T(8,128)(2,1)} %copy-done.4) | copy-start | bytes 4718596
  154.6 6.6 %collective-permute-start.19 = (bf16[128,1024]{1,0:T(8,128)(2,1)}, bf16[128,1024]{1,0:T(8,128)(2,1)S(1)}, u32[]{:S(2)}, u32[]{:S(2)}) collective-permute-start(bf16[128,1024]{1,0:T(8,128)(2,1)} %pad_maximum_fusion.2), channel_id=1, source_target_pairs={{0,16},{16,32},{32,48},{48,0},{1,17},{17,33},{33,49},{49,1},{2,18}... | collective-permute-start | bytes 786440 | tf_op jit(solution)/shard_map/ppermute | solution.py:44
  155.5 7.9 %collective-permute-start.21 = (bf16[128,1024]{1,0:T(8,128)(2,1)}, bf16[128,1024]{1,0:T(8,128)(2,1)}, u32[]{:S(2)}, u32[]{:S(2)}) collective-permute-start(bf16[128,1024]{1,0:T(8,128)(2,1)} %pad_maximum_fusion.3), channel_id=1, source_target_pairs={{0,48},{16,0},{32,16},{48,32},{1,49},{17,1},{33,17},{49,33},{2,50}... | collective-permute-start | bytes 786440 | tf_op jit(solution)/shard_map/ppermute | solution.py:45
  165.3 17.2 %all-to-all-start.2 = ((bf16[8,16,1024]{2,1,0:T(8,128)(2,1)}), bf16[8,16,1024]{2,1,0:T(8,128)(2,1)S(1)}, u32[]{:S(2)}, u32[]{:S(2)}) async-start(bf16[8,16,1024]{2,1,0:T(8,128)(2,1)} %bitcast.5), calls=%async_computation.2 | async-start | bytes 524288 | tf_op jit(solution)/shard_map/all_to_all | solution.py:102
  (5 other events, 8.8 us)

commit v5 on v4

--- a/solution.py
+++ b/solution.py
@@ -127,7 +127,12 @@
     context_bottom = lax.ppermute(context_after[mid:], "x", LEFT)
     context_pieces = (context, context_after, context_top, context_bottom, context_before)
     block = jnp.concatenate(ring_gather(block, "x")).reshape(4, 128, 1024)
-    pieces = ring_gather(block, "y")
+    before = lax.ppermute(block, "y", RIGHT)
+    after = lax.ppermute(block, "y", LEFT)
+    before, after, returned = lax.optimization_barrier((before, after, returned))
+    top = lax.ppermute(before[:2], "y", RIGHT)
+    bottom = lax.ppermute(after[2:], "y", LEFT)
+    pieces = (block, after, top, bottom, before)
     pieces, returned, context_pieces = lax.optimization_barrier((pieces, returned, context_pieces))
 
     weight_t, partial_proj = project(context, pieces)

time: 184 us -> 188 us (1.022)
  waiting for transfers between devices: 55.9 us -> 62.4 us
  starting transfers between devices: 50.8 us -> 47.4 us
  local copies, waits for them, and re-layouts: 23.7 us -> 26.1 us
  matrix products: 12.2 us -> 10.2 us
    ppermute x2 -> x1, waiting for transfers between devices: 19.2 us -> 0.01 us  [ring_gather(): before = lax.ppermute(piece, axis, RIGHT)]
    ppermute x0 -> x4, waiting for transfers between devices: none -> 11.8 us  [the longest x1 10.3 us: shards(): before = lax.ppermute(block, 'y', RIGHT)]
    all_to_all x1, waiting for transfers between devices: 0.01 us -> 11.1 us  [shards(): lax.all_to_all(mine, ('x', 'y', 'z'), split_axis=0, concat_axis=0, tiled=...]
    ppermute x0 -> x4, starting transfers between devices: none -> 4.21 us  [the longest x1 2.02 us: shards(): after = lax.ppermute(block, 'y', LEFT)]
    ppermute x1, waiting for transfers between devices: 1.1 us -> 5.2 us  [shards(): context_top = lax.ppermute(context_before[:mid], 'x', RIGHT)]
    ppermute x1, starting transfers between devices: 6.04 us -> 2.59 us  [shards(): context_bottom = lax.ppermute(context_after[mid:], 'x', LEFT)]
    all_to_all x1, starting transfers between devices: 13.7 us -> 11.4 us  [shards(): lax.all_to_all(mine, ('x', 'y', 'z'), split_axis=0, concat_axis=0, tiled=...]
    ppermute x2 -> x1, starting transfers between devices: 3.75 us -> 1.74 us  [ring_gather(): bottom = lax.ppermute(after[mid:], axis, LEFT)]
  transfers between devices with their start and end apart: 24 -> 24, of which waited for: 15 -> 17; matrix products, arithmetic and copies ran while one was open for 16% -> 17% of each run, Pallas kernels for 0% -> 0%
where the time goes in v5:
time: 188 us; the launch traced here: 186 us
  waiting for transfers between devices  62.4 us (33%)
  starting transfers between devices  47.4 us (25%)
  local copies, waits for them, and re-layouts  26.1 us (14%)
  blocking collectives  19.6 us (10%)
  other arithmetic  13.8 us (7%)
  matrix products  10.2 us (5%)
  Pallas kernels  5.3 us (3%)
    all_to_all x1, blocking collectives, spread(): return lax.all_to_all(whole, axis, split_axis=0, concat_axis=0)  19.6 us
    ppermute x1, waiting for transfers between devices, ring_columns(): before = lax.ppermute(right, axis, RIGHT)  11.6 us
    all_to_all x1, starting transfers between devices, shards(): lax.all_to_all(mine, ('x', 'y', 'z'), split_axis=0, concat_axis=0, tiled=...  11.4 us
    all_to_all x1, waiting for transfers between devices, shards(): lax.all_to_all(mine, ('x', 'y', 'z'), split_axis=0, concat_axis=0, tiled=...  11.1 us
    ppermute x1, waiting for transfers between devices, shards(): before = lax.ppermute(block, 'y', RIGHT)  10.3 us
    unnamed x36, local copies, waits for them, and re-layouts  8.21 us
    all_to_all x1, waiting for transfers between devices, collect(): got = lax.all_to_all(share, axis, split_axis=0, concat_axis=0)  5.62 us
    dot_general x5, matrix products, shards(): lax.dot_general(columns, rows, (((0,), (0,)), ((), ())), preferred_elemen...  5.32 us
  transfers between devices with their start and end apart: 24, of which 17 were waited for; matrix products, arithmetic and copies ran while one was open for 17% of the time, Pallas kernels for 0%

profile of v5, /device:TPU:24, one launch (start us, length us, event | category | flops | bytes accessed | tf_op | source)
XLA Modules:
  0.0 186.3 jit_solution(18090531818197448462)
XLA Ops:
  2.2 1.7 collective-permute-start.1
  4.8 19.6 %all_to_all.22 = bf16[8,16,1024]{2,1,0:T(8,128)(2,1)S(1)} all-to-all(bf16[8,16,1024]{2,1,0:T(8,128)(2,1)S(1)} %broadcast_in_dim.16), channel_id=1, replica_groups=mesh['x'=4,'y'=4,'z'=8,'core'=2] {'z'}, dimensions={0} | all-to-all | bytes 524288 | tf_op jit(solution)/shard_map/all_to_all | solution.py:96
  24.8 3.0 %collective-permute-start.2 = (bf16[128,1024]{1,0:T(8,128)(2,1)S(1)}, bf16[128,1024]{1,0:T(8,128)(2,1)}, u32[]{:S(2)}, u32[]{:S(2)}) collective-permute-start(bf16[128,1024]{1,0:T(8,128)(2,1)S(1)} %bitcast.20), channel_id=1, source_target_pairs={{0,192},{64,0},{128,64},{192,128},{1,193},{65,1},{129,65},{193,129... | collective-permute-start | bytes 786440 | tf_op jit(solution)/shard_map/ppermute | solution.py:30
  29.0 11.4 %all-to-all-start.1 = ((bf16[128,3,1024]{2,1,0:T(4,128)(2,1)}), bf16[128,3,1024]{2,1,0:T(4,128)(2,1)}, u32[]{:S(2)}, u32[]{:S(2)}) async-start(bf16[128,3,1024]{2,1,0:T(4,128)(2,1)} %all_to_all.15), calls=%async_computation.1 | async-start | bytes 2097152 | tf_op jit(solution)/shard_map/all_to_all | solution.py:118
  41.3 1.8 collective-permute-start.4
  44.7 1.7 collective-permute-start.5
  53.7 2.0 %collective-permute-start.7 = (bf16[4,128,1024]{2,1,0:T(8,128)(2,1)}, bf16[4,128,1024]{2,1,0:T(8,128)(2,1)}, u32[]{:S(2)}, u32[]{:S(2)}) collective-permute-start(bf16[4,128,1024]{2,1,0:T(8,128)(2,1)} %bitcast.2.refs_1_), channel_id=1, source_target_pairs={{0,48},{16,0},{32,16},{48,32},{1,49},{17,1},{33,17},{49,33},{2,50}... | collective-permute-start | bytes 3145736 | tf_op jit(solution)/shard_map/ppermute | solution.py:131
  55.7 11.1 %all-to-all-done.1 = bf16[128,3,1024]{2,1,0:T(4,128)(2,1)} async-done(((bf16[128,3,1024]{2,1,0:T(4,128)(2,1)}), bf16[128,3,1024]{2,1,0:T(4,128)(2,1)}, u32[]{:S(2)}, u32[]{:S(2)}) %all-to-all-start.1) | async-done | bytes 786464 | tf_op jit(solution)/shard_map/all_to_all | solution.py:118
  66.9 3.2 %all_to_all.17 = bf16[384,1024]{1,0:T(8,128)(2,1)} reshape(bf16[128,3,1024]{2,1,0:T(4,128)(2,1)} %all-to-all-done.1) | data formatting | bytes 1572864 | tf_op jit(solution)/shard_map/all_to_all | solution.py:118
  70.1 10.3 %collective-permute-done.6.refs_5_ = bf16[4,128,1024]{2,1,0:T(8,128)(2,1)S(1)} collective-permute-done((bf16[4,128,1024]{2,1,0:T(8,128)(2,1)}, bf16[4,128,1024]{2,1,0:T(8,128)(2,1)S(1)}, u32[]{:S(2)}, u32[]{:S(2)}) %collective-permute-start.6) | collective-permute-done | bytes 1048608 | tf_op jit(solution)/shard_map/ppermute | solution.py:130
  87.8 2.6 %collective-permute-start.11 = (bf16[192,1024]{1,0:T(8,128)(2,1)S(1)}, bf16[192,1024]{1,0:T(8,128)(2,1)S(1)}, u32[]{:S(2)}, u32[]{:S(2)}) collective-permute-start(bf16[192,1024]{1,0:T(8,128)(2,1)S(1)} %slice.61), channel_id=1, source_target_pairs={{0,192},{64,0},{128,64},{192,128},{1,193},{65,1},{129,65},{193,129... | collective-permute-start | bytes 1179656 | tf_op jit(solution)/shard_map/ppermute | solution.py:127
  90.4 5.2 %collective-permute-done.10 = bf16[192,1024]{1,0:T(8,128)(2,1)S(1)} collective-permute-done((bf16[192,1024]{1,0:T(8,128)(2,1)S(1)}, bf16[192,1024]{1,0:T(8,128)(2,1)S(1)}, u32[]{:S(2)}, u32[]{:S(2)}) %collective-permute-start.10) | collective-permute-done | bytes 393248 | tf_op jit(solution)/shard_map/ppermute | solution.py:126
  97.3 5.3 %project.1 = (bf16[4,4,128,1024]{3,2,1,0:T(8,128)(2,1)S(1)}, f32[384,2048]{1,0:T(8,128)}) custom-call(bf16[384,1024]{1,0:T(8,128)(2,1)S(1)} %copy-done.1, bf16[4,128,1024]{2,1,0:T(8,128)(2,1)} %bitcast.2.refs_1_, bf16[4,128,1024]{2,1,0:T(8,128)(2,1)} %collective-permute-done.7.refs_2_, bf16[2,128,1024]{2,1,0:T(8,128)(2,1)S(1)} %collective-permute-done.8.refs_3_, ...), custom_call_target="tpu_custom_call" | custom-call | flops 1610612736 | bytes 16777216 | tf_op jit(solution)/shard_map/project/pallas_call | solution.py:79
  102.6 2.0 %copy-done.2 = bf16[4,4,128,1024]{3,2,1,0:T(8,128)(2,1)} copy-done((bf16[4,4,128,1024]{3,2,1,0:T(8,128)(2,1)}, bf16[4,4,128,1024]{3,2,1,0:T(8,128)(2,1)S(1)}, u32[]{:S(2)}) %copy-start.2) | copy-done | bytes 4194328
  105.3 4.0 %gather_fusion = bf16[384,1024]{1,0:T(8,128)(2,1)S(1)} fusion(bf16[384,1024]{1,0:T(8,128)(2,1)} %all_to_all.17, s32[1024]{0:T(1024)S(1)} %pad_clamp_fusion), kind=kCustom, calls=%fused_computation | custom fusion | bytes 1574400 | tf_op jit(solution)/shard_map/gather | solution.py:140
  110.7 3.6 %fusion.12 = (f32[384]{0:T(512)S(1)}, f32[384,2048]{1,0:T(8,128)S(1)}) fusion(f32[2048]{0:T(1024)S(1)} %copy-done.14, f32[384,2048]{1,0:T(8,128)} %get-tuple-element.37, f32[384,2048]{1,0:T(8,128)} %collective-permute-done.12, bf16[384,2048]{1,0:T(8,128)(2,1)S(1)} %copy-done.8), kind=kLoop, calls=%fused_computation.48 | loop fusion | flops 3931776 | bytes 11019776 | tf_op jit(solution)/shard_map/reduce_sum | solution.py:16
  119.9 3.1 %collective-permute-start.14 = (bf16[576,512]{1,0:T(8,128)(2,1)}, bf16[576,512]{1,0:T(8,128)(2,1)S(1)}, u32[]{:S(2)}, u32[]{:S(2)}) collective-permute-start(bf16[576,512]{1,0:T(8,128)(2,1)} %pad_maximum_fusion), channel_id=1, source_target_pairs={{0,192},{64,0},{128,64},{192,128},{1,193},{65,1},{129,65},{193,129... | collective-permute-start | bytes 1769480 | tf_op jit(solution)/shard_map/ppermute | solution.py:56
  123.0 1.7 fusion.7
  124.7 11.6 %collective-permute-done.15 = bf16[576,512]{1,0:T(8,128)(2,1)S(1)} collective-permute-done((bf16[576,512]{1,0:T(8,128)(2,1)}, bf16[576,512]{1,0:T(8,128)(2,1)S(1)}, u32[]{:S(2)}, u32[]{:S(2)}) %collective-permute-start.15) | collective-permute-done | bytes 589856 | tf_op jit(solution)/shard_map/ppermute | solution.py:55
  136.5 3.9 %collective-permute-start.17 = (bf16[192,512]{1,0:T(8,128)(2,1)S(1)}, bf16[192,512]{1,0:T(8,128)(2,1)S(1)}, u32[]{:S(2)}, u32[]{:S(2)}) collective-permute-start(bf16[192,512]{1,0:T(8,128)(2,1)S(1)} %slice.80), channel_id=1, source_target_pairs={{0,192},{64,0},{128,64},{192,128},{1,193},{65,1},{129,65},{193,129... | collective-permute-start | bytes 589832 | tf_op jit(solution)/shard_map/ppermute | solution.py:58
  140.4 1.9 fusion.5
  142.3 2.0 %collective-permute-done.16 = bf16[192,512]{1,0:T(8,128)(2,1)S(1)} collective-permute-done((bf16[192,512]{1,0:T(8,128)(2,1)S(1)}, bf16[192,512]{1,0:T(8,128)(2,1)S(1)}, u32[]{:S(2)}, u32[]{:S(2)}) %collective-permute-start.16) | collective-permute-done | bytes 196640 | tf_op jit(solution)/shard_map/ppermute | solution.py:57
  148.2 2.9 %collective-permute-start.18 = (bf16[64,1024]{1,0:T(8,128)(2,1)}, bf16[64,1024]{1,0:T(8,128)(2,1)S(1)}, u32[]{:S(2)}, u32[]{:S(2)}) collective-permute-start(bf16[64,1024]{1,0:T(8,128)(2,1)} %get-tuple-element.57), channel_id=1, source_target_pairs={{0,16},{16,32},{32,48},{48,0},{1,17},{17,33},{33,49},{49,1},{2,18}... | collective-permute-start | bytes 393224 | tf_op jit(solution)/shard_map/ppermute | solution.py:39
  152.3 1.8 collective-permute-done.18
  154.0 3.3 %collective-permute-done.20 = bf16[64,1024]{1,0:T(8,128)(2,1)S(1)} collective-permute-done((bf16[64,1024]{1,0:T(8,128)(2,1)S(1)}, bf16[64,1024]{1,0:T(8,128)(2,1)S(1)}, u32[]{:S(2)}, u32[]{:S(2)}) %collective-permute-start.20) | collective-permute-done | bytes 131104 | tf_op jit(solution)/shard_map/ppermute | solution.py:40
  160.1 1.8 collective-permute-start.21
  161.9 3.8 %collective-permute-done.19 = bf16[128,1024]{1,0:T(8,128)(2,1)S(1)} collective-permute-done((bf16[128,1024]{1,0:T(8,128)(2,1)}, bf16[128,1024]{1,0:T(8,128)(2,1)S(1)}, u32[]{:S(2)}, u32[]{:S(2)}) %collective-permute-start.19) | collective-permute-done | bytes 262176 | tf_op jit(solution)/shard_map/ppermute | solution.py:44
  165.8 2.3 %collective-permute-done.21 = bf16[128,1024]{1,0:T(8,128)(2,1)} collective-permute-done((bf16[128,1024]{1,0:T(8,128)(2,1)}, bf16[128,1024]{1,0:T(8,128)(2,1)}, u32[]{:S(2)}, u32[]{:S(2)}) %collective-permute-start.21) | collective-permute-done | bytes 262176 | tf_op jit(solution)/shard_map/ppermute | solution.py:45
  168.0 1.9 %add_convert_fusion = bf16[128,1024]{1,0:T(8,128)(2,1)} fusion(bf16[128,1024]{1,0:T(8,128)(2,1)} %collective-permute-done.21, bf16[128,1024]{1,0:T(8,128)(2,1)S(1)} %collective-permute-done.19, f32[512,1024]{1,0:T(8,128)} %copy-done.3, s32[]{:T(128)S(6)} %select_n.51), kind=kLoop, calls=%fused_computation.14 | loop fusion | flops 655360 | bytes 1310724 | tf_op jit(solution)/shard_map/convert_element_type | solution.py:101
  169.9 5.2 %all-to-all-start.2 = ((bf16[8,16,1024]{2,1,0:T(8,128)(2,1)}), bf16[8,16,1024]{2,1,0:T(8,128)(2,1)S(1)}, u32[]{:S(2)}, u32[]{:S(2)}) async-start(bf16[8,16,1024]{2,1,0:T(8,128)(2,1)} %bitcast.5), calls=%async_computation.2 | async-start | bytes 524288 | tf_op jit(solution)/shard_map/all_to_all | solution.py:102
  175.2 4.9 %convolution_convert_fusion = bf16[384,1024]{1,0:T(8,128)(2,1)} fusion(bf16[384,2048]{1,0:T(8,128)(2,1)S(1)} %copy-done.5, bf16[2048,1024]{1,0:T(8,128)(2,1)} %bitcast.18), kind=kOutput, calls=%fused_computation.9 | convolution fusion | flops 1611005952 | bytes 6553600 | tf_op jit(solution)/shard_map/dot_general | solution.py:166
  180.0 5.6 %all-to-all-done.2 = bf16[8,16,1024]{2,1,0:T(8,128)(2,1)S(1)} async-done(((bf16[8,16,1024]{2,1,0:T(8,128)(2,1)}), bf16[8,16,1024]{2,1,0:T(8,128)(2,1)S(1)}, u32[]{:S(2)}, u32[]{:S(2)}) %all-to-all-start.2) | async-done | bytes 262176 | tf_op jit(solution)/shard_map/all_to_all | solution.py:102
  (98 shorter events, 38.5 us)
Async XLA Ops:
  0.6 3.3 %copy-start = (bf16[384,2048]{1,0:T(8,128)(2,1)S(1)}, bf16[384,2048]{1,0:T(8,128)(2,1)}, u32[]{:S(2)}) copy-start(bf16[384,2048]{1,0:T(8,128)(2,1)} %param.13) | copy-start | bytes 4718596
  0.6 23.8 %collective-permute-start = (bf16[384,1024]{1,0:T(8,128)(2,1)}, bf16[384,1024]{1,0:T(8,128)(2,1)S(1)}, u32[]{:S(2)}, u32[]{:S(2)}) collective-permute-start(bf16[384,1024]{1,0:T(8,128)(2,1)} %refs_0_.1), channel_id=1, source_target_pairs={{0,64},{64,128},{128,192},{192,0},{1,65},{65,129},{129,193},{193,1... | collective-permute-start | bytes 2359304 | tf_op jit(solution)/shard_map/ppermute | solution.py:120
  2.2 22.2 %collective-permute-start.1 = (bf16[384,1024]{1,0:T(8,128)(2,1)}, bf16[384,1024]{1,0:T(8,128)(2,1)}, u32[]{:S(2)}, u32[]{:S(2)}) collective-permute-start(bf16[384,1024]{1,0:T(8,128)(2,1)} %refs_0_.1), channel_id=1, source_target_pairs={{0,192},{64,0},{128,64},{192,128},{1,193},{65,1},{129,65},{193,129... | collective-permute-start | bytes 2359304 | tf_op jit(solution)/shard_map/ppermute | solution.py:121
  24.4 16.9 %copy-start.6 = (bf16[384,1024]{1,0:T(8,128)(2,1)}, bf16[384,1024]{1,0:T(8,128)(2,1)S(1)}, u32[]{:S(2)}) copy-start(bf16[384,1024]{1,0:T(8,128)(2,1)S(1)} %collective-permute-done) | copy-start | bytes 2359300
  24.4 16.0 %collective-permute-start.3 = (bf16[128,1024]{1,0:T(8,128)(2,1)S(1)}, bf16[128,1024]{1,0:T(8,128)(2,1)}, u32[]{:S(2)}, u32[]{:S(2)}) collective-permute-start(bf16[128,1024]{1,0:T(8,128)(2,1)S(1)} %bitcast.19), channel_id=1, source_target_pairs={{0,64},{64,128},{128,192},{192,0},{1,65},{65,129},{129,193},{193,1... | collective-permute-start | bytes 786440 | tf_op jit(solution)/shard_map/ppermute | solution.py:29
  24.8 19.0 %collective-permute-start.2 = (bf16[128,1024]{1,0:T(8,128)(2,1)S(1)}, bf16[128,1024]{1,0:T(8,128)(2,1)}, u32[]{:S(2)}, u32[]{:S(2)}) collective-permute-start(bf16[128,1024]{1,0:T(8,128)(2,1)S(1)} %bitcast.20), channel_id=1, source_target_pairs={{0,192},{64,0},{128,64},{192,128},{1,193},{65,1},{129,65},{193,129... | collective-permute-start | bytes 786440 | tf_op jit(solution)/shard_map/ppermute | solution.py:30
  29.0 37.9 %all-to-all-start.1 = ((bf16[128,3,1024]{2,1,0:T(4,128)(2,1)}), bf16[128,3,1024]{2,1,0:T(4,128)(2,1)}, u32[]{:S(2)}, u32[]{:S(2)}) async-start(bf16[128,3,1024]{2,1,0:T(4,128)(2,1)} %all_to_all.15), calls=%async_computation.1 | async-start | bytes 2097152 | tf_op jit(solution)/shard_map/all_to_all | solution.py:118
  41.3 7.7 %collective-permute-start.4 = (bf16[64,1024]{1,0:T(8,128)(2,1)S(1)}, bf16[64,1024]{1,0:T(8,128)(2,1)S(1)}, u32[]{:S(2)}, u32[]{:S(2)}) collective-permute-start(bf16[64,1024]{1,0:T(8,128)(2,1)S(1)} %slice.76), channel_id=1, source_target_pairs={{0,64},{64,128},{128,192},{192,0},{1,65},{65,129},{129,193},{193,1... | collective-permute-start | bytes 393224 | tf_op jit(solution)/shard_map/ppermute | solution.py:31
  44.7 6.7 %collective-permute-start.5 = (bf16[64,1024]{1,0:T(8,128)(2,1)S(1)}, bf16[64,1024]{1,0:T(8,128)(2,1)S(1)}, u32[]{:S(2)}, u32[]{:S(2)}) collective-permute-start(bf16[64,1024]{1,0:T(8,128)(2,1)S(1)} %slice.77), channel_id=1, source_target_pairs={{0,192},{64,0},{128,64},{192,128},{1,193},{65,1},{129,65},{193,129... | collective-permute-start | bytes 393224 | tf_op jit(solution)/shard_map/ppermute | solution.py:32
  53.7 26.7 %collective-permute-start.6 = (bf16[4,128,1024]{2,1,0:T(8,128)(2,1)}, bf16[4,128,1024]{2,1,0:T(8,128)(2,1)S(1)}, u32[]{:S(2)}, u32[]{:S(2)}) collective-permute-start(bf16[4,128,1024]{2,1,0:T(8,128)(2,1)} %bitcast.2.refs_1_), channel_id=1, source_target_pairs={{0,16},{16,32},{32,48},{48,0},{1,17},{17,33},{33,49},{49,1},{2,18}... | collective-permute-start | bytes 3145736 | tf_op jit(solution)/shard_map/ppermute | solution.py:130
  53.7 27.7 %collective-permute-start.7 = (bf16[4,128,1024]{2,1,0:T(8,128)(2,1)}, bf16[4,128,1024]{2,1,0:T(8,128)(2,1)}, u32[]{:S(2)}, u32[]{:S(2)}) collective-permute-start(bf16[4,128,1024]{2,1,0:T(8,128)(2,1)} %bitcast.2.refs_1_), channel_id=1, source_target_pairs={{0,48},{16,0},{32,16},{48,32},{1,49},{17,1},{33,17},{49,33},{2,50}... | collective-permute-start | bytes 3145736 | tf_op jit(solution)/shard_map/ppermute | solution.py:131
  70.1 27.2 %copy-start.1 = (bf16[384,1024]{1,0:T(8,128)(2,1)S(1)}, bf16[384,1024]{1,0:T(8,128)(2,1)}, u32[]{:S(2)}) copy-start(bf16[384,1024]{1,0:T(8,128)(2,1)} %refs_0_.1) | copy-start | bytes 2359300
  81.5 14.7 %collective-permute-start.8 = (bf16[2,128,1024]{2,1,0:T(8,128)(2,1)S(1)}, bf16[2,128,1024]{2,1,0:T(8,128)(2,1)S(1)}, u32[]{:S(2)}, u32[]{:S(2)}) collective-permute-start(bf16[2,128,1024]{2,1,0:T(8,128)(2,1)S(1)} %slice.58), channel_id=1, source_target_pairs={{0,16},{16,32},{32,48},{48,0},{1,17},{17,33},{33,49},{49,1},{2,18}... | collective-permute-start | bytes 1572872 | tf_op jit(solution)/shard_map/ppermute | solution.py:133
  84.2 13.1 %collective-permute-start.9 = (bf16[2,128,1024]{2,1,0:T(8,128)(2,1)S(1)}, bf16[2,128,1024]{2,1,0:T(8,128)(2,1)S(1)}, u32[]{:S(2)}, u32[]{:S(2)}) collective-permute-start(bf16[2,128,1024]{2,1,0:T(8,128)(2,1)S(1)} %slice.59), channel_id=1, source_target_pairs={{0,48},{16,0},{32,16},{48,32},{1,49},{17,1},{33,17},{49,33},{2,50}... | collective-permute-start | bytes 1572872 | tf_op jit(solution)/shard_map/ppermute | solution.py:134
  85.8 9.8 %collective-permute-start.10 = (bf16[192,1024]{1,0:T(8,128)(2,1)S(1)}, bf16[192,1024]{1,0:T(8,128)(2,1)S(1)}, u32[]{:S(2)}, u32[]{:S(2)}) collective-permute-start(bf16[192,1024]{1,0:T(8,128)(2,1)S(1)} %slice.60), channel_id=1, source_target_pairs={{0,64},{64,128},{128,192},{192,0},{1,65},{65,129},{129,193},{193,1... | collective-permute-start | bytes 1179656 | tf_op jit(solution)/shard_map/ppermute | solution.py:126
  87.8 17.4 %copy-start.15 = (s32[384]{0:T(512)S(1)}, s32[384]{0:T(512)}, u32[]{:S(2)}) copy-start(s32[384]{0:T(512)} %param.15) | copy-start | bytes 4612
  87.8 8.3 %collective-permute-start.11 = (bf16[192,1024]{1,0:T(8,128)(2,1)S(1)}, bf16[192,1024]{1,0:T(8,128)(2,1)S(1)}, u32[]{:S(2)}, u32[]{:S(2)}) collective-permute-start(bf16[192,1024]{1,0:T(8,128)(2,1)S(1)} %slice.61), channel_id=1, source_target_pairs={{0,192},{64,0},{128,64},{192,128},{1,193},{65,1},{129,65},{193,129... | collective-permute-start | bytes 1179656 | tf_op jit(solution)/shard_map/ppermute | solution.py:127
  104.5 6.0 %collective-permute-start.12 = (f32[384,2048]{1,0:T(8,128)}, f32[384,2048]{1,0:T(8,128)}, u32[]{:S(2)}, u32[]{:S(2)}) collective-permute-start(f32[384,2048]{1,0:T(8,128)} %get-tuple-element.37), channel_id=1, source_target_pairs={{0,1},{1,0},{2,3},{3,2},{4,5},{5,4},{6,7},{7,6},{8,9},{9,8},{10,11... | collective-permute-start | bytes 9437192 | tf_op jit(solution)/shard_map/ppermute | solution.py:148
  105.2 5.3 %copy-start.14 = (f32[2048]{0:T(1024)S(1)}, f32[2048]{0:T(1024)}, u32[]{:S(2)}) copy-start(f32[2048]{0:T(1024)} %param.10) | copy-start | bytes 24580
  109.4 5.3 %collective-permute-start.13 = (bf16[384,1024]{1,0:T(8,128)(2,1)S(1)}, bf16[384,1024]{1,0:T(8,128)(2,1)S(1)}, u32[]{:S(2)}, u32[]{:S(2)}) collective-permute-start(bf16[384,1024]{1,0:T(8,128)(2,1)S(1)} %broadcast_select_fusion), channel_id=1, source_target_pairs={{0,1},{1,0},{2,3},{3,2},{4,5},{5,4},{6,7},{7,6},{8,9},{9,8},{10,11... | collective-permute-start | bytes 2359304 | tf_op jit(solution)/shard_map/ppermute | solution.py:142
  118.8 17.5 %collective-permute-start.15 = (bf16[576,512]{1,0:T(8,128)(2,1)}, bf16[576,512]{1,0:T(8,128)(2,1)S(1)}, u32[]{:S(2)}, u32[]{:S(2)}) collective-permute-start(bf16[576,512]{1,0:T(8,128)(2,1)} %pad_maximum_fusion.1), channel_id=1, source_target_pairs={{0,64},{64,128},{128,192},{192,0},{1,65},{65,129},{129,193},{193,1... | collective-permute-start | bytes 1769480 | tf_op jit(solution)/shard_map/ppermute | solution.py:55
  119.9 16.6 %collective-permute-start.14 = (bf16[576,512]{1,0:T(8,128)(2,1)}, bf16[576,512]{1,0:T(8,128)(2,1)S(1)}, u32[]{:S(2)}, u32[]{:S(2)}) collective-permute-start(bf16[576,512]{1,0:T(8,128)(2,1)} %pad_maximum_fusion), channel_id=1, source_target_pairs={{0,192},{64,0},{128,64},{192,128},{1,193},{65,1},{129,65},{193,129... | collective-permute-start | bytes 1769480 | tf_op jit(solution)/shard_map/ppermute | solution.py:56
  124.7 19.7 %copy-start.12 = (bf16[192,1024]{1,0:T(8,128)(2,1)S(1)}, bf16[192,1024]{1,0:T(8,128)(2,1)}, u32[]{:S(2)}) copy-start(bf16[192,1024]{1,0:T(8,128)(2,1)} %copy-done.11) | copy-start | bytes 1179652
  136.3 8.0 %collective-permute-start.16 = (bf16[192,512]{1,0:T(8,128)(2,1)S(1)}, bf16[192,512]{1,0:T(8,128)(2,1)S(1)}, u32[]{:S(2)}, u32[]{:S(2)}) collective-permute-start(bf16[192,512]{1,0:T(8,128)(2,1)S(1)} %slice.79), channel_id=1, source_target_pairs={{0,64},{64,128},{128,192},{192,0},{1,65},{65,129},{129,193},{193,1... | collective-permute-start | bytes 589832 | tf_op jit(solution)/shard_map/ppermute | solution.py:57
  136.5 8.3 %collective-permute-start.17 = (bf16[192,512]{1,0:T(8,128)(2,1)S(1)}, bf16[192,512]{1,0:T(8,128)(2,1)S(1)}, u32[]{:S(2)}, u32[]{:S(2)}) collective-permute-start(bf16[192,512]{1,0:T(8,128)(2,1)S(1)} %slice.80), channel_id=1, source_target_pairs={{0,192},{64,0},{128,64},{192,128},{1,193},{65,1},{129,65},{193,129... | collective-permute-start | bytes 589832 | tf_op jit(solution)/shard_map/ppermute | solution.py:58
  142.3 3.0 %copy-start.7 = (bf16[384,1024]{1,0:T(8,128)(2,1)S(1)}, bf16[384,1024]{1,0:T(8,128)(2,1)}, u32[]{:S(2)}) copy-start(bf16[384,1024]{1,0:T(8,128)(2,1)} %copy-done.6) | copy-start | bytes 2359300
  148.2 5.8 %collective-permute-start.18 = (bf16[64,1024]{1,0:T(8,128)(2,1)}, bf16[64,1024]{1,0:T(8,128)(2,1)S(1)}, u32[]{:S(2)}, u32[]{:S(2)}) collective-permute-start(bf16[64,1024]{1,0:T(8,128)(2,1)} %get-tuple-element.57), channel_id=1, source_target_pairs={{0,16},{16,32},{32,48},{48,0},{1,17},{17,33},{33,49},{49,1},{2,18}... | collective-permute-start | bytes 393224 | tf_op jit(solution)/shard_map/ppermute | solution.py:39
  151.2 6.2 %collective-permute-start.20 = (bf16[64,1024]{1,0:T(8,128)(2,1)S(1)}, bf16[64,1024]{1,0:T(8,128)(2,1)S(1)}, u32[]{:S(2)}, u32[]{:S(2)}) collective-permute-start(bf16[64,1024]{1,0:T(8,128)(2,1)S(1)} %get-tuple-element.58), channel_id=1, source_target_pairs={{0,48},{16,0},{32,16},{48,32},{1,49},{17,1},{33,17},{49,33},{2,50}... | collective-permute-start | bytes 393224 | tf_op jit(solution)/shard_map/ppermute | solution.py:40
  152.2 22.9 %copy-start.5 = (bf16[384,2048]{1,0:T(8,128)(2,1)S(1)}, bf16[384,2048]{1,0:T(8,128)(2,1)}, u32[]{:S(2)}) copy-start(bf16[384,2048]{1,0:T(8,128)(2,1)} %copy-done.4) | copy-start | bytes 4718596
  159.2 6.6 %collective-permute-start.19 = (bf16[128,1024]{1,0:T(8,128)(2,1)}, bf16[128,1024]{1,0:T(8,128)(2,1)S(1)}, u32[]{:S(2)}, u32[]{:S(2)}) collective-permute-start(bf16[128,1024]{1,0:T(8,128)(2,1)} %pad_maximum_fusion.2), channel_id=1, source_target_pairs={{0,16},{16,32},{32,48},{48,0},{1,17},{17,33},{33,49},{49,1},{2,18}... | collective-permute-start | bytes 786440 | tf_op jit(solution)/shard_map/ppermute | solution.py:44
  160.1 7.9 %collective-permute-start.21 = (bf16[128,1024]{1,0:T(8,128)(2,1)}, bf16[128,1024]{1,0:T(8,128)(2,1)}, u32[]{:S(2)}, u32[]{:S(2)}) collective-permute-start(bf16[128,1024]{1,0:T(8,128)(2,1)} %pad_maximum_fusion.3), channel_id=1, source_target_pairs={{0,48},{16,0},{32,16},{48,32},{1,49},{17,1},{33,17},{49,33},{2,50}... | collective-permute-start | bytes 786440 | tf_op jit(solution)/shard_map/ppermute | solution.py:45
  169.9 15.7 %all-to-all-start.2 = ((bf16[8,16,1024]{2,1,0:T(8,128)(2,1)}), bf16[8,16,1024]{2,1,0:T(8,128)(2,1)S(1)}, u32[]{:S(2)}, u32[]{:S(2)}) async-start(bf16[8,16,1024]{2,1,0:T(8,128)(2,1)} %bitcast.5), calls=%async_computation.2 | async-start | bytes 524288 | tf_op jit(solution)/shard_map/all_to_all | solution.py:102
  (8 other events, 11.8 us)

commit v6 on v5

--- a/solution.py
+++ b/solution.py
@@ -9,6 +9,7 @@
 BF16 = jnp.bfloat16
 RIGHT = [(i, (i + 1) % 4) for i in range(4)]
 LEFT = [(i, (i - 1) % 4) for i in range(4)]
+ACROSS = [(i, (i + 2) % 4) for i in range(4)]
 
 
 def norm_back(projected, residual, bias_out, norm_gain, grad_out):
@@ -46,6 +47,19 @@
     return chunk_of(0) + from_before.astype(F32) + from_after.astype(F32)
 
 
+def ring_reduce(chunk_of, axis):
+    far = chunk_of(2).astype(BF16)
+    mid = far.shape[0] // 2
+    top = lax.ppermute(far[:mid], axis, RIGHT)
+    bottom = lax.ppermute(far[mid:], axis, LEFT)
+    ahead, behind = chunk_of(1), chunk_of(3)
+    ahead = jnp.concatenate([ahead[:mid] + top.astype(F32), ahead[mid:]]).astype(BF16)
+    behind = jnp.concatenate([behind[:mid], behind[mid:] + bottom.astype(F32)]).astype(BF16)
+    from_before = lax.ppermute(ahead, axis, RIGHT)
+    from_after = lax.ppermute(behind, axis, LEFT)
+    return chunk_of(0) + from_before.astype(F32) + from_after.astype(F32)
+
+
 def ring_columns(columns_of, axis):
     far = columns_of(2)
     rows = far.shape[0]
@@ -62,26 +76,41 @@
 def project_kernel(*refs):
     context_ref, pieces = refs[0], refs[1:6]
     weight_ref, out_ref = refs[6], refs[7]
+    placed, sems = refs[8], refs[9]
     ix, iy = lax.axis_index("x"), lax.axis_index("y")
     for ref, step, low in zip(pieces, (0, 1, 2, 2, 3), (0, 0, 0, 2, 0)):
         at = lax.rem(iy + step, 4)
         for k in range(ref.shape[0]):
-            weight_ref[lax.rem(ix + low + k, 4), at] = ref[k]
+            placed[lax.rem(ix + low + k, 4), at] = ref[k]
+    copies = [
+        pltpu.make_async_copy(placed.at[x], weight_ref.at[x], sems.at[x]) for x in range(4)
+    ]
+    for copy in copies:
+        copy.start()
     for x in range(4):
-        block = weight_ref[x].reshape(512, 1024)
+        block = placed[x].reshape(512, 1024)
         out_ref[:, x * 512:(x + 1) * 512] = lax.dot_general(
             context_ref[...], block, (((1,), (1,)), ((), ())), preferred_element_type=F32
         )
+    for copy in copies:
+        copy.wait()
 
 
 def project(context, pieces):
     rows = context.shape[0]
+    vmem = pl.BlockSpec(memory_space=pltpu.VMEM)
     return pl.pallas_call(
         project_kernel,
         out_shape=(
             jax.ShapeDtypeStruct((4, 4, 128, 1024), BF16),
             jax.ShapeDtypeStruct((rows, 2048), F32),
         ),
+        in_specs=[vmem] * 6,
+        out_specs=(pl.BlockSpec(memory_space=pltpu.HBM), vmem),
+        scratch_shapes=[
+            pltpu.VMEM((4, 4, 128, 1024), BF16),
+            pltpu.SemaphoreType.DMA((4,)),
+        ],
         compiler_params=pltpu.CompilerParams(vmem_limit_bytes=40 << 20),
         cost_estimate=pl.CostEstimate(
             flops=2 * rows * 1024 * 2048, bytes_accessed=16 << 20, transcendentals=0
@@ -129,11 +158,11 @@
     block = jnp.concatenate(ring_gather(block, "x")).reshape(4, 128, 1024)
     before = lax.ppermute(block, "y", RIGHT)
     after = lax.ppermute(block, "y", LEFT)
-    before, after, returned = lax.optimization_barrier((before, after, returned))
+    before, after, context_pieces = lax.optimization_barrier((before, after, context_pieces))
     top = lax.ppermute(before[:2], "y", RIGHT)
     bottom = lax.ppermute(after[2:], "y", LEFT)
     pieces = (block, after, top, bottom, before)
-    pieces, returned, context_pieces = lax.optimization_barrier((pieces, returned, context_pieces))
+    pieces, returned = lax.optimization_barrier((pieces, returned))
 
     weight_t, partial_proj = project(context, pieces)
     weight_t = weight_t.reshape(2048, 1024)
@@ -152,11 +181,33 @@
         at = lax.rem(ix + step, 4)
         return lax.dynamic_slice_in_dim(grad_resid, at * 512, 512, axis=1)
 
-    share = jnp.zeros((), F32)
-    for columns, rows in zip(ring_columns(columns_of, "x"), context_pieces):
-        share = share + lax.dot_general(
+    def product(columns, rows):
+        return lax.dot_general(
             columns, rows, (((0,), (0,)), ((), ())), preferred_element_type=F32
         )
+
+    def half_of(step):
+        at = lax.rem(ix + step, 4)
+        return lax.dynamic_slice(grad_resid, (core * mid, at * 512), (mid, 512))
+
+    fetched = jnp.concatenate([
+        lax.ppermute(half_of(3), "x", LEFT),
+        lax.ppermute(half_of(2), "x", ACROSS),
+        lax.ppermute(half_of(1), "x", RIGHT),
+    ])
+    swapped = lax.ppermute(fetched, "core", swap)
+    far_rows = jnp.concatenate(context_pieces[2:4])
+    three = (context_pieces[1], far_rows, context_pieces[4])
+
+    def halves(which):
+        return jnp.concatenate(
+            [lax.dynamic_slice_in_dim(rows, which * mid, mid, axis=0) for rows in three]
+        )
+
+    share = product(columns_of(0), context)
+    share = share + product(fetched, halves(core))
+    share = share + product(swapped, halves(1 - core))
+
     def strip_of(step):
         return lax.dynamic_slice_in_dim(share, lax.rem(iy + step, 4) * 128, 128, axis=0)
 

time: 188 us -> 173 us (0.920)
  waiting for transfers between devices: 62.4 us -> 53.6 us
  matrix products: 10.2 us -> 7.6 us
  local copies, waits for them, and re-layouts: 26.1 us -> 24.2 us
    ppermute x1, waiting for transfers between devices: 10.3 us -> 0.01 us  [shards(): before = lax.ppermute(block, 'y', RIGHT)]
    all_to_all x1, waiting for transfers between devices: 11.1 us -> 1.78 us  [shards(): lax.all_to_all(mine, ('x', 'y', 'z'), split_axis=0, concat_axis=0, tiled=...]
    ppermute x1, waiting for transfers between devices: 5.2 us -> 10.8 us  [shards(): context_top = lax.ppermute(context_before[:mid], 'x', RIGHT)]
    ppermute x1, waiting for transfers between devices: 0.01 us -> 4.35 us  [ring_gather(): before = lax.ppermute(piece, axis, RIGHT)]
    ppermute x1, waiting for transfers between devices: 0.01 us -> 3.23 us  [shards(): top = lax.ppermute(before[:2], 'y', RIGHT)]
    ppermute x1, starting transfers between devices: 2.94 us -> 0.01 us  [ring_reduce(): top = lax.ppermute(far[:mid], axis, RIGHT)]
    ppermute x4, starting transfers between devices: 7.28 us -> 4.7 us  [the longest x1 3.58 us: shards(): lax.ppermute(half_of(3), 'x', LEFT)]
    dot_general x5 -> x3, matrix products: 5.32 us -> 2.75 us  [product(): lax.dot_general(columns, rows, (((0,), (0,)), ((), ())), preferred_elemen...]
  transfers between devices with their start and end apart: 24 -> 24, of which waited for: 17 -> 15; matrix products, arithmetic and copies ran while one was open for 17% -> 15% of each run, Pallas kernels for 0% -> 0%
where the time goes in v6:
time: 173 us; the launch traced here: 172 us
  waiting for transfers between devices  53.6 us (31%)
  starting transfers between devices  46.3 us (27%)
  local copies, waits for them, and re-layouts  24.2 us (14%)
  blocking collectives  19.6 us (11%)
  other arithmetic  13.2 us (8%)
  matrix products  7.6 us (4%)
  Pallas kernels  5.91 us (3%)
  between operations  1.74 us (1%)
    all_to_all x1, blocking collectives, spread(): return lax.all_to_all(whole, axis, split_axis=0, concat_axis=0)  19.6 us
    all_to_all x1, starting transfers between devices, shards(): lax.all_to_all(mine, ('x', 'y', 'z'), split_axis=0, concat_axis=0, tiled=...  13.9 us
    ppermute x1, waiting for transfers between devices, shards(): context_top = lax.ppermute(context_before[:mid], 'x', RIGHT)  10.8 us
    ppermute x1, waiting for transfers between devices, shards(): lax.ppermute(half_of(3), 'x', LEFT)  7.58 us
    unnamed x47, local copies, waits for them, and re-layouts  7.39 us
    pallas_call x1, Pallas kernels, project(): pl.pallas_call(project_kernel, out_shape=(jax.ShapeDtypeStruct((4, 4, 128...  5.91 us
    all_to_all x1, waiting for transfers between devices, collect(): got = lax.all_to_all(share, axis, split_axis=0, concat_axis=0)  5.79 us
    all_to_all x1, starting transfers between devices, collect(): got = lax.all_to_all(share, axis, split_axis=0, concat_axis=0)  5.52 us
  transfers between devices with their start and end apart: 24, of which 15 were waited for; matrix products, arithmetic and copies ran while one was open for 15% of the time, Pallas kernels for 0%

profile of v6, /device:TPU:24, one launch (start us, length us, event | category | flops | bytes accessed | tf_op | source)
XLA Modules:
  0.0 172.2 jit_solution(16507767183358099457)
XLA Ops:
  2.2 1.7 %collective-permute-start.1 = (bf16[384,1024]{1,0:T(8,128)(2,1)}, bf16[384,1024]{1,0:T(8,128)(2,1)}, u32[]{:S(2)}, u32[]{:S(2)}) collective-permute-start(bf16[384,1024]{1,0:T(8,128)(2,1)} %refs_0_.1), channel_id=1, source_target_pairs={{0,192},{64,0},{128,64},{192,128},{1,193},{65,1},{129,65},{193,129... | collective-permute-start | bytes 2359304 | tf_op jit(solution)/shard_map/ppermute | solution.py:150
  4.8 19.6 %all_to_all.22 = bf16[8,16,1024]{2,1,0:T(8,128)(2,1)S(1)} all-to-all(bf16[8,16,1024]{2,1,0:T(8,128)(2,1)S(1)} %broadcast_in_dim.16), channel_id=1, replica_groups=mesh['x'=4,'y'=4,'z'=8,'core'=2] {'z'}, dimensions={0} | all-to-all | bytes 524288 | tf_op jit(solution)/shard_map/all_to_all | solution.py:125
  24.8 3.0 %collective-permute-start.2 = (bf16[128,1024]{1,0:T(8,128)(2,1)S(1)}, bf16[128,1024]{1,0:T(8,128)(2,1)S(1)}, u32[]{:S(2)}, u32[]{:S(2)}) collective-permute-start(bf16[128,1024]{1,0:T(8,128)(2,1)S(1)} %bitcast.16), channel_id=1, source_target_pairs={{0,192},{64,0},{128,64},{192,128},{1,193},{65,1},{129,65},{193,129... | collective-permute-start | bytes 786440 | tf_op jit(solution)/shard_map/ppermute | solution.py:31
  27.7 4.3 %collective-permute-done.3 = bf16[128,1024]{1,0:T(8,128)(2,1)S(1)} collective-permute-done((bf16[128,1024]{1,0:T(8,128)(2,1)S(1)}, bf16[128,1024]{1,0:T(8,128)(2,1)S(1)}, u32[]{:S(2)}, u32[]{:S(2)}) %collective-permute-start.3) | collective-permute-done | bytes 262176 | tf_op jit(solution)/shard_map/ppermute | solution.py:30
  32.9 3.3 %collective-permute-start.5 = (bf16[64,1024]{1,0:T(8,128)(2,1)S(1)}, bf16[64,1024]{1,0:T(8,128)(2,1)S(1)}, u32[]{:S(2)}, u32[]{:S(2)}) collective-permute-start(bf16[64,1024]{1,0:T(8,128)(2,1)S(1)} %slice.53), channel_id=1, source_target_pairs={{0,192},{64,0},{128,64},{192,128},{1,193},{65,1},{129,65},{193,129... | collective-permute-start | bytes 393224 | tf_op jit(solution)/shard_map/ppermute | solution.py:33
  40.6 1.8 %collective-permute-start.7 = (bf16[4,128,1024]{2,1,0:T(8,128)(2,1)}, bf16[4,128,1024]{2,1,0:T(8,128)(2,1)}, u32[]{:S(2)}, u32[]{:S(2)}) collective-permute-start(bf16[4,128,1024]{2,1,0:T(8,128)(2,1)} %bitcast.2.refs_1_), channel_id=1, source_target_pairs={{0,48},{16,0},{32,16},{48,32},{1,49},{17,1},{33,17},{49,33},{2,50}... | collective-permute-start | bytes 3145736 | tf_op jit(solution)/shard_map/ppermute | solution.py:160
  43.7 13.9 %all-to-all-start.1 = ((bf16[128,3,1024]{2,1,0:T(4,128)(2,1)}), bf16[128,3,1024]{2,1,0:T(4,128)(2,1)}, u32[]{:S(2)}, u32[]{:S(2)}) async-start(bf16[128,3,1024]{2,1,0:T(4,128)(2,1)} %all_to_all.15), calls=%async_computation.1 | async-start | bytes 2097152 | tf_op jit(solution)/shard_map/all_to_all | solution.py:147
  57.6 1.8 %collective-permute-start.8 = (bf16[192,1024]{1,0:T(8,128)(2,1)S(1)}, bf16[192,1024]{1,0:T(8,128)(2,1)S(1)}, u32[]{:S(2)}, u32[]{:S(2)}) collective-permute-start(bf16[192,1024]{1,0:T(8,128)(2,1)S(1)} %slice.40), channel_id=1, source_target_pairs={{0,64},{64,128},{128,192},{192,0},{1,65},{65,129},{129,193},{193,1... | collective-permute-start | bytes 1179656 | tf_op jit(solution)/shard_map/ppermute | solution.py:155
  60.4 1.8 %collective-permute-start.9 = (bf16[192,1024]{1,0:T(8,128)(2,1)S(1)}, bf16[192,1024]{1,0:T(8,128)(2,1)S(1)}, u32[]{:S(2)}, u32[]{:S(2)}) collective-permute-start(bf16[192,1024]{1,0:T(8,128)(2,1)S(1)} %slice.41), channel_id=1, source_target_pairs={{0,192},{64,0},{128,64},{192,128},{1,193},{65,1},{129,65},{193,129... | collective-permute-start | bytes 1179656 | tf_op jit(solution)/shard_map/ppermute | solution.py:156
  62.2 10.8 %collective-permute-done.8 = bf16[192,1024]{1,0:T(8,128)(2,1)S(1)} collective-permute-done((bf16[192,1024]{1,0:T(8,128)(2,1)S(1)}, bf16[192,1024]{1,0:T(8,128)(2,1)S(1)}, u32[]{:S(2)}, u32[]{:S(2)}) %collective-permute-start.8) | collective-permute-done | bytes 393248 | tf_op jit(solution)/shard_map/ppermute | solution.py:155
  73.1 1.6 collective-permute-done.9
  76.8 1.9 %slice.43 = bf16[2,128,1024]{2,1,0:T(8,128)(2,1)} slice(bf16[4,128,1024]{2,1,0:T(8,128)(2,1)} %collective-permute-done.7.refs_2_), slice={[2:4], [0:128], [0:1024]} | slice | bytes 1048576 | tf_op jit(solution)/shard_map/slice | solution.py:163
  80.2 1.8 %all-to-all-done.1 = bf16[128,3,1024]{2,1,0:T(4,128)(2,1)} async-done(((bf16[128,3,1024]{2,1,0:T(4,128)(2,1)}), bf16[128,3,1024]{2,1,0:T(4,128)(2,1)}, u32[]{:S(2)}, u32[]{:S(2)}) %all-to-all-start.1) | async-done | bytes 786464 | tf_op jit(solution)/shard_map/all_to_all | solution.py:147
  82.0 3.2 %all_to_all.17 = bf16[384,1024]{1,0:T(8,128)(2,1)} reshape(bf16[128,3,1024]{2,1,0:T(4,128)(2,1)} %all-to-all-done.1) | data formatting | bytes 1572864 | tf_op jit(solution)/shard_map/all_to_all | solution.py:147
  85.2 3.2 %collective-permute-done.10.refs_3_ = bf16[2,128,1024]{2,1,0:T(8,128)(2,1)} collective-permute-done((bf16[2,128,1024]{2,1,0:T(8,128)(2,1)}, bf16[2,128,1024]{2,1,0:T(8,128)(2,1)}, u32[]{:S(2)}, u32[]{:S(2)}) %collective-permute-start.10) | collective-permute-done | bytes 524320 | tf_op jit(solution)/shard_map/ppermute | solution.py:162
  88.4 1.8 %collective-permute-done.11.refs_4_ = bf16[2,128,1024]{2,1,0:T(8,128)(2,1)} collective-permute-done((bf16[2,128,1024]{2,1,0:T(8,128)(2,1)}, bf16[2,128,1024]{2,1,0:T(8,128)(2,1)}, u32[]{:S(2)}, u32[]{:S(2)}) %collective-permute-start.11) | collective-permute-done | bytes 524320 | tf_op jit(solution)/shard_map/ppermute | solution.py:163
  90.2 5.9 %project.1 = (bf16[4,4,128,1024]{3,2,1,0:T(8,128)(2,1)S(1)}, f32[384,2048]{1,0:T(8,128)}) custom-call(bf16[384,1024]{1,0:T(8,128)(2,1)S(1)} %copy-done.1, bf16[4,128,1024]{2,1,0:T(8,128)(2,1)} %bitcast.2.refs_1_, bf16[4,128,1024]{2,1,0:T(8,128)(2,1)} %collective-permute-done.7.refs_2_, bf16[2,128,1024]{2,1,0:T(8,128)(2,1)} %collective-permute-done.10.refs_3_, ...), custom_call_target="tpu_custom_call" | custom-call | flops 1610612736 | bytes 16777216 | tf_op jit(solution)/shard_map/project/pallas_call | solution.py:102
  96.2 2.0 %copy-done.2 = bf16[4,4,128,1024]{3,2,1,0:T(8,128)(2,1)} copy-done((bf16[4,4,128,1024]{3,2,1,0:T(8,128)(2,1)}, bf16[4,4,128,1024]{3,2,1,0:T(8,128)(2,1)S(1)}, u32[]{:S(2)}) %copy-start.2) | copy-done | bytes 4194328
  98.9 2.4 %constant_dynamic-slice_fusion = (bf16[192,1024]{1,0:T(8,128)(2,1)S(1)}, bf16[192,1024]{1,0:T(8,128)(2,1)}, bf16[192,1024]{1,0:T(8,128)(2,1)}, bf16[192,1024]{1,0:T(8,128)(2,1)}) fusion(bf16[384,1024]{1,0:T(8,128)(2,1)} %copy-done.7, s32[]{:T(128)S(6)} %select_n.65, s32[]{:T(128)S(6)} %select_n.61, bf16[384,1024]{1,0:T(8,128)(2,1)} %collective-permute-done.1), kind=kLoop, calls=%fused_computation.48 | loop fusion | bytes 3145736 | tf_op jit(solution)/shard_map/dynamic_slice | solution.py:204
  101.3 2.7 %gather_fusion = bf16[384,1024]{1,0:T(8,128)(2,1)} fusion(bf16[384,1024]{1,0:T(8,128)(2,1)S(1)} %copy-done.3, s32[1024]{0:T(1024)S(1)} %pad_clamp_fusion), kind=kCustom, calls=%fused_computation | custom fusion | bytes 1574400 | tf_op jit(solution)/shard_map/gather | solution.py:169
  105.9 3.6 %fusion.19 = (f32[384]{0:T(512)S(1)}, f32[384,2048]{1,0:T(8,128)S(1)}) fusion(f32[2048]{0:T(1024)S(1)} %copy-done.18, f32[384,2048]{1,0:T(8,128)} %get-tuple-element.34, f32[384,2048]{1,0:T(8,128)} %collective-permute-done.12, bf16[384,2048]{1,0:T(8,128)(2,1)S(1)} %copy-done.10), kind=kLoop, calls=%fused_computation.63 | loop fusion | flops 3931776 | bytes 11019776 | tf_op jit(solution)/shard_map/reduce_sum | solution.py:17
  112.9 3.6 %collective-permute-start.14 = (bf16[192,512]{1,0:T(8,128)(2,1)S(1)}, bf16[192,512]{1,0:T(8,128)(2,1)S(1)}, u32[]{:S(2)}, u32[]{:S(2)}) collective-permute-start(bf16[192,512]{1,0:T(8,128)(2,1)S(1)} %get-tuple-element.51), channel_id=1, source_target_pairs={{0,192},{64,0},{128,64},{192,128},{1,193},{65,1},{129,65},{193,129... | collective-permute-start | bytes 589832 | tf_op jit(solution)/shard_map/ppermute | solution.py:194
  117.6 7.6 %collective-permute-done.14 = bf16[192,512]{1,0:T(8,128)(2,1)S(1)} collective-permute-done((bf16[192,512]{1,0:T(8,128)(2,1)S(1)}, bf16[192,512]{1,0:T(8,128)(2,1)S(1)}, u32[]{:S(2)}, u32[]{:S(2)}) %collective-permute-start.14) | collective-permute-done | bytes 196640 | tf_op jit(solution)/shard_map/ppermute | solution.py:194
  125.9 2.9 %collective-permute-done.16 = bf16[192,512]{1,0:T(8,128)(2,1)S(1)} collective-permute-done((bf16[192,512]{1,0:T(8,128)(2,1)S(1)}, bf16[192,512]{1,0:T(8,128)(2,1)S(1)}, u32[]{:S(2)}, u32[]{:S(2)}) %collective-permute-start.16) | collective-permute-done | bytes 196640 | tf_op jit(solution)/shard_map/ppermute | solution.py:196
  134.1 2.0 %collective-permute-start.20 = (bf16[64,1024]{1,0:T(8,128)(2,1)S(1)}, bf16[64,1024]{1,0:T(8,128)(2,1)S(1)}, u32[]{:S(2)}, u32[]{:S(2)}) collective-permute-start(bf16[64,1024]{1,0:T(8,128)(2,1)S(1)} %get-tuple-element.59), channel_id=1, source_target_pairs={{0,48},{16,0},{32,16},{48,32},{1,49},{17,1},{33,17},{49,33},{2,50}... | collective-permute-start | bytes 393224 | tf_op jit(solution)/shard_map/ppermute | solution.py:54
  137.2 2.9 %collective-permute-done.18 = bf16[64,1024]{1,0:T(8,128)(2,1)S(1)} collective-permute-done((bf16[64,1024]{1,0:T(8,128)(2,1)}, bf16[64,1024]{1,0:T(8,128)(2,1)S(1)}, u32[]{:S(2)}, u32[]{:S(2)}) %collective-permute-start.18) | collective-permute-done | bytes 131104 | tf_op jit(solution)/shard_map/ppermute | solution.py:53
  145.7 5.2 %collective-permute-done.19 = bf16[128,1024]{1,0:T(8,128)(2,1)S(1)} collective-permute-done((bf16[128,1024]{1,0:T(8,128)(2,1)}, bf16[128,1024]{1,0:T(8,128)(2,1)S(1)}, u32[]{:S(2)}, u32[]{:S(2)}) %collective-permute-start.19) | collective-permute-done | bytes 262176 | tf_op jit(solution)/shard_map/ppermute | solution.py:58
  150.9 2.5 %collective-permute-done.21 = bf16[128,1024]{1,0:T(8,128)(2,1)} collective-permute-done((bf16[128,1024]{1,0:T(8,128)(2,1)}, bf16[128,1024]{1,0:T(8,128)(2,1)}, u32[]{:S(2)}, u32[]{:S(2)}) %collective-permute-start.21) | collective-permute-done | bytes 262176 | tf_op jit(solution)/shard_map/ppermute | solution.py:59
  153.4 1.9 %add_convert_fusion = bf16[128,1024]{1,0:T(8,128)(2,1)} fusion(bf16[128,1024]{1,0:T(8,128)(2,1)} %collective-permute-done.21, bf16[128,1024]{1,0:T(8,128)(2,1)S(1)} %collective-permute-done.19, f32[512,1024]{1,0:T(8,128)} %copy-done.4, s32[]{:T(128)S(6)} %select_n.66), kind=kLoop, calls=%fused_computation.23 | loop fusion | flops 655360 | bytes 1310724 | tf_op jit(solution)/shard_map/convert_element_type | solution.py:130
  155.3 5.5 %all-to-all-start.2 = ((bf16[8,16,1024]{2,1,0:T(8,128)(2,1)}), bf16[8,16,1024]{2,1,0:T(8,128)(2,1)S(1)}, u32[]{:S(2)}, u32[]{:S(2)}) async-start(bf16[8,16,1024]{2,1,0:T(8,128)(2,1)} %bitcast.5), calls=%async_computation.2 | async-start | bytes 524288 | tf_op jit(solution)/shard_map/all_to_all | solution.py:131
  160.8 4.9 %convolution_convert_fusion = bf16[384,1024]{1,0:T(8,128)(2,1)} fusion(bf16[384,2048]{1,0:T(8,128)(2,1)S(1)} %copy-done.6, bf16[2048,1024]{1,0:T(8,128)(2,1)} %bitcast.14), kind=kOutput, calls=%fused_computation.9 | convolution fusion | flops 1611005952 | bytes 6553600 | tf_op jit(solution)/shard_map/dot_general | solution.py:217
  165.7 5.8 %all-to-all-done.2 = bf16[8,16,1024]{2,1,0:T(8,128)(2,1)S(1)} async-done(((bf16[8,16,1024]{2,1,0:T(8,128)(2,1)}), bf16[8,16,1024]{2,1,0:T(8,128)(2,1)S(1)}, u32[]{:S(2)}, u32[]{:S(2)}) %all-to-all-start.2) | async-done | bytes 262176 | tf_op jit(solution)/shard_map/all_to_all | solution.py:131
  (106 shorter events, 33.6 us)
Async XLA Ops:
  0.6 23.8 %collective-permute-start = (bf16[384,1024]{1,0:T(8,128)(2,1)}, bf16[384,1024]{1,0:T(8,128)(2,1)S(1)}, u32[]{:S(2)}, u32[]{:S(2)}) collective-permute-start(bf16[384,1024]{1,0:T(8,128)(2,1)} %refs_0_.1), channel_id=1, source_target_pairs={{0,64},{64,128},{128,192},{192,0},{1,65},{65,129},{129,193},{193,1... | collective-permute-start | bytes 2359304 | tf_op jit(solution)/shard_map/ppermute | solution.py:149
  2.2 22.2 %collective-permute-start.1 = (bf16[384,1024]{1,0:T(8,128)(2,1)}, bf16[384,1024]{1,0:T(8,128)(2,1)}, u32[]{:S(2)}, u32[]{:S(2)}) collective-permute-start(bf16[384,1024]{1,0:T(8,128)(2,1)} %refs_0_.1), channel_id=1, source_target_pairs={{0,192},{64,0},{128,64},{192,128},{1,193},{65,1},{129,65},{193,129... | collective-permute-start | bytes 2359304 | tf_op jit(solution)/shard_map/ppermute | solution.py:150
  24.4 16.0 %copy-start.7 = (bf16[384,1024]{1,0:T(8,128)(2,1)}, bf16[384,1024]{1,0:T(8,128)(2,1)S(1)}, u32[]{:S(2)}) copy-start(bf16[384,1024]{1,0:T(8,128)(2,1)S(1)} %collective-permute-done) | copy-start | bytes 2359300
  24.4 7.7 %collective-permute-start.3 = (bf16[128,1024]{1,0:T(8,128)(2,1)S(1)}, bf16[128,1024]{1,0:T(8,128)(2,1)S(1)}, u32[]{:S(2)}, u32[]{:S(2)}) collective-permute-start(bf16[128,1024]{1,0:T(8,128)(2,1)S(1)} %bitcast.15), channel_id=1, source_target_pairs={{0,64},{64,128},{128,192},{192,0},{1,65},{65,129},{129,193},{193,1... | collective-permute-start | bytes 786440 | tf_op jit(solution)/shard_map/ppermute | solution.py:30
  24.8 8.1 %collective-permute-start.2 = (bf16[128,1024]{1,0:T(8,128)(2,1)S(1)}, bf16[128,1024]{1,0:T(8,128)(2,1)S(1)}, u32[]{:S(2)}, u32[]{:S(2)}) collective-permute-start(bf16[128,1024]{1,0:T(8,128)(2,1)S(1)} %bitcast.16), channel_id=1, source_target_pairs={{0,192},{64,0},{128,64},{192,128},{1,193},{65,1},{129,65},{193,129... | collective-permute-start | bytes 786440 | tf_op jit(solution)/shard_map/ppermute | solution.py:31
  32.1 6.3 %collective-permute-start.4 = (bf16[64,1024]{1,0:T(8,128)(2,1)S(1)}, bf16[64,1024]{1,0:T(8,128)(2,1)S(1)}, u32[]{:S(2)}, u32[]{:S(2)}) collective-permute-start(bf16[64,1024]{1,0:T(8,128)(2,1)S(1)} %slice.52), channel_id=1, source_target_pairs={{0,64},{64,128},{128,192},{192,0},{1,65},{65,129},{129,193},{193,1... | collective-permute-start | bytes 393224 | tf_op jit(solution)/shard_map/ppermute | solution.py:32
  32.9 6.1 %collective-permute-start.5 = (bf16[64,1024]{1,0:T(8,128)(2,1)S(1)}, bf16[64,1024]{1,0:T(8,128)(2,1)S(1)}, u32[]{:S(2)}, u32[]{:S(2)}) collective-permute-start(bf16[64,1024]{1,0:T(8,128)(2,1)S(1)} %slice.53), channel_id=1, source_target_pairs={{0,192},{64,0},{128,64},{192,128},{1,193},{65,1},{129,65},{193,129... | collective-permute-start | bytes 393224 | tf_op jit(solution)/shard_map/ppermute | solution.py:33
  40.4 34.3 %collective-permute-start.6 = (bf16[4,128,1024]{2,1,0:T(8,128)(2,1)}, bf16[4,128,1024]{2,1,0:T(8,128)(2,1)S(1)}, u32[]{:S(2)}, u32[]{:S(2)}) collective-permute-start(bf16[4,128,1024]{2,1,0:T(8,128)(2,1)} %bitcast.2.refs_1_), channel_id=1, source_target_pairs={{0,16},{16,32},{32,48},{48,0},{1,17},{17,33},{33,49},{49,1},{2,18}... | collective-permute-start | bytes 3145736 | tf_op jit(solution)/shard_map/ppermute | solution.py:159
  40.6 34.9 %collective-permute-start.7 = (bf16[4,128,1024]{2,1,0:T(8,128)(2,1)}, bf16[4,128,1024]{2,1,0:T(8,128)(2,1)}, u32[]{:S(2)}, u32[]{:S(2)}) collective-permute-start(bf16[4,128,1024]{2,1,0:T(8,128)(2,1)} %bitcast.2.refs_1_), channel_id=1, source_target_pairs={{0,48},{16,0},{32,16},{48,32},{1,49},{17,1},{33,17},{49,33},{2,50}... | collective-permute-start | bytes 3145736 | tf_op jit(solution)/shard_map/ppermute | solution.py:160
  43.7 13.9 %copy-start.8 = (bf16[384,1024]{1,0:T(8,128)(2,1)S(1)}, bf16[384,1024]{1,0:T(8,128)(2,1)}, u32[]{:S(2)}) copy-start(bf16[384,1024]{1,0:T(8,128)(2,1)} %copy-done.7) | copy-start | bytes 2359300
  43.7 38.3 %all-to-all-start.1 = ((bf16[128,3,1024]{2,1,0:T(4,128)(2,1)}), bf16[128,3,1024]{2,1,0:T(4,128)(2,1)}, u32[]{:S(2)}, u32[]{:S(2)}) async-start(bf16[128,3,1024]{2,1,0:T(4,128)(2,1)} %all_to_all.15), calls=%async_computation.1 | async-start | bytes 2097152 | tf_op jit(solution)/shard_map/all_to_all | solution.py:147
  57.6 32.6 %copy-start.1 = (bf16[384,1024]{1,0:T(8,128)(2,1)S(1)}, bf16[384,1024]{1,0:T(8,128)(2,1)}, u32[]{:S(2)}) copy-start(bf16[384,1024]{1,0:T(8,128)(2,1)} %refs_0_.1) | copy-start | bytes 2359300
  57.6 15.4 %collective-permute-start.8 = (bf16[192,1024]{1,0:T(8,128)(2,1)S(1)}, bf16[192,1024]{1,0:T(8,128)(2,1)S(1)}, u32[]{:S(2)}, u32[]{:S(2)}) collective-permute-start(bf16[192,1024]{1,0:T(8,128)(2,1)S(1)} %slice.40), channel_id=1, source_target_pairs={{0,64},{64,128},{128,192},{192,0},{1,65},{65,129},{129,193},{193,1... | collective-permute-start | bytes 1179656 | tf_op jit(solution)/shard_map/ppermute | solution.py:155
  60.4 14.3 %collective-permute-start.9 = (bf16[192,1024]{1,0:T(8,128)(2,1)S(1)}, bf16[192,1024]{1,0:T(8,128)(2,1)S(1)}, u32[]{:S(2)}, u32[]{:S(2)}) collective-permute-start(bf16[192,1024]{1,0:T(8,128)(2,1)S(1)} %slice.41), channel_id=1, source_target_pairs={{0,192},{64,0},{128,64},{192,128},{1,193},{65,1},{129,65},{193,129... | collective-permute-start | bytes 1179656 | tf_op jit(solution)/shard_map/ppermute | solution.py:156
  76.3 12.1 %collective-permute-start.10 = (bf16[2,128,1024]{2,1,0:T(8,128)(2,1)}, bf16[2,128,1024]{2,1,0:T(8,128)(2,1)}, u32[]{:S(2)}, u32[]{:S(2)}) collective-permute-start(bf16[2,128,1024]{2,1,0:T(8,128)(2,1)} %slice.42), channel_id=1, source_target_pairs={{0,16},{16,32},{32,48},{48,0},{1,17},{17,33},{33,49},{49,1},{2,18}... | collective-permute-start | bytes 1572872 | tf_op jit(solution)/shard_map/ppermute | solution.py:162
  78.6 11.6 %collective-permute-start.11 = (bf16[2,128,1024]{2,1,0:T(8,128)(2,1)}, bf16[2,128,1024]{2,1,0:T(8,128)(2,1)}, u32[]{:S(2)}, u32[]{:S(2)}) collective-permute-start(bf16[2,128,1024]{2,1,0:T(8,128)(2,1)} %slice.43), channel_id=1, source_target_pairs={{0,48},{16,0},{32,16},{48,32},{1,49},{17,1},{33,17},{49,33},{2,50}... | collective-permute-start | bytes 1572872 | tf_op jit(solution)/shard_map/ppermute | solution.py:163
  85.2 13.7 %copy-start.19 = (s32[384]{0:T(512)S(1)}, s32[384]{0:T(512)}, u32[]{:S(2)}) copy-start(s32[384]{0:T(512)} %param.15) | copy-start | bytes 4612
  98.1 7.8 %collective-permute-start.12 = (f32[384,2048]{1,0:T(8,128)}, f32[384,2048]{1,0:T(8,128)}, u32[]{:S(2)}, u32[]{:S(2)}) collective-permute-start(f32[384,2048]{1,0:T(8,128)} %get-tuple-element.34), channel_id=1, source_target_pairs={{0,1},{1,0},{2,3},{3,2},{4,5},{5,4},{6,7},{7,6},{8,9},{9,8},{10,11... | collective-permute-start | bytes 9437192 | tf_op jit(solution)/shard_map/ppermute | solution.py:177
  105.4 4.6 %collective-permute-start.13 = (bf16[384,1024]{1,0:T(8,128)(2,1)S(1)}, bf16[384,1024]{1,0:T(8,128)(2,1)S(1)}, u32[]{:S(2)}, u32[]{:S(2)}) collective-permute-start(bf16[384,1024]{1,0:T(8,128)(2,1)S(1)} %broadcast_select_fusion), channel_id=1, source_target_pairs={{0,1},{1,0},{2,3},{3,2},{4,5},{5,4},{6,7},{7,6},{8,9},{9,8},{10,11... | collective-permute-start | bytes 2359304 | tf_op jit(solution)/shard_map/ppermute | solution.py:171
  111.2 5.3 %copy-start.14 = (bf16[192,1024]{1,0:T(8,128)(2,1)S(1)}, bf16[192,1024]{1,0:T(8,128)(2,1)}, u32[]{:S(2)}) copy-start(bf16[192,1024]{1,0:T(8,128)(2,1)} %copy-done.13) | copy-start | bytes 1179652
  111.2 5.4 %copy-start.12 = (bf16[192,1024]{1,0:T(8,128)(2,1)S(1)}, bf16[192,1024]{1,0:T(8,128)(2,1)}, u32[]{:S(2)}) copy-start(bf16[192,1024]{1,0:T(8,128)(2,1)} %copy-done.11) | copy-start | bytes 1179652
  112.8 16.2 %copy-start.5 = (bf16[384,2048]{1,0:T(8,128)(2,1)}, bf16[384,2048]{1,0:T(8,128)(2,1)S(1)}, u32[]{:S(2)}) copy-start(bf16[384,2048]{1,0:T(8,128)(2,1)S(1)} %multiply_convert_fusion) | copy-start | bytes 4718596
  112.9 12.3 %collective-permute-start.14 = (bf16[192,512]{1,0:T(8,128)(2,1)S(1)}, bf16[192,512]{1,0:T(8,128)(2,1)S(1)}, u32[]{:S(2)}, u32[]{:S(2)}) collective-permute-start(bf16[192,512]{1,0:T(8,128)(2,1)S(1)} %get-tuple-element.51), channel_id=1, source_target_pairs={{0,192},{64,0},{128,64},{192,128},{1,193},{65,1},{129,65},{193,129... | collective-permute-start | bytes 589832 | tf_op jit(solution)/shard_map/ppermute | solution.py:194
  116.5 9.4 %collective-permute-start.15 = (bf16[192,512]{1,0:T(8,128)(2,1)S(1)}, bf16[192,512]{1,0:T(8,128)(2,1)S(1)}, u32[]{:S(2)}, u32[]{:S(2)}) collective-permute-start(bf16[192,512]{1,0:T(8,128)(2,1)S(1)} %get-tuple-element.50), channel_id=1, source_target_pairs={{0,128},{64,192},{128,0},{192,64},{1,129},{65,193},{129,1},{193,65... | collective-permute-start | bytes 589832 | tf_op jit(solution)/shard_map/ppermute | solution.py:195
  116.7 12.2 %collective-permute-start.16 = (bf16[192,512]{1,0:T(8,128)(2,1)S(1)}, bf16[192,512]{1,0:T(8,128)(2,1)S(1)}, u32[]{:S(2)}, u32[]{:S(2)}) collective-permute-start(bf16[192,512]{1,0:T(8,128)(2,1)S(1)} %get-tuple-element.49), channel_id=1, source_target_pairs={{0,64},{64,128},{128,192},{192,0},{1,65},{65,129},{129,193},{193,1... | collective-permute-start | bytes 589832 | tf_op jit(solution)/shard_map/ppermute | solution.py:196
  128.9 2.1 %collective-permute-start.17 = (bf16[576,512]{1,0:T(8,128)(2,1)S(1)}, bf16[576,512]{1,0:T(8,128)(2,1)S(1)}, u32[]{:S(2)}, u32[]{:S(2)}) collective-permute-start(bf16[576,512]{1,0:T(8,128)(2,1)S(1)} %constant_dynamic-update-slice_fusion.5), channel_id=1, source_target_pairs={{0,1},{1,0},{2,3},{3,2},{4,5},{5,4},{6,7},{7,6},{8,9},{9,8},{10,11... | collective-permute-start | bytes 1769480 | tf_op jit(solution)/shard_map/ppermute | solution.py:198
  134.1 26.7 %copy-start.6 = (bf16[384,2048]{1,0:T(8,128)(2,1)S(1)}, bf16[384,2048]{1,0:T(8,128)(2,1)}, u32[]{:S(2)}) copy-start(bf16[384,2048]{1,0:T(8,128)(2,1)} %copy-done.5) | copy-start | bytes 4718596
  134.1 6.0 %collective-permute-start.18 = (bf16[64,1024]{1,0:T(8,128)(2,1)}, bf16[64,1024]{1,0:T(8,128)(2,1)S(1)}, u32[]{:S(2)}, u32[]{:S(2)}) collective-permute-start(bf16[64,1024]{1,0:T(8,128)(2,1)} %get-tuple-element.58), channel_id=1, source_target_pairs={{0,16},{16,32},{32,48},{48,0},{1,17},{17,33},{33,49},{49,1},{2,18}... | collective-permute-start | bytes 393224 | tf_op jit(solution)/shard_map/ppermute | solution.py:53
  134.1 7.0 %collective-permute-start.20 = (bf16[64,1024]{1,0:T(8,128)(2,1)S(1)}, bf16[64,1024]{1,0:T(8,128)(2,1)S(1)}, u32[]{:S(2)}, u32[]{:S(2)}) collective-permute-start(bf16[64,1024]{1,0:T(8,128)(2,1)S(1)} %get-tuple-element.59), channel_id=1, source_target_pairs={{0,48},{16,0},{32,16},{48,32},{1,49},{17,1},{33,17},{49,33},{2,50}... | collective-permute-start | bytes 393224 | tf_op jit(solution)/shard_map/ppermute | solution.py:54
  142.9 8.0 %collective-permute-start.19 = (bf16[128,1024]{1,0:T(8,128)(2,1)}, bf16[128,1024]{1,0:T(8,128)(2,1)S(1)}, u32[]{:S(2)}, u32[]{:S(2)}) collective-permute-start(bf16[128,1024]{1,0:T(8,128)(2,1)} %pad_maximum_fusion), channel_id=1, source_target_pairs={{0,16},{16,32},{32,48},{48,0},{1,17},{17,33},{33,49},{49,1},{2,18}... | collective-permute-start | bytes 786440 | tf_op jit(solution)/shard_map/ppermute | solution.py:58
  144.1 9.2 %collective-permute-start.21 = (bf16[128,1024]{1,0:T(8,128)(2,1)}, bf16[128,1024]{1,0:T(8,128)(2,1)}, u32[]{:S(2)}, u32[]{:S(2)}) collective-permute-start(bf16[128,1024]{1,0:T(8,128)(2,1)} %pad_maximum_fusion.1), channel_id=1, source_target_pairs={{0,48},{16,0},{32,16},{48,32},{1,49},{17,1},{33,17},{49,33},{2,50}... | collective-permute-start | bytes 786440 | tf_op jit(solution)/shard_map/ppermute | solution.py:59
  155.3 16.2 %all-to-all-start.2 = ((bf16[8,16,1024]{2,1,0:T(8,128)(2,1)}), bf16[8,16,1024]{2,1,0:T(8,128)(2,1)S(1)}, u32[]{:S(2)}, u32[]{:S(2)}) async-start(bf16[8,16,1024]{2,1,0:T(8,128)(2,1)} %bitcast.5), calls=%async_computation.2 | async-start | bytes 524288 | tf_op jit(solution)/shard_map/all_to_all | solution.py:131
  (12 other events, 23.4 us)

commit v7 on v6

--- a/solution.py
+++ b/solution.py
@@ -12,17 +12,60 @@
 ACROSS = [(i, (i + 2) % 4) for i in range(4)]
 
 
-def norm_back(projected, residual, bias_out, norm_gain, grad_out):
-    summed_in = residual.astype(F32) + projected + bias_out
+def norm_kernel(own_ref, other_ref, residual_ref, bias_ref, gain_ref, low_ref, high_ref, out_ref):
+    summed_in = residual_ref[...].astype(F32) + (own_ref[...] + other_ref[...]) + bias_ref[...]
     mean_in = jnp.mean(summed_in, axis=-1, keepdims=True)
     centred = summed_in - mean_in
     variance = jnp.mean(centred * centred, axis=-1, keepdims=True)
     inv_std = lax.rsqrt(variance + 1e-05)
     normed = centred * inv_std
-    grad_norm = grad_out.astype(F32) * norm_gain
+    grad_out = jnp.concatenate([low_ref[...], high_ref[...]], axis=1)
+    grad_norm = grad_out.astype(F32) * gain_ref[...]
     first_mean = jnp.mean(grad_norm, axis=-1, keepdims=True)
     second_mean = jnp.mean(grad_norm * normed, axis=-1, keepdims=True)
-    return (inv_std * (grad_norm - first_mean - normed * second_mean)).astype(BF16)
+    out_ref[...] = (inv_std * (grad_norm - first_mean - normed * second_mean)).astype(BF16)
+
+
+def norm_back(own, other, residual, bias_out, norm_gain, low, high):
+    rows, features = residual.shape
+    step = 64
+    wide = pl.BlockSpec((step, features), lambda i: (i, 0))
+    narrow = pl.BlockSpec((step, features // 2), lambda i: (i, 0))
+    single = pl.BlockSpec((1, features), lambda i: (0, 0))
+    return pl.pallas_call(
+        norm_kernel,
+        grid=(rows // step,),
+        out_shape=jax.ShapeDtypeStruct((rows, features), BF16),
+        in_specs=[wide, wide, wide, single, single, narrow, narrow],
+        out_specs=wide,
+        compiler_params=pltpu.CompilerParams(vmem_limit_bytes=24 << 20),
+        cost_estimate=pl.CostEstimate(
+            flops=20 * rows * features, bytes_accessed=14 * rows * features, transcendentals=rows
+        ),
+        name="norm_back",
+    )(own, other, residual, bias_out[None], norm_gain[None], low, high)
+
+
+def order_kernel(*refs):
+    iz = lax.axis_index("z")
+    out_ref = refs[-1]
+    for step, ref in enumerate(refs[:-1]):
+        out_ref[lax.rem(iz + step, 8)] = ref[...]
+
+
+def gather_z(piece):
+    pieces = [piece] + [
+        lax.ppermute(piece, "z", [(i, (i - step) % 8) for i in range(8)]) for step in range(1, 8)
+    ]
+    vmem = pl.BlockSpec(memory_space=pltpu.VMEM)
+    return pl.pallas_call(
+        order_kernel,
+        out_shape=jax.ShapeDtypeStruct((8,) + piece.shape, piece.dtype),
+        in_specs=[vmem] * 8,
+        out_specs=vmem,
+        cost_estimate=pl.CostEstimate(flops=0, bytes_accessed=1 << 19, transcendentals=0),
+        name="order_z",
+    )(*pieces)
 
 
 def ring_gather(piece, axis):
@@ -119,12 +162,6 @@
     )(context, *pieces)
 
 
-def spread(piece, axis):
-    ways = lax.axis_size(axis)
-    whole = jnp.broadcast_to(piece[None], (ways,) + piece.shape)
-    return lax.all_to_all(whole, axis, split_axis=0, concat_axis=0)
-
-
 def collect(total, axis):
     ways = lax.axis_size(axis)
     share = total.astype(BF16).reshape(ways, -1, total.shape[1])
@@ -145,7 +182,7 @@
     weight_t = out_weight.T
     mine, weight_t = lax.optimization_barrier((mine, weight_t))
     returned = lax.all_to_all(mine, ("x", "y", "z"), split_axis=0, concat_axis=0, tiled=True)
-    block = spread(weight_t, "z").reshape(128, 1024)
+    block = gather_z(weight_t).reshape(128, 1024)
     context_before = lax.ppermute(context, "x", RIGHT)
     context_after = lax.ppermute(context, "x", LEFT)
     block, context_before, context_after = lax.optimization_barrier(
@@ -169,13 +206,10 @@
     picked = returned.at[slot_codes].get(mode="promise_in_bounds")
     picked = jnp.where(live_mask[:, None], picked, jnp.zeros((), picked.dtype))
     other = lax.ppermute(picked, "core", swap)
-    grad_out = jnp.where(
-        core == 0,
-        jnp.concatenate([picked, other], axis=1),
-        jnp.concatenate([other, picked], axis=1),
-    )
-    projected = partial_proj + lax.ppermute(partial_proj, "core", swap)
-    grad_resid = norm_back(projected, residual, bias_out, norm_gain, grad_out)
+    low = jnp.where(core == 0, picked, other)
+    high = jnp.where(core == 0, other, picked)
+    theirs = lax.ppermute(partial_proj, "core", swap)
+    grad_resid = norm_back(partial_proj, theirs, residual, bias_out, norm_gain, low, high)
 
     def columns_of(step):
         at = lax.rem(ix + step, 4)

time: 173 us -> 179 us (1.035)
  blocking collectives: 19.6 us -> 0 us
  starting transfers between devices: 46.3 us -> 62.8 us
  Pallas kernels: 5.91 us -> 14.1 us
  other arithmetic: 13.2 us -> 7.41 us
  waiting for transfers between devices: 53.6 us -> 57.3 us
  local copies, waits for them, and re-layouts: 24.2 us -> 26.1 us
    all_to_all x1 -> x0, blocking collectives: 19.6 us -> none  [spread(): return lax.all_to_all(whole, axis, split_axis=0, concat_axis=0)]
    ppermute x1 -> x8, starting transfers between devices: 0.01 us -> 16.2 us  [the longest x7 16.2 us: gather_z(): lax.ppermute(piece, 'z', [(i, (i - step) % 8) for i in range(8)])]
    pallas_call x0 -> x2, Pallas kernels: none -> 8.18 us  [the longest x1 6.57 us: norm_back(): pl.pallas_call(norm_kernel, grid=(rows // step,), out_shape=jax.ShapeDtyp...]
    ppermute x1 -> x8, waiting for transfers between devices: 0.01 us -> 6.19 us  [the longest x7 6.18 us: gather_z(): lax.ppermute(piece, 'z', [(i, (i - step) % 8) for i in range(8)])]
    reduce_sum x3 -> x0, other arithmetic: 5.04 us -> none  [the longest x1 3.56 us: norm_back(): mean_in = jnp.mean(summed_in, axis=-1, keepdims=True)]
    ppermute x1, waiting for transfers between devices: 10.8 us -> 8.52 us  [shards(): context_top = lax.ppermute(context_before[:mid], 'x', RIGHT)]
    unnamed x47 -> x51, local copies, waits for them, and re-layouts: 7.39 us -> 8.55 us
  transfers between devices with their start and end apart: 24 -> 31, of which waited for: 15 -> 22; matrix products, arithmetic and copies ran while one was open for 15% -> 14% of each run, Pallas kernels for 0% -> 1%
where the time goes in v7:
time: 179 us; the launch traced here: 178 us
  starting transfers between devices  62.8 us (35%)
  waiting for transfers between devices  57.3 us (32%)
  local copies, waits for them, and re-layouts  26.1 us (15%)
  Pallas kernels  14.1 us (8%)
  matrix products  8.58 us (5%)
  other arithmetic  7.41 us (4%)
    ppermute x7, starting transfers between devices, gather_z(): lax.ppermute(piece, 'z', [(i, (i - step) % 8) for i in range(8)])  16.2 us
    all_to_all x1, starting transfers between devices, shards(): lax.all_to_all(mine, ('x', 'y', 'z'), split_axis=0, concat_axis=0, tiled=...  13.7 us
    unnamed x51, local copies, waits for them, and re-layouts  8.55 us
    ppermute x1, waiting for transfers between devices, shards(): context_top = lax.ppermute(context_before[:mid], 'x', RIGHT)  8.52 us
    ppermute x1, waiting for transfers between devices, shards(): lax.ppermute(half_of(3), 'x', LEFT)  7.51 us
    pallas_call x1, Pallas kernels, norm_back(): pl.pallas_call(norm_kernel, grid=(rows // step,), out_shape=jax.ShapeDtyp...  6.57 us
    ppermute x7, waiting for transfers between devices, gather_z(): lax.ppermute(piece, 'z', [(i, (i - step) % 8) for i in range(8)])  6.18 us
    pallas_call x1, Pallas kernels, project(): pl.pallas_call(project_kernel, out_shape=(jax.ShapeDtypeStruct((4, 4, 128...  5.92 us
  transfers between devices with their start and end apart: 31, of which 22 were waited for; matrix products, arithmetic and copies ran while one was open for 14% of the time, Pallas kernels for 1%

profile of v7, /device:TPU:24, one launch (start us, length us, event | category | flops | bytes accessed | tf_op | source)
XLA Modules:
  0.0 178.0 jit_solution(6787767057765969881)
XLA Ops:
  2.2 1.7 collective-permute-start.8
  4.0 5.9 %collective-permute-start = (bf16[16,1024]{1,0:T(8,128)(2,1)}, bf16[16,1024]{1,0:T(8,128)(2,1)S(1)}, u32[]{:S(2)}, u32[]{:S(2)}) collective-permute-start(bf16[16,1024]{1,0:T(8,128)(2,1)} %bitcast.22), channel_id=1, source_target_pairs={{0,14},{2,0},{4,2},{6,4},{8,6},{10,8},{12,10},{14,12},{1,15},{3,1}... | collective-permute-start | bytes 98312 | tf_op jit(solution)/shard_map/ppermute | solution.py:58
  12.4 4.5 %collective-permute-start.3 = (bf16[16,1024]{1,0:T(8,128)(2,1)}, bf16[16,1024]{1,0:T(8,128)(2,1)S(1)}, u32[]{:S(2)}, u32[]{:S(2)}) collective-permute-start(bf16[16,1024]{1,0:T(8,128)(2,1)} %bitcast.25), channel_id=1, source_target_pairs={{0,8},{2,10},{4,12},{6,14},{8,0},{10,2},{12,4},{14,6},{1,9},{3,11}... | collective-permute-start | bytes 98312 | tf_op jit(solution)/shard_map/ppermute | solution.py:58
  16.9 2.6 %collective-permute-start.4 = (bf16[16,1024]{1,0:T(8,128)(2,1)}, bf16[16,1024]{1,0:T(8,128)(2,1)S(1)}, u32[]{:S(2)}, u32[]{:S(2)}) collective-permute-start(bf16[16,1024]{1,0:T(8,128)(2,1)} %bitcast.26), channel_id=1, source_target_pairs={{0,6},{2,8},{4,10},{6,12},{8,14},{10,0},{12,2},{14,4},{1,7},{3,9},... | collective-permute-start | bytes 98312 | tf_op jit(solution)/shard_map/ppermute | solution.py:58
  21.5 3.2 %collective-permute-done.4.refs_5_ = bf16[16,1024]{1,0:T(8,128)(2,1)S(1)} collective-permute-done((bf16[16,1024]{1,0:T(8,128)(2,1)}, bf16[16,1024]{1,0:T(8,128)(2,1)S(1)}, u32[]{:S(2)}, u32[]{:S(2)}) %collective-permute-start.4) | collective-permute-done | bytes 32800 | tf_op jit(solution)/shard_map/ppermute | solution.py:58
  29.0 3.0 %collective-permute-start.9 = (bf16[128,1024]{1,0:T(8,128)(2,1)}, bf16[128,1024]{1,0:T(8,128)(2,1)S(1)}, u32[]{:S(2)}, u32[]{:S(2)}) collective-permute-start(bf16[128,1024]{1,0:T(8,128)(2,1)} %bitcast.20), channel_id=1, source_target_pairs={{0,192},{64,0},{128,64},{192,128},{1,193},{65,1},{129,65},{193,129... | collective-permute-start | bytes 786440 | tf_op jit(solution)/shard_map/ppermute | solution.py:74
  32.0 5.1 %collective-permute-done.10 = bf16[128,1024]{1,0:T(8,128)(2,1)S(1)} collective-permute-done((bf16[128,1024]{1,0:T(8,128)(2,1)}, bf16[128,1024]{1,0:T(8,128)(2,1)S(1)}, u32[]{:S(2)}, u32[]{:S(2)}) %collective-permute-start.10) | collective-permute-done | bytes 262176 | tf_op jit(solution)/shard_map/ppermute | solution.py:73
  38.9 3.3 %collective-permute-start.12 = (bf16[64,1024]{1,0:T(8,128)(2,1)S(1)}, bf16[64,1024]{1,0:T(8,128)(2,1)S(1)}, u32[]{:S(2)}, u32[]{:S(2)}) collective-permute-start(bf16[64,1024]{1,0:T(8,128)(2,1)S(1)} %slice.53), channel_id=1, source_target_pairs={{0,192},{64,0},{128,64},{192,128},{1,193},{65,1},{129,65},{193,129... | collective-permute-start | bytes 393224 | tf_op jit(solution)/shard_map/ppermute | solution.py:76
  46.1 2.0 %collective-permute-start.14 = (bf16[4,128,1024]{2,1,0:T(8,128)(2,1)}, bf16[4,128,1024]{2,1,0:T(8,128)(2,1)}, u32[]{:S(2)}, u32[]{:S(2)}) collective-permute-start(bf16[4,128,1024]{2,1,0:T(8,128)(2,1)} %bitcast.2.refs_1_), channel_id=1, source_target_pairs={{0,48},{16,0},{32,16},{48,32},{1,49},{17,1},{33,17},{49,33},{2,50}... | collective-permute-start | bytes 3145736 | tf_op jit(solution)/shard_map/ppermute | solution.py:197
  49.4 13.7 %all-to-all-start = ((bf16[128,3,1024]{2,1,0:T(4,128)(2,1)}), bf16[128,3,1024]{2,1,0:T(4,128)(2,1)}, u32[]{:S(2)}, u32[]{:S(2)}) async-start(bf16[128,3,1024]{2,1,0:T(4,128)(2,1)} %all_to_all.11), calls=%async_computation | async-start | bytes 2097152 | tf_op jit(solution)/shard_map/all_to_all | solution.py:184
  63.2 1.8 collective-permute-start.15
  66.0 1.7 collective-permute-start.16
  67.7 8.5 %collective-permute-done.15 = bf16[192,1024]{1,0:T(8,128)(2,1)S(1)} collective-permute-done((bf16[192,1024]{1,0:T(8,128)(2,1)S(1)}, bf16[192,1024]{1,0:T(8,128)(2,1)S(1)}, u32[]{:S(2)}, u32[]{:S(2)}) %collective-permute-start.15) | collective-permute-done | bytes 393248 | tf_op jit(solution)/shard_map/ppermute | solution.py:192
  79.1 1.9 %slice.43 = bf16[2,128,1024]{2,1,0:T(8,128)(2,1)} slice(bf16[4,128,1024]{2,1,0:T(8,128)(2,1)} %collective-permute-done.14.refs_2_), slice={[2:4], [0:128], [0:1024]} | slice | bytes 1048576 | tf_op jit(solution)/shard_map/slice | solution.py:200
  81.0 1.9 %collective-permute-start.18 = (bf16[2,128,1024]{2,1,0:T(8,128)(2,1)}, bf16[2,128,1024]{2,1,0:T(8,128)(2,1)}, u32[]{:S(2)}, u32[]{:S(2)}) collective-permute-start(bf16[2,128,1024]{2,1,0:T(8,128)(2,1)} %slice.43), channel_id=1, source_target_pairs={{0,48},{16,0},{32,16},{48,32},{1,49},{17,1},{33,17},{49,33},{2,50}... | collective-permute-start | bytes 1572872 | tf_op jit(solution)/shard_map/ppermute | solution.py:200
  84.0 3.2 %all_to_all.13 = bf16[384,1024]{1,0:T(8,128)(2,1)} reshape(bf16[128,3,1024]{2,1,0:T(4,128)(2,1)} %all-to-all-done) | data formatting | bytes 1572864 | tf_op jit(solution)/shard_map/all_to_all | solution.py:184
  88.7 3.0 %collective-permute-done.18.refs_4_ = bf16[2,128,1024]{2,1,0:T(8,128)(2,1)} collective-permute-done((bf16[2,128,1024]{2,1,0:T(8,128)(2,1)}, bf16[2,128,1024]{2,1,0:T(8,128)(2,1)}, u32[]{:S(2)}, u32[]{:S(2)}) %collective-permute-start.18) | collective-permute-done | bytes 524320 | tf_op jit(solution)/shard_map/ppermute | solution.py:200
  91.7 5.9 %project.1 = (bf16[4,4,128,1024]{3,2,1,0:T(8,128)(2,1)S(1)}, f32[384,2048]{1,0:T(8,128)}) custom-call(bf16[384,1024]{1,0:T(8,128)(2,1)S(1)} %copy-done.2, bf16[4,128,1024]{2,1,0:T(8,128)(2,1)} %bitcast.2.refs_1_, bf16[4,128,1024]{2,1,0:T(8,128)(2,1)} %collective-permute-done.14.refs_2_, bf16[2,128,1024]{2,1,0:T(8,128)(2,1)} %collective-permute-done.17.refs_3_, ...), custom_call_target="tpu_custom_call" | custom-call | flops 1610612736 | bytes 16777216 | tf_op jit(solution)/shard_map/project/pallas_call | solution.py:145
  97.7 2.0 %copy-done.5 = bf16[4,4,128,1024]{3,2,1,0:T(8,128)(2,1)} copy-done((bf16[4,4,128,1024]{3,2,1,0:T(8,128)(2,1)}, bf16[4,4,128,1024]{3,2,1,0:T(8,128)(2,1)S(1)}, u32[]{:S(2)}) %copy-start.5) | copy-done | bytes 4194328
  100.3 4.0 %gather_fusion = bf16[384,1024]{1,0:T(8,128)(2,1)S(1)} fusion(bf16[384,1024]{1,0:T(8,128)(2,1)} %all_to_all.13, s32[1024]{0:T(1024)S(1)} %pad_clamp_fusion), kind=kCustom, calls=%fused_computation | custom fusion | bytes 1574400 | tf_op jit(solution)/shard_map/gather | solution.py:206
  109.5 6.6 %norm_back.1 = bf16[384,2048]{1,0:T(8,128)(2,1)} custom-call(f32[384,2048]{1,0:T(8,128)} %get-tuple-element.34.own_ref, f32[384,2048]{1,0:T(8,128)} %collective-permute-done.19.other_ref, bf16[384,2048]{1,0:T(8,128)(2,1)S(1)} %copy-done.1, f32[1,2048]{1,0:T(1,128)S(1)} %bitcast.16, f32[1,2048]{1,0:T(1,128)S(1)} %bitcast.17, ...), custom_call_target="tpu_custom_call" | custom-call | flops 15728640 | bytes 11010048 | tf_op jit(solution)/shard_map/norm_back/pallas_call | solution.py:35
  117.3 3.7 %collective-permute-start.21 = (bf16[192,512]{1,0:T(8,128)(2,1)S(1)}, bf16[192,512]{1,0:T(8,128)(2,1)S(1)}, u32[]{:S(2)}, u32[]{:S(2)}) collective-permute-start(bf16[192,512]{1,0:T(8,128)(2,1)S(1)} %get-tuple-element.47), channel_id=1, source_target_pairs={{0,192},{64,0},{128,64},{192,128},{1,193},{65,1},{129,65},{193,129... | collective-permute-start | bytes 589832 | tf_op jit(solution)/shard_map/ppermute | solution.py:228
  122.4 7.5 %collective-permute-done.21 = bf16[192,512]{1,0:T(8,128)(2,1)S(1)} collective-permute-done((bf16[192,512]{1,0:T(8,128)(2,1)S(1)}, bf16[192,512]{1,0:T(8,128)(2,1)S(1)}, u32[]{:S(2)}, u32[]{:S(2)}) %collective-permute-start.21) | collective-permute-done | bytes 196640 | tf_op jit(solution)/shard_map/ppermute | solution.py:228
  130.4 3.3 %collective-permute-done.23 = bf16[192,512]{1,0:T(8,128)(2,1)S(1)} collective-permute-done((bf16[192,512]{1,0:T(8,128)(2,1)S(1)}, bf16[192,512]{1,0:T(8,128)(2,1)S(1)}, u32[]{:S(2)}, u32[]{:S(2)}) %collective-permute-start.23) | collective-permute-done | bytes 196640 | tf_op jit(solution)/shard_map/ppermute | solution.py:230
  139.7 2.0 %collective-permute-start.27 = (bf16[64,1024]{1,0:T(8,128)(2,1)S(1)}, bf16[64,1024]{1,0:T(8,128)(2,1)S(1)}, u32[]{:S(2)}, u32[]{:S(2)}) collective-permute-start(bf16[64,1024]{1,0:T(8,128)(2,1)S(1)} %get-tuple-element.57), channel_id=1, source_target_pairs={{0,48},{16,0},{32,16},{48,32},{1,49},{17,1},{33,17},{49,33},{2,50}... | collective-permute-start | bytes 393224 | tf_op jit(solution)/shard_map/ppermute | solution.py:97
  142.8 3.0 %collective-permute-done.25 = bf16[64,1024]{1,0:T(8,128)(2,1)S(1)} collective-permute-done((bf16[64,1024]{1,0:T(8,128)(2,1)}, bf16[64,1024]{1,0:T(8,128)(2,1)S(1)}, u32[]{:S(2)}, u32[]{:S(2)}) %collective-permute-start.25) | collective-permute-done | bytes 131104 | tf_op jit(solution)/shard_map/ppermute | solution.py:96
  151.3 5.4 %collective-permute-done.26 = bf16[128,1024]{1,0:T(8,128)(2,1)S(1)} collective-permute-done((bf16[128,1024]{1,0:T(8,128)(2,1)}, bf16[128,1024]{1,0:T(8,128)(2,1)S(1)}, u32[]{:S(2)}, u32[]{:S(2)}) %collective-permute-start.26) | collective-permute-done | bytes 262176 | tf_op jit(solution)/shard_map/ppermute | solution.py:101
  156.7 2.5 %collective-permute-done.28 = bf16[128,1024]{1,0:T(8,128)(2,1)} collective-permute-done((bf16[128,1024]{1,0:T(8,128)(2,1)}, bf16[128,1024]{1,0:T(8,128)(2,1)}, u32[]{:S(2)}, u32[]{:S(2)}) %collective-permute-start.28) | collective-permute-done | bytes 262176 | tf_op jit(solution)/shard_map/ppermute | solution.py:102
  159.2 1.9 %add_convert_fusion = bf16[128,1024]{1,0:T(8,128)(2,1)} fusion(bf16[128,1024]{1,0:T(8,128)(2,1)} %collective-permute-done.28, bf16[128,1024]{1,0:T(8,128)(2,1)S(1)} %collective-permute-done.26, f32[512,1024]{1,0:T(8,128)} %copy-done.6, s32[]{:T(128)S(6)} %select_n.71), kind=kLoop, calls=%fused_computation.19 | loop fusion | flops 655360 | bytes 1310724 | tf_op jit(solution)/shard_map/convert_element_type | solution.py:167
  161.1 5.7 %all-to-all-start.1 = ((bf16[8,16,1024]{2,1,0:T(8,128)(2,1)}), bf16[8,16,1024]{2,1,0:T(8,128)(2,1)S(1)}, u32[]{:S(2)}, u32[]{:S(2)}) async-start(bf16[8,16,1024]{2,1,0:T(8,128)(2,1)} %bitcast.7), calls=%async_computation.1 | async-start | bytes 524288 | tf_op jit(solution)/shard_map/all_to_all | solution.py:168
  166.8 4.9 %convolution_convert_fusion = bf16[384,1024]{1,0:T(8,128)(2,1)} fusion(bf16[384,2048]{1,0:T(8,128)(2,1)S(1)} %copy-done.7, bf16[2048,1024]{1,0:T(8,128)(2,1)} %bitcast.18), kind=kOutput, calls=%fused_computation.2 | convolution fusion | flops 1611005952 | bytes 6553600 | tf_op jit(solution)/shard_map/dot_general | solution.py:251
  171.7 5.7 %all-to-all-done.1 = bf16[8,16,1024]{2,1,0:T(8,128)(2,1)S(1)} async-done(((bf16[8,16,1024]{2,1,0:T(8,128)(2,1)}), bf16[8,16,1024]{2,1,0:T(8,128)(2,1)S(1)}, u32[]{:S(2)}, u32[]{:S(2)}) %all-to-all-start.1) | async-done | bytes 262176 | tf_op jit(solution)/shard_map/all_to_all | solution.py:168
  (118 shorter events, 45.2 us)
Async XLA Ops:
  0.6 28.0 %collective-permute-start.7 = (bf16[384,1024]{1,0:T(8,128)(2,1)}, bf16[384,1024]{1,0:T(8,128)(2,1)S(1)}, u32[]{:S(2)}, u32[]{:S(2)}) collective-permute-start(bf16[384,1024]{1,0:T(8,128)(2,1)} %refs_0_.1), channel_id=1, source_target_pairs={{0,64},{64,128},{128,192},{192,0},{1,65},{65,129},{129,193},{193,1... | collective-permute-start | bytes 2359304 | tf_op jit(solution)/shard_map/ppermute | solution.py:186
  2.2 26.5 %collective-permute-start.8 = (bf16[384,1024]{1,0:T(8,128)(2,1)}, bf16[384,1024]{1,0:T(8,128)(2,1)}, u32[]{:S(2)}, u32[]{:S(2)}) collective-permute-start(bf16[384,1024]{1,0:T(8,128)(2,1)} %refs_0_.1), channel_id=1, source_target_pairs={{0,192},{64,0},{128,64},{192,128},{1,193},{65,1},{129,65},{193,129... | collective-permute-start | bytes 2359304 | tf_op jit(solution)/shard_map/ppermute | solution.py:187
  4.0 8.3 %collective-permute-start = (bf16[16,1024]{1,0:T(8,128)(2,1)}, bf16[16,1024]{1,0:T(8,128)(2,1)S(1)}, u32[]{:S(2)}, u32[]{:S(2)}) collective-permute-start(bf16[16,1024]{1,0:T(8,128)(2,1)} %bitcast.22), channel_id=1, source_target_pairs={{0,14},{2,0},{4,2},{6,4},{8,6},{10,8},{12,10},{14,12},{1,15},{3,1}... | collective-permute-start | bytes 98312 | tf_op jit(solution)/shard_map/ppermute | solution.py:58
  10.0 7.0 %collective-permute-start.1 = (bf16[16,1024]{1,0:T(8,128)(2,1)}, bf16[16,1024]{1,0:T(8,128)(2,1)S(1)}, u32[]{:S(2)}, u32[]{:S(2)}) collective-permute-start(bf16[16,1024]{1,0:T(8,128)(2,1)} %bitcast.23), channel_id=1, source_target_pairs={{0,12},{2,14},{4,0},{6,2},{8,4},{10,6},{12,8},{14,10},{1,13},{3,15... | collective-permute-start | bytes 98312 | tf_op jit(solution)/shard_map/ppermute | solution.py:58
  11.4 8.1 %collective-permute-start.2 = (bf16[16,1024]{1,0:T(8,128)(2,1)}, bf16[16,1024]{1,0:T(8,128)(2,1)S(1)}, u32[]{:S(2)}, u32[]{:S(2)}) collective-permute-start(bf16[16,1024]{1,0:T(8,128)(2,1)} %bitcast.24), channel_id=1, source_target_pairs={{0,10},{2,12},{4,14},{6,0},{8,2},{10,4},{12,6},{14,8},{1,11},{3,13... | collective-permute-start | bytes 98312 | tf_op jit(solution)/shard_map/ppermute | solution.py:58
  12.4 8.4 %collective-permute-start.3 = (bf16[16,1024]{1,0:T(8,128)(2,1)}, bf16[16,1024]{1,0:T(8,128)(2,1)S(1)}, u32[]{:S(2)}, u32[]{:S(2)}) collective-permute-start(bf16[16,1024]{1,0:T(8,128)(2,1)} %bitcast.25), channel_id=1, source_target_pairs={{0,8},{2,10},{4,12},{6,14},{8,0},{10,2},{12,4},{14,6},{1,9},{3,11}... | collective-permute-start | bytes 98312 | tf_op jit(solution)/shard_map/ppermute | solution.py:58
  16.9 7.8 %collective-permute-start.4 = (bf16[16,1024]{1,0:T(8,128)(2,1)}, bf16[16,1024]{1,0:T(8,128)(2,1)S(1)}, u32[]{:S(2)}, u32[]{:S(2)}) collective-permute-start(bf16[16,1024]{1,0:T(8,128)(2,1)} %bitcast.26), channel_id=1, source_target_pairs={{0,6},{2,8},{4,10},{6,12},{8,14},{10,0},{12,2},{14,4},{1,7},{3,9},... | collective-permute-start | bytes 98312 | tf_op jit(solution)/shard_map/ppermute | solution.py:58
  19.6 6.2 %collective-permute-start.5 = (bf16[16,1024]{1,0:T(8,128)(2,1)}, bf16[16,1024]{1,0:T(8,128)(2,1)S(1)}, u32[]{:S(2)}, u32[]{:S(2)}) collective-permute-start(bf16[16,1024]{1,0:T(8,128)(2,1)} %bitcast.27), channel_id=1, source_target_pairs={{0,4},{2,6},{4,8},{6,10},{8,12},{10,14},{12,0},{14,2},{1,5},{3,7},... | collective-permute-start | bytes 98312 | tf_op jit(solution)/shard_map/ppermute | solution.py:58
  20.8 5.7 %collective-permute-start.6 = (bf16[16,1024]{1,0:T(8,128)(2,1)}, bf16[16,1024]{1,0:T(8,128)(2,1)S(1)}, u32[]{:S(2)}, u32[]{:S(2)}) collective-permute-start(bf16[16,1024]{1,0:T(8,128)(2,1)} %bitcast.28), channel_id=1, source_target_pairs={{0,2},{2,4},{4,6},{6,8},{8,10},{10,12},{12,14},{14,0},{1,3},{3,5},... | collective-permute-start | bytes 98312 | tf_op jit(solution)/shard_map/ppermute | solution.py:58
  28.7 8.4 %collective-permute-start.10 = (bf16[128,1024]{1,0:T(8,128)(2,1)}, bf16[128,1024]{1,0:T(8,128)(2,1)S(1)}, u32[]{:S(2)}, u32[]{:S(2)}) collective-permute-start(bf16[128,1024]{1,0:T(8,128)(2,1)} %bitcast.19), channel_id=1, source_target_pairs={{0,64},{64,128},{128,192},{192,0},{1,65},{65,129},{129,193},{193,1... | collective-permute-start | bytes 786440 | tf_op jit(solution)/shard_map/ppermute | solution.py:73
  29.0 9.9 %collective-permute-start.9 = (bf16[128,1024]{1,0:T(8,128)(2,1)}, bf16[128,1024]{1,0:T(8,128)(2,1)S(1)}, u32[]{:S(2)}, u32[]{:S(2)}) collective-permute-start(bf16[128,1024]{1,0:T(8,128)(2,1)} %bitcast.20), channel_id=1, source_target_pairs={{0,192},{64,0},{128,64},{192,128},{1,193},{65,1},{129,65},{193,129... | collective-permute-start | bytes 786440 | tf_op jit(solution)/shard_map/ppermute | solution.py:74
  37.1 6.3 %collective-permute-start.11 = (bf16[64,1024]{1,0:T(8,128)(2,1)S(1)}, bf16[64,1024]{1,0:T(8,128)(2,1)S(1)}, u32[]{:S(2)}, u32[]{:S(2)}) collective-permute-start(bf16[64,1024]{1,0:T(8,128)(2,1)S(1)} %slice.52), channel_id=1, source_target_pairs={{0,64},{64,128},{128,192},{192,0},{1,65},{65,129},{129,193},{193,1... | collective-permute-start | bytes 393224 | tf_op jit(solution)/shard_map/ppermute | solution.py:75
  38.9 5.8 %collective-permute-start.12 = (bf16[64,1024]{1,0:T(8,128)(2,1)S(1)}, bf16[64,1024]{1,0:T(8,128)(2,1)S(1)}, u32[]{:S(2)}, u32[]{:S(2)}) collective-permute-start(bf16[64,1024]{1,0:T(8,128)(2,1)S(1)} %slice.53), channel_id=1, source_target_pairs={{0,192},{64,0},{128,64},{192,128},{1,193},{65,1},{129,65},{193,129... | collective-permute-start | bytes 393224 | tf_op jit(solution)/shard_map/ppermute | solution.py:76
  46.1 31.3 %collective-permute-start.13 = (bf16[4,128,1024]{2,1,0:T(8,128)(2,1)}, bf16[4,128,1024]{2,1,0:T(8,128)(2,1)S(1)}, u32[]{:S(2)}, u32[]{:S(2)}) collective-permute-start(bf16[4,128,1024]{2,1,0:T(8,128)(2,1)} %bitcast.2.refs_1_), channel_id=1, source_target_pairs={{0,16},{16,32},{32,48},{48,0},{1,17},{17,33},{33,49},{49,1},{2,18}... | collective-permute-start | bytes 3145736 | tf_op jit(solution)/shard_map/ppermute | solution.py:196
  46.1 32.1 %collective-permute-start.14 = (bf16[4,128,1024]{2,1,0:T(8,128)(2,1)}, bf16[4,128,1024]{2,1,0:T(8,128)(2,1)}, u32[]{:S(2)}, u32[]{:S(2)}) collective-permute-start(bf16[4,128,1024]{2,1,0:T(8,128)(2,1)} %bitcast.2.refs_1_), channel_id=1, source_target_pairs={{0,48},{16,0},{32,16},{48,32},{1,49},{17,1},{33,17},{49,33},{2,50}... | collective-permute-start | bytes 3145736 | tf_op jit(solution)/shard_map/ppermute | solution.py:197
  49.4 34.6 %all-to-all-start = ((bf16[128,3,1024]{2,1,0:T(4,128)(2,1)}), bf16[128,3,1024]{2,1,0:T(4,128)(2,1)}, u32[]{:S(2)}, u32[]{:S(2)}) async-start(bf16[128,3,1024]{2,1,0:T(4,128)(2,1)} %all_to_all.11), calls=%async_computation | async-start | bytes 2097152 | tf_op jit(solution)/shard_map/all_to_all | solution.py:184
  63.2 13.1 %collective-permute-start.15 = (bf16[192,1024]{1,0:T(8,128)(2,1)S(1)}, bf16[192,1024]{1,0:T(8,128)(2,1)S(1)}, u32[]{:S(2)}, u32[]{:S(2)}) collective-permute-start(bf16[192,1024]{1,0:T(8,128)(2,1)S(1)} %slice.40), channel_id=1, source_target_pairs={{0,64},{64,128},{128,192},{192,0},{1,65},{65,129},{129,193},{193,1... | collective-permute-start | bytes 1179656 | tf_op jit(solution)/shard_map/ppermute | solution.py:192
  66.0 25.8 %copy-start.2 = (bf16[384,1024]{1,0:T(8,128)(2,1)S(1)}, bf16[384,1024]{1,0:T(8,128)(2,1)}, u32[]{:S(2)}) copy-start(bf16[384,1024]{1,0:T(8,128)(2,1)} %refs_0_.1) | copy-start | bytes 2359300
  66.0 11.5 %collective-permute-start.16 = (bf16[192,1024]{1,0:T(8,128)(2,1)S(1)}, bf16[192,1024]{1,0:T(8,128)(2,1)S(1)}, u32[]{:S(2)}, u32[]{:S(2)}) collective-permute-start(bf16[192,1024]{1,0:T(8,128)(2,1)S(1)} %slice.41), channel_id=1, source_target_pairs={{0,192},{64,0},{128,64},{192,128},{1,193},{65,1},{129,65},{193,129... | collective-permute-start | bytes 1179656 | tf_op jit(solution)/shard_map/ppermute | solution.py:193
  79.0 9.7 %collective-permute-start.17 = (bf16[2,128,1024]{2,1,0:T(8,128)(2,1)}, bf16[2,128,1024]{2,1,0:T(8,128)(2,1)}, u32[]{:S(2)}, u32[]{:S(2)}) collective-permute-start(bf16[2,128,1024]{2,1,0:T(8,128)(2,1)} %slice.42), channel_id=1, source_target_pairs={{0,16},{16,32},{32,48},{48,0},{1,17},{17,33},{33,49},{49,1},{2,18}... | collective-permute-start | bytes 1572872 | tf_op jit(solution)/shard_map/ppermute | solution.py:199
  81.0 10.7 %collective-permute-start.18 = (bf16[2,128,1024]{2,1,0:T(8,128)(2,1)}, bf16[2,128,1024]{2,1,0:T(8,128)(2,1)}, u32[]{:S(2)}, u32[]{:S(2)}) collective-permute-start(bf16[2,128,1024]{2,1,0:T(8,128)(2,1)} %slice.43), channel_id=1, source_target_pairs={{0,48},{16,0},{32,16},{48,32},{1,49},{17,1},{33,17},{49,33},{2,50}... | collective-permute-start | bytes 1572872 | tf_op jit(solution)/shard_map/ppermute | solution.py:200
  99.6 9.8 %collective-permute-start.19 = (f32[384,2048]{1,0:T(8,128)}, f32[384,2048]{1,0:T(8,128)}, u32[]{:S(2)}, u32[]{:S(2)}) collective-permute-start(f32[384,2048]{1,0:T(8,128)} %get-tuple-element.34.own_ref), channel_id=1, source_target_pairs={{0,1},{1,0},{2,3},{3,2},{4,5},{5,4},{6,7},{7,6},{8,9},{9,8},{10,11... | collective-permute-start | bytes 9437192 | tf_op jit(solution)/shard_map/ppermute | solution.py:211
  105.4 2.8 %collective-permute-start.20 = (bf16[384,1024]{1,0:T(8,128)(2,1)}, bf16[384,1024]{1,0:T(8,128)(2,1)}, u32[]{:S(2)}, u32[]{:S(2)}) collective-permute-start(bf16[384,1024]{1,0:T(8,128)(2,1)} %broadcast_select_fusion), channel_id=1, source_target_pairs={{0,1},{1,0},{2,3},{3,2},{4,5},{5,4},{6,7},{7,6},{8,9},{9,8},{10,11... | collective-permute-start | bytes 2359304 | tf_op jit(solution)/shard_map/ppermute | solution.py:208
  117.3 12.6 %collective-permute-start.21 = (bf16[192,512]{1,0:T(8,128)(2,1)S(1)}, bf16[192,512]{1,0:T(8,128)(2,1)S(1)}, u32[]{:S(2)}, u32[]{:S(2)}) collective-permute-start(bf16[192,512]{1,0:T(8,128)(2,1)S(1)} %get-tuple-element.47), channel_id=1, source_target_pairs={{0,192},{64,0},{128,64},{192,128},{1,193},{65,1},{129,65},{193,129... | collective-permute-start | bytes 589832 | tf_op jit(solution)/shard_map/ppermute | solution.py:228
  121.0 9.4 %collective-permute-start.22 = (bf16[192,512]{1,0:T(8,128)(2,1)S(1)}, bf16[192,512]{1,0:T(8,128)(2,1)S(1)}, u32[]{:S(2)}, u32[]{:S(2)}) collective-permute-start(bf16[192,512]{1,0:T(8,128)(2,1)S(1)} %get-tuple-element.46), channel_id=1, source_target_pairs={{0,128},{64,192},{128,0},{192,64},{1,129},{65,193},{129,1},{193,65... | collective-permute-start | bytes 589832 | tf_op jit(solution)/shard_map/ppermute | solution.py:229
  121.3 12.4 %collective-permute-start.23 = (bf16[192,512]{1,0:T(8,128)(2,1)S(1)}, bf16[192,512]{1,0:T(8,128)(2,1)S(1)}, u32[]{:S(2)}, u32[]{:S(2)}) collective-permute-start(bf16[192,512]{1,0:T(8,128)(2,1)S(1)} %get-tuple-element.45), channel_id=1, source_target_pairs={{0,64},{64,128},{128,192},{192,0},{1,65},{65,129},{129,193},{193,1... | collective-permute-start | bytes 589832 | tf_op jit(solution)/shard_map/ppermute | solution.py:230
  133.7 2.9 %collective-permute-start.24 = (bf16[576,512]{1,0:T(8,128)(2,1)S(1)}, bf16[576,512]{1,0:T(8,128)(2,1)S(1)}, u32[]{:S(2)}, u32[]{:S(2)}) collective-permute-start(bf16[576,512]{1,0:T(8,128)(2,1)S(1)} %constant_dynamic-update-slice_fusion.5), channel_id=1, source_target_pairs={{0,1},{1,0},{2,3},{3,2},{4,5},{5,4},{6,7},{7,6},{8,9},{9,8},{10,11... | collective-permute-start | bytes 1769480 | tf_op jit(solution)/shard_map/ppermute | solution.py:232
  139.7 6.1 %collective-permute-start.25 = (bf16[64,1024]{1,0:T(8,128)(2,1)}, bf16[64,1024]{1,0:T(8,128)(2,1)S(1)}, u32[]{:S(2)}, u32[]{:S(2)}) collective-permute-start(bf16[64,1024]{1,0:T(8,128)(2,1)} %get-tuple-element.56), channel_id=1, source_target_pairs={{0,16},{16,32},{32,48},{48,0},{1,17},{17,33},{33,49},{49,1},{2,18}... | collective-permute-start | bytes 393224 | tf_op jit(solution)/shard_map/ppermute | solution.py:96
  139.7 7.1 %collective-permute-start.27 = (bf16[64,1024]{1,0:T(8,128)(2,1)S(1)}, bf16[64,1024]{1,0:T(8,128)(2,1)S(1)}, u32[]{:S(2)}, u32[]{:S(2)}) collective-permute-start(bf16[64,1024]{1,0:T(8,128)(2,1)S(1)} %get-tuple-element.57), channel_id=1, source_target_pairs={{0,48},{16,0},{32,16},{48,32},{1,49},{17,1},{33,17},{49,33},{2,50}... | collective-permute-start | bytes 393224 | tf_op jit(solution)/shard_map/ppermute | solution.py:97
  148.6 8.1 %collective-permute-start.26 = (bf16[128,1024]{1,0:T(8,128)(2,1)}, bf16[128,1024]{1,0:T(8,128)(2,1)S(1)}, u32[]{:S(2)}, u32[]{:S(2)}) collective-permute-start(bf16[128,1024]{1,0:T(8,128)(2,1)} %pad_maximum_fusion), channel_id=1, source_target_pairs={{0,16},{16,32},{32,48},{48,0},{1,17},{17,33},{33,49},{49,1},{2,18}... | collective-permute-start | bytes 786440 | tf_op jit(solution)/shard_map/ppermute | solution.py:101
  149.8 9.4 %collective-permute-start.28 = (bf16[128,1024]{1,0:T(8,128)(2,1)}, bf16[128,1024]{1,0:T(8,128)(2,1)}, u32[]{:S(2)}, u32[]{:S(2)}) collective-permute-start(bf16[128,1024]{1,0:T(8,128)(2,1)} %pad_maximum_fusion.1), channel_id=1, source_target_pairs={{0,48},{16,0},{32,16},{48,32},{1,49},{17,1},{33,17},{49,33},{2,50}... | collective-permute-start | bytes 786440 | tf_op jit(solution)/shard_map/ppermute | solution.py:102
  161.1 16.3 %all-to-all-start.1 = ((bf16[8,16,1024]{2,1,0:T(8,128)(2,1)}), bf16[8,16,1024]{2,1,0:T(8,128)(2,1)S(1)}, u32[]{:S(2)}, u32[]{:S(2)}) async-start(bf16[8,16,1024]{2,1,0:T(8,128)(2,1)} %bitcast.7), calls=%async_computation.1 | async-start | bytes 524288 | tf_op jit(solution)/shard_map/all_to_all | solution.py:168
  (21 other events, 139.8 us)

commit v8 on v6

--- a/solution.py
+++ b/solution.py
@@ -146,23 +146,21 @@
     mine, weight_t = lax.optimization_barrier((mine, weight_t))
     returned = lax.all_to_all(mine, ("x", "y", "z"), split_axis=0, concat_axis=0, tiled=True)
     block = spread(weight_t, "z").reshape(128, 1024)
-    context_before = lax.ppermute(context, "x", RIGHT)
-    context_after = lax.ppermute(context, "x", LEFT)
-    block, context_before, context_after = lax.optimization_barrier(
-        (block, context_before, context_after)
-    )
-    mid = capacity // 2
-    context_top = lax.ppermute(context_before[:mid], "x", RIGHT)
-    context_bottom = lax.ppermute(context_after[mid:], "x", LEFT)
-    context_pieces = (context, context_after, context_top, context_bottom, context_before)
     block = jnp.concatenate(ring_gather(block, "x")).reshape(4, 128, 1024)
+    block, held = lax.optimization_barrier((block, context))
+    context_before = lax.ppermute(held, "x", RIGHT)
+    context_after = lax.ppermute(held, "x", LEFT)
     before = lax.ppermute(block, "y", RIGHT)
     after = lax.ppermute(block, "y", LEFT)
-    before, after, context_pieces = lax.optimization_barrier((before, after, context_pieces))
+    mid = capacity // 2
     top = lax.ppermute(before[:2], "y", RIGHT)
     bottom = lax.ppermute(after[2:], "y", LEFT)
     pieces = (block, after, top, bottom, before)
-    pieces, returned = lax.optimization_barrier((pieces, returned))
+    pieces, returned, context_before, context_after = lax.optimization_barrier(
+        (pieces, returned, context_before, context_after)
+    )
+    context_top = lax.ppermute(context_before[:mid], "x", RIGHT)
+    context_bottom = lax.ppermute(context_after[mid:], "x", LEFT)
 
     weight_t, partial_proj = project(context, pieces)
     weight_t = weight_t.reshape(2048, 1024)
@@ -174,7 +172,10 @@
         jnp.concatenate([picked, other], axis=1),
         jnp.concatenate([other, picked], axis=1),
     )
-    projected = partial_proj + lax.ppermute(partial_proj, "core", swap)
+    theirs = lax.ppermute(partial_proj, "core", swap)
+    context_pieces = (context, context_after, context_top, context_bottom, context_before)
+    theirs, context_pieces = lax.optimization_barrier((theirs, context_pieces))
+    projected = partial_proj + theirs
     grad_resid = norm_back(projected, residual, bias_out, norm_gain, grad_out)
 
     def columns_of(step):

time: 173 us -> 176 us (1.017)
  local copies, waits for them, and re-layouts: 24.2 us -> 29.4 us
    ppermute x1, waiting for transfers between devices: 0.01 us -> 13.4 us  [shards(): before = lax.ppermute(block, 'y', RIGHT)]
    ppermute x1, waiting for transfers between devices: 10.8 us -> 3.75 us  [shards(): context_top = lax.ppermute(context_before[:mid], 'x', RIGHT)]
    ppermute x1, waiting for transfers between devices: 5.22 us -> 0.01 us  [ring_reduce(): from_before = lax.ppermute(ahead, axis, RIGHT)]
    all_to_all x1, starting transfers between devices: 13.9 us -> 10.4 us  [shards(): lax.all_to_all(mine, ('x', 'y', 'z'), split_axis=0, concat_axis=0, tiled=...]
    ppermute x1, waiting for transfers between devices: 7.58 us -> 4.27 us  [shards(): lax.ppermute(half_of(3), 'x', LEFT)]
    ppermute x1, waiting for transfers between devices: 3.23 us -> 0.01 us  [shards(): top = lax.ppermute(before[:2], 'y', RIGHT)]
    ppermute x1, waiting for transfers between devices: 2.48 us -> 5.32 us  [ring_reduce(): from_after = lax.ppermute(behind, axis, LEFT)]
    ppermute x1, starting transfers between devices: 0.49 us -> 2.87 us  [ring_reduce(): from_before = lax.ppermute(ahead, axis, RIGHT)]
  transfers between devices with their start and end apart: 24 -> 24, of which waited for: 15 -> 16; matrix products, arithmetic and copies ran while one was open for 15% -> 16% of each run, Pallas kernels for 0% -> 0%
where the time goes in v8:
time: 176 us; the launch traced here: 174 us
  waiting for transfers between devices  52.4 us (30%)
  starting transfers between devices  44.6 us (25%)
  local copies, waits for them, and re-layouts  29.4 us (17%)
  blocking collectives  20.1 us (11%)
  other arithmetic  11.7 us (7%)
  matrix products  8.11 us (5%)
  Pallas kernels  5.94 us (3%)
    all_to_all x1, blocking collectives, spread(): return lax.all_to_all(whole, axis, split_axis=0, concat_axis=0)  20.1 us
    ppermute x1, waiting for transfers between devices, shards(): before = lax.ppermute(block, 'y', RIGHT)  13.4 us
    all_to_all x1, starting transfers between devices, shards(): lax.all_to_all(mine, ('x', 'y', 'z'), split_axis=0, concat_axis=0, tiled=...  10.4 us
    unnamed x27, local copies, waits for them, and re-layouts  7.79 us
    all_to_all x2, local copies, waits for them, and re-layouts, shards(): lax.all_to_all(mine, ('x', 'y', 'z'), split_axis=0, concat_axis=0, tiled=...  6.47 us
    pallas_call x1, Pallas kernels, project(): pl.pallas_call(project_kernel, out_shape=(jax.ShapeDtypeStruct((4, 4, 128...  5.94 us
    dot_general x1, matrix products, shards(): jnp.dot(grad_resid, weight_t, preferred_element_type=F32).astype(BF16)  5.34 us
    ppermute x1, waiting for transfers between devices, ring_reduce(): from_after = lax.ppermute(behind, axis, LEFT)  5.32 us
  transfers between devices with their start and end apart: 24, of which 16 were waited for; matrix products, arithmetic and copies ran while one was open for 16% of the time, Pallas kernels for 0%

profile of v8, /device:TPU:24, one launch (start us, length us, event | category | flops | bytes accessed | tf_op | source)
XLA Modules:
  0.0 174.0 jit_solution(12615451834560655657)
XLA Ops:
  3.8 20.1 %all_to_all.22 = bf16[8,16,1024]{2,1,0:T(8,128)(2,1)S(1)} all-to-all(bf16[8,16,1024]{2,1,0:T(8,128)(2,1)S(1)} %broadcast_in_dim.16), channel_id=1, replica_groups=mesh['x'=4,'y'=4,'z'=8,'core'=2] {'z'}, dimensions={0} | all-to-all | bytes 524288 | tf_op jit(solution)/shard_map/all_to_all | solution.py:125
  25.4 1.7 %collective-permute-start = (bf16[128,1024]{1,0:T(8,128)(2,1)S(1)}, bf16[128,1024]{1,0:T(8,128)(2,1)S(1)}, u32[]{:S(2)}, u32[]{:S(2)}) collective-permute-start(bf16[128,1024]{1,0:T(8,128)(2,1)S(1)} %bitcast.16), channel_id=1, source_target_pairs={{0,192},{64,0},{128,64},{192,128},{1,193},{65,1},{129,65},{193,129... | collective-permute-start | bytes 786440 | tf_op jit(solution)/shard_map/ppermute | solution.py:31
  27.2 4.3 %collective-permute-done.1 = bf16[128,1024]{1,0:T(8,128)(2,1)S(1)} collective-permute-done((bf16[128,1024]{1,0:T(8,128)(2,1)S(1)}, bf16[128,1024]{1,0:T(8,128)(2,1)S(1)}, u32[]{:S(2)}, u32[]{:S(2)}) %collective-permute-start.1) | collective-permute-done | bytes 262176 | tf_op jit(solution)/shard_map/ppermute | solution.py:30
  33.0 2.7 %collective-permute-start.3 = (bf16[64,1024]{1,0:T(8,128)(2,1)S(1)}, bf16[64,1024]{1,0:T(8,128)(2,1)S(1)}, u32[]{:S(2)}, u32[]{:S(2)}) collective-permute-start(bf16[64,1024]{1,0:T(8,128)(2,1)S(1)} %slice.53), channel_id=1, source_target_pairs={{0,192},{64,0},{128,64},{192,128},{1,193},{65,1},{129,65},{193,129... | collective-permute-start | bytes 393224 | tf_op jit(solution)/shard_map/ppermute | solution.py:33
  40.0 1.8 %collective-permute-start.4 = (bf16[4,128,1024]{2,1,0:T(8,128)(2,1)}, bf16[4,128,1024]{2,1,0:T(8,128)(2,1)}, u32[]{:S(2)}, u32[]{:S(2)}) collective-permute-start(bf16[4,128,1024]{2,1,0:T(8,128)(2,1)} %bitcast.2.refs_1_), channel_id=1, source_target_pairs={{0,48},{16,0},{32,16},{48,32},{1,49},{17,1},{33,17},{49,33},{2,50}... | collective-permute-start | bytes 3145736 | tf_op jit(solution)/shard_map/ppermute | solution.py:154
  41.9 3.3 %all_to_all.15 = bf16[128,3,1024]{2,1,0:T(4,128)(2,1)} reshape(bf16[384,1024]{1,0:T(8,128)(2,1)} %constant_dynamic-slice_fusion.6) | data formatting | bytes 1572864 | tf_op jit(solution)/shard_map/all_to_all | solution.py:147
  45.1 10.4 %all-to-all-start.1 = ((bf16[128,3,1024]{2,1,0:T(4,128)(2,1)}), bf16[128,3,1024]{2,1,0:T(4,128)(2,1)}, u32[]{:S(2)}, u32[]{:S(2)}) async-start(bf16[128,3,1024]{2,1,0:T(4,128)(2,1)} %all_to_all.15), calls=%async_computation.1 | async-start | bytes 2097152 | tf_op jit(solution)/shard_map/all_to_all | solution.py:147
  55.6 1.8 %collective-permute-start.8 = (bf16[384,1024]{1,0:T(8,128)(2,1)S(1)}, bf16[384,1024]{1,0:T(8,128)(2,1)}, u32[]{:S(2)}, u32[]{:S(2)}) collective-permute-start(bf16[384,1024]{1,0:T(8,128)(2,1)S(1)} %copy-done.1), channel_id=1, source_target_pairs={{0,64},{64,128},{128,192},{192,0},{1,65},{65,129},{129,193},{193,1... | collective-permute-start | bytes 2359304 | tf_op jit(solution)/shard_map/ppermute | solution.py:151
  59.1 13.4 %collective-permute-done.5.refs_5_ = bf16[4,128,1024]{2,1,0:T(8,128)(2,1)S(1)} collective-permute-done((bf16[4,128,1024]{2,1,0:T(8,128)(2,1)}, bf16[4,128,1024]{2,1,0:T(8,128)(2,1)S(1)}, u32[]{:S(2)}, u32[]{:S(2)}) %collective-permute-start.5) | collective-permute-done | bytes 1048608 | tf_op jit(solution)/shard_map/ppermute | solution.py:153
  73.9 1.9 %slice.55 = bf16[2,128,1024]{2,1,0:T(8,128)(2,1)} slice(bf16[4,128,1024]{2,1,0:T(8,128)(2,1)} %collective-permute-done.4.refs_2_), slice={[2:4], [0:128], [0:1024]} | slice | bytes 1048576 | tf_op jit(solution)/shard_map/slice | solution.py:157
  77.2 3.2 %all-to-all-done.1 = bf16[128,3,1024]{2,1,0:T(4,128)(2,1)} async-done(((bf16[128,3,1024]{2,1,0:T(4,128)(2,1)}), bf16[128,3,1024]{2,1,0:T(4,128)(2,1)}, u32[]{:S(2)}, u32[]{:S(2)}) %all-to-all-start.1) | async-done | bytes 786464 | tf_op jit(solution)/shard_map/all_to_all | solution.py:147
  80.4 3.2 %all_to_all.17 = bf16[384,1024]{1,0:T(8,128)(2,1)} reshape(bf16[128,3,1024]{2,1,0:T(4,128)(2,1)} %all-to-all-done.1) | data formatting | bytes 1572864 | tf_op jit(solution)/shard_map/all_to_all | solution.py:147
  83.6 2.8 %collective-permute-done.7.refs_4_ = bf16[2,128,1024]{2,1,0:T(8,128)(2,1)} collective-permute-done((bf16[2,128,1024]{2,1,0:T(8,128)(2,1)}, bf16[2,128,1024]{2,1,0:T(8,128)(2,1)}, u32[]{:S(2)}, u32[]{:S(2)}) %collective-permute-start.7) | collective-permute-done | bytes 524320 | tf_op jit(solution)/shard_map/ppermute | solution.py:157
  86.5 5.9 %project.1 = (bf16[4,4,128,1024]{3,2,1,0:T(8,128)(2,1)S(1)}, f32[384,2048]{1,0:T(8,128)}) custom-call(bf16[384,1024]{1,0:T(8,128)(2,1)S(1)} %copy-done.1, bf16[4,128,1024]{2,1,0:T(8,128)(2,1)} %bitcast.2.refs_1_, bf16[4,128,1024]{2,1,0:T(8,128)(2,1)} %collective-permute-done.4.refs_2_, bf16[2,128,1024]{2,1,0:T(8,128)(2,1)} %collective-permute-done.6.refs_3_, ...), custom_call_target="tpu_custom_call" | custom-call | flops 1610612736 | bytes 16777216 | tf_op jit(solution)/shard_map/project/pallas_call | solution.py:102
  92.4 2.0 %copy-done.2 = bf16[4,4,128,1024]{3,2,1,0:T(8,128)(2,1)} copy-done((bf16[4,4,128,1024]{3,2,1,0:T(8,128)(2,1)}, bf16[4,4,128,1024]{3,2,1,0:T(8,128)(2,1)S(1)}, u32[]{:S(2)}) %copy-start.2) | copy-done | bytes 4194328
  95.1 1.8 %slice.42 = bf16[192,1024]{1,0:T(8,128)(2,1)} slice(bf16[384,1024]{1,0:T(8,128)(2,1)} %collective-permute-done.8), slice={[0:192], [0:1024]} | slice | bytes 786432 | tf_op jit(solution)/shard_map/slice | solution.py:162
  96.9 1.8 %collective-permute-start.11 = (bf16[192,1024]{1,0:T(8,128)(2,1)}, bf16[192,1024]{1,0:T(8,128)(2,1)S(1)}, u32[]{:S(2)}, u32[]{:S(2)}) collective-permute-start(bf16[192,1024]{1,0:T(8,128)(2,1)} %slice.42), channel_id=1, source_target_pairs={{0,64},{64,128},{128,192},{192,0},{1,65},{65,129},{129,193},{193,1... | collective-permute-start | bytes 1179656 | tf_op jit(solution)/shard_map/ppermute | solution.py:162
  98.7 1.8 %slice.43 = bf16[192,1024]{1,0:T(8,128)(2,1)} slice(bf16[384,1024]{1,0:T(8,128)(2,1)} %collective-permute-done.9), slice={[192:384], [0:1024]} | slice | bytes 786432 | tf_op jit(solution)/shard_map/slice | solution.py:163
  100.5 3.6 %collective-permute-start.12 = (bf16[192,1024]{1,0:T(8,128)(2,1)}, bf16[192,1024]{1,0:T(8,128)(2,1)}, u32[]{:S(2)}, u32[]{:S(2)}) collective-permute-start(bf16[192,1024]{1,0:T(8,128)(2,1)} %slice.43), channel_id=1, source_target_pairs={{0,192},{64,0},{128,64},{192,128},{1,193},{65,1},{129,65},{193,129... | collective-permute-start | bytes 1179656 | tf_op jit(solution)/shard_map/ppermute | solution.py:163
  104.1 2.7 %gather_fusion = bf16[384,1024]{1,0:T(8,128)(2,1)} fusion(bf16[384,1024]{1,0:T(8,128)(2,1)S(1)} %copy-done.3, s32[1024]{0:T(1024)S(1)} %pad_clamp_fusion), kind=kCustom, calls=%fused_computation | custom fusion | bytes 1574400 | tf_op jit(solution)/shard_map/gather | solution.py:167
  108.4 3.8 %collective-permute-done.11 = bf16[192,1024]{1,0:T(8,128)(2,1)S(1)} collective-permute-done((bf16[192,1024]{1,0:T(8,128)(2,1)}, bf16[192,1024]{1,0:T(8,128)(2,1)S(1)}, u32[]{:S(2)}, u32[]{:S(2)}) %collective-permute-start.11) | collective-permute-done | bytes 393248 | tf_op jit(solution)/shard_map/ppermute | solution.py:162
  113.4 3.6 %fusion.19 = (f32[384]{0:T(512)S(1)}, f32[384,2048]{1,0:T(8,128)S(1)}) fusion(f32[2048]{0:T(1024)S(1)} %copy-done.8, f32[384,2048]{1,0:T(8,128)} %get-tuple-element.31, f32[384,2048]{1,0:T(8,128)} %collective-permute-done.10, bf16[384,2048]{1,0:T(8,128)(2,1)S(1)} %copy-done.6), kind=kLoop, calls=%fused_computation.63 | loop fusion | flops 3931776 | bytes 11019776 | tf_op jit(solution)/shard_map/reduce_sum | solution.py:17
  120.4 3.8 %collective-permute-start.14 = (bf16[192,512]{1,0:T(8,128)(2,1)S(1)}, bf16[192,512]{1,0:T(8,128)(2,1)S(1)}, u32[]{:S(2)}, u32[]{:S(2)}) collective-permute-start(bf16[192,512]{1,0:T(8,128)(2,1)S(1)} %get-tuple-element.51), channel_id=1, source_target_pairs={{0,192},{64,0},{128,64},{192,128},{1,193},{65,1},{129,65},{193,129... | collective-permute-start | bytes 589832 | tf_op jit(solution)/shard_map/ppermute | solution.py:195
  128.1 4.3 %collective-permute-done.14 = bf16[192,512]{1,0:T(8,128)(2,1)S(1)} collective-permute-done((bf16[192,512]{1,0:T(8,128)(2,1)S(1)}, bf16[192,512]{1,0:T(8,128)(2,1)S(1)}, u32[]{:S(2)}, u32[]{:S(2)}) %collective-permute-start.14) | collective-permute-done | bytes 196640 | tf_op jit(solution)/shard_map/ppermute | solution.py:195
  133.5 2.3 %collective-permute-done.16 = bf16[192,512]{1,0:T(8,128)(2,1)S(1)} collective-permute-done((bf16[192,512]{1,0:T(8,128)(2,1)S(1)}, bf16[192,512]{1,0:T(8,128)(2,1)S(1)}, u32[]{:S(2)}, u32[]{:S(2)}) %collective-permute-start.16) | collective-permute-done | bytes 196640 | tf_op jit(solution)/shard_map/ppermute | solution.py:197
  143.7 2.7 %collective-permute-done.18 = bf16[64,1024]{1,0:T(8,128)(2,1)S(1)} collective-permute-done((bf16[64,1024]{1,0:T(8,128)(2,1)S(1)}, bf16[64,1024]{1,0:T(8,128)(2,1)S(1)}, u32[]{:S(2)}, u32[]{:S(2)}) %collective-permute-start.18) | collective-permute-done | bytes 131104 | tf_op jit(solution)/shard_map/ppermute | solution.py:53
  149.3 2.9 %collective-permute-start.19 = (bf16[128,1024]{1,0:T(8,128)(2,1)S(1)}, bf16[128,1024]{1,0:T(8,128)(2,1)S(1)}, u32[]{:S(2)}, u32[]{:S(2)}) collective-permute-start(bf16[128,1024]{1,0:T(8,128)(2,1)S(1)} %pad_maximum_fusion), channel_id=1, source_target_pairs={{0,16},{16,32},{32,48},{48,0},{1,17},{17,33},{33,49},{49,1},{2,18}... | collective-permute-start | bytes 786440 | tf_op jit(solution)/shard_map/ppermute | solution.py:58
  152.2 5.3 %collective-permute-done.21 = bf16[128,1024]{1,0:T(8,128)(2,1)S(1)} collective-permute-done((bf16[128,1024]{1,0:T(8,128)(2,1)S(1)}, bf16[128,1024]{1,0:T(8,128)(2,1)S(1)}, u32[]{:S(2)}, u32[]{:S(2)}) %collective-permute-start.21) | collective-permute-done | bytes 262176 | tf_op jit(solution)/shard_map/ppermute | solution.py:59
  157.5 1.9 %add_convert_fusion = bf16[128,1024]{1,0:T(8,128)(2,1)} fusion(bf16[128,1024]{1,0:T(8,128)(2,1)S(1)} %collective-permute-done.21, bf16[128,1024]{1,0:T(8,128)(2,1)S(1)} %collective-permute-done.19, f32[512,1024]{1,0:T(8,128)} %copy-done.4, s32[]{:T(128)S(6)} %select_n.66), kind=kLoop, calls=%fused_computation.23 | loop fusion | flops 655360 | bytes 1310724 | tf_op jit(solution)/shard_map/convert_element_type | solution.py:130
  159.4 3.4 %all-to-all-start.2 = ((bf16[8,16,1024]{2,1,0:T(8,128)(2,1)}), bf16[8,16,1024]{2,1,0:T(8,128)(2,1)S(1)}, u32[]{:S(2)}, u32[]{:S(2)}) async-start(bf16[8,16,1024]{2,1,0:T(8,128)(2,1)} %bitcast.5), calls=%async_computation.2 | async-start | bytes 524288 | tf_op jit(solution)/shard_map/all_to_all | solution.py:131
  162.8 5.3 %convolution_convert_fusion = bf16[384,1024]{1,0:T(8,128)(2,1)} fusion(bf16[384,2048]{1,0:T(8,128)(2,1)} %copy-done.5, bf16[2048,1024]{1,0:T(8,128)(2,1)} %bitcast.14), kind=kOutput, calls=%fused_computation.9 | convolution fusion | flops 1611005952 | bytes 6553600 | tf_op jit(solution)/shard_map/dot_general | solution.py:218
  168.2 5.2 %all-to-all-done.2 = bf16[8,16,1024]{2,1,0:T(8,128)(2,1)S(1)} async-done(((bf16[8,16,1024]{2,1,0:T(8,128)(2,1)}), bf16[8,16,1024]{2,1,0:T(8,128)(2,1)S(1)}, u32[]{:S(2)}, u32[]{:S(2)}) %all-to-all-start.2) | async-done | bytes 262176 | tf_op jit(solution)/shard_map/all_to_all | solution.py:131
  (86 shorter events, 37.9 us)
Async XLA Ops:
  0.6 1.4 copy-start
  23.9 7.6 %collective-permute-start.1 = (bf16[128,1024]{1,0:T(8,128)(2,1)S(1)}, bf16[128,1024]{1,0:T(8,128)(2,1)S(1)}, u32[]{:S(2)}, u32[]{:S(2)}) collective-permute-start(bf16[128,1024]{1,0:T(8,128)(2,1)S(1)} %bitcast.15), channel_id=1, source_target_pairs={{0,64},{64,128},{128,192},{192,0},{1,65},{65,129},{129,193},{193,1... | collective-permute-start | bytes 786440 | tf_op jit(solution)/shard_map/ppermute | solution.py:30
  25.4 7.5 %collective-permute-start = (bf16[128,1024]{1,0:T(8,128)(2,1)S(1)}, bf16[128,1024]{1,0:T(8,128)(2,1)S(1)}, u32[]{:S(2)}, u32[]{:S(2)}) collective-permute-start(bf16[128,1024]{1,0:T(8,128)(2,1)S(1)} %bitcast.16), channel_id=1, source_target_pairs={{0,192},{64,0},{128,64},{192,128},{1,193},{65,1},{129,65},{193,129... | collective-permute-start | bytes 786440 | tf_op jit(solution)/shard_map/ppermute | solution.py:31
  31.5 6.3 %collective-permute-start.2 = (bf16[64,1024]{1,0:T(8,128)(2,1)S(1)}, bf16[64,1024]{1,0:T(8,128)(2,1)S(1)}, u32[]{:S(2)}, u32[]{:S(2)}) collective-permute-start(bf16[64,1024]{1,0:T(8,128)(2,1)S(1)} %slice.52), channel_id=1, source_target_pairs={{0,64},{64,128},{128,192},{192,0},{1,65},{65,129},{129,193},{193,1... | collective-permute-start | bytes 393224 | tf_op jit(solution)/shard_map/ppermute | solution.py:32
  33.0 5.5 %collective-permute-start.3 = (bf16[64,1024]{1,0:T(8,128)(2,1)S(1)}, bf16[64,1024]{1,0:T(8,128)(2,1)S(1)}, u32[]{:S(2)}, u32[]{:S(2)}) collective-permute-start(bf16[64,1024]{1,0:T(8,128)(2,1)S(1)} %slice.53), channel_id=1, source_target_pairs={{0,192},{64,0},{128,64},{192,128},{1,193},{65,1},{129,65},{193,129... | collective-permute-start | bytes 393224 | tf_op jit(solution)/shard_map/ppermute | solution.py:33
  38.4 17.2 %copy-start.1 = (bf16[384,1024]{1,0:T(8,128)(2,1)S(1)}, bf16[384,1024]{1,0:T(8,128)(2,1)}, u32[]{:S(2)}) copy-start(bf16[384,1024]{1,0:T(8,128)(2,1)} %refs_0_.1) | copy-start | bytes 2359300
  39.8 32.6 %collective-permute-start.5 = (bf16[4,128,1024]{2,1,0:T(8,128)(2,1)}, bf16[4,128,1024]{2,1,0:T(8,128)(2,1)S(1)}, u32[]{:S(2)}, u32[]{:S(2)}) collective-permute-start(bf16[4,128,1024]{2,1,0:T(8,128)(2,1)} %bitcast.2.refs_1_), channel_id=1, source_target_pairs={{0,16},{16,32},{32,48},{48,0},{1,17},{17,33},{33,49},{49,1},{2,18}... | collective-permute-start | bytes 3145736 | tf_op jit(solution)/shard_map/ppermute | solution.py:153
  40.0 33.8 %collective-permute-start.4 = (bf16[4,128,1024]{2,1,0:T(8,128)(2,1)}, bf16[4,128,1024]{2,1,0:T(8,128)(2,1)}, u32[]{:S(2)}, u32[]{:S(2)}) collective-permute-start(bf16[4,128,1024]{2,1,0:T(8,128)(2,1)} %bitcast.2.refs_1_), channel_id=1, source_target_pairs={{0,48},{16,0},{32,16},{48,32},{1,49},{17,1},{33,17},{49,33},{2,50}... | collective-permute-start | bytes 3145736 | tf_op jit(solution)/shard_map/ppermute | solution.py:154
  45.1 35.3 %all-to-all-start.1 = ((bf16[128,3,1024]{2,1,0:T(4,128)(2,1)}), bf16[128,3,1024]{2,1,0:T(4,128)(2,1)}, u32[]{:S(2)}, u32[]{:S(2)}) async-start(bf16[128,3,1024]{2,1,0:T(4,128)(2,1)} %all_to_all.15), calls=%async_computation.1 | async-start | bytes 2097152 | tf_op jit(solution)/shard_map/all_to_all | solution.py:147
  55.6 28.0 %collective-permute-start.8 = (bf16[384,1024]{1,0:T(8,128)(2,1)S(1)}, bf16[384,1024]{1,0:T(8,128)(2,1)}, u32[]{:S(2)}, u32[]{:S(2)}) collective-permute-start(bf16[384,1024]{1,0:T(8,128)(2,1)S(1)} %copy-done.1), channel_id=1, source_target_pairs={{0,64},{64,128},{128,192},{192,0},{1,65},{65,129},{129,193},{193,1... | collective-permute-start | bytes 2359304 | tf_op jit(solution)/shard_map/ppermute | solution.py:151
  57.4 26.3 %collective-permute-start.9 = (bf16[384,1024]{1,0:T(8,128)(2,1)S(1)}, bf16[384,1024]{1,0:T(8,128)(2,1)}, u32[]{:S(2)}, u32[]{:S(2)}) collective-permute-start(bf16[384,1024]{1,0:T(8,128)(2,1)S(1)} %copy-done.1), channel_id=1, source_target_pairs={{0,192},{64,0},{128,64},{192,128},{1,193},{65,1},{129,65},{193,129... | collective-permute-start | bytes 2359304 | tf_op jit(solution)/shard_map/ppermute | solution.py:152
  73.3 10.3 %collective-permute-start.6 = (bf16[2,128,1024]{2,1,0:T(8,128)(2,1)}, bf16[2,128,1024]{2,1,0:T(8,128)(2,1)}, u32[]{:S(2)}, u32[]{:S(2)}) collective-permute-start(bf16[2,128,1024]{2,1,0:T(8,128)(2,1)} %slice.54), channel_id=1, source_target_pairs={{0,16},{16,32},{32,48},{48,0},{1,17},{17,33},{33,49},{49,1},{2,18}... | collective-permute-start | bytes 1572872 | tf_op jit(solution)/shard_map/ppermute | solution.py:156
  75.7 10.7 %collective-permute-start.7 = (bf16[2,128,1024]{2,1,0:T(8,128)(2,1)}, bf16[2,128,1024]{2,1,0:T(8,128)(2,1)}, u32[]{:S(2)}, u32[]{:S(2)}) collective-permute-start(bf16[2,128,1024]{2,1,0:T(8,128)(2,1)} %slice.55), channel_id=1, source_target_pairs={{0,48},{16,0},{32,16},{48,32},{1,49},{17,1},{33,17},{49,33},{2,50}... | collective-permute-start | bytes 1572872 | tf_op jit(solution)/shard_map/ppermute | solution.py:157
  83.6 11.5 %copy-start.9 = (s32[384]{0:T(512)S(1)}, s32[384]{0:T(512)}, u32[]{:S(2)}) copy-start(s32[384]{0:T(512)} %param.15) | copy-start | bytes 4612
  92.4 2.0 %copy-start.2 = (bf16[4,4,128,1024]{3,2,1,0:T(8,128)(2,1)}, bf16[4,4,128,1024]{3,2,1,0:T(8,128)(2,1)S(1)}, u32[]{:S(2)}) copy-start(bf16[4,4,128,1024]{3,2,1,0:T(8,128)(2,1)S(1)} %get-tuple-element.36) | copy-start | bytes 12582916
  94.4 9.7 %copy-start.3 = (bf16[384,1024]{1,0:T(8,128)(2,1)S(1)}, bf16[384,1024]{1,0:T(8,128)(2,1)}, u32[]{:S(2)}) copy-start(bf16[384,1024]{1,0:T(8,128)(2,1)} %all_to_all.17) | copy-start | bytes 2359300
  94.4 19.0 %collective-permute-start.10 = (f32[384,2048]{1,0:T(8,128)}, f32[384,2048]{1,0:T(8,128)}, u32[]{:S(2)}, u32[]{:S(2)}) collective-permute-start(f32[384,2048]{1,0:T(8,128)} %get-tuple-element.31), channel_id=1, source_target_pairs={{0,1},{1,0},{2,3},{3,2},{4,5},{5,4},{6,7},{7,6},{8,9},{9,8},{10,11... | collective-permute-start | bytes 9437192 | tf_op jit(solution)/shard_map/ppermute | solution.py:175
  96.9 15.3 %collective-permute-start.11 = (bf16[192,1024]{1,0:T(8,128)(2,1)}, bf16[192,1024]{1,0:T(8,128)(2,1)S(1)}, u32[]{:S(2)}, u32[]{:S(2)}) collective-permute-start(bf16[192,1024]{1,0:T(8,128)(2,1)} %slice.42), channel_id=1, source_target_pairs={{0,64},{64,128},{128,192},{192,0},{1,65},{65,129},{129,193},{193,1... | collective-permute-start | bytes 1179656 | tf_op jit(solution)/shard_map/ppermute | solution.py:162
  100.5 12.9 %collective-permute-start.12 = (bf16[192,1024]{1,0:T(8,128)(2,1)}, bf16[192,1024]{1,0:T(8,128)(2,1)}, u32[]{:S(2)}, u32[]{:S(2)}) collective-permute-start(bf16[192,1024]{1,0:T(8,128)(2,1)} %slice.43), channel_id=1, source_target_pairs={{0,192},{64,0},{128,64},{192,128},{1,193},{65,1},{129,65},{193,129... | collective-permute-start | bytes 1179656 | tf_op jit(solution)/shard_map/ppermute | solution.py:163
  104.1 9.3 %copy-start.8 = (f32[2048]{0:T(1024)S(1)}, f32[2048]{0:T(1024)}, u32[]{:S(2)}) copy-start(f32[2048]{0:T(1024)} %param.10) | copy-start | bytes 24580
  106.8 6.6 %copy-start.6 = (bf16[384,2048]{1,0:T(8,128)(2,1)S(1)}, bf16[384,2048]{1,0:T(8,128)(2,1)}, u32[]{:S(2)}) copy-start(bf16[384,2048]{1,0:T(8,128)(2,1)} %param.9) | copy-start | bytes 4718596
  108.2 9.2 %collective-permute-start.13 = (bf16[384,1024]{1,0:T(8,128)(2,1)S(1)}, bf16[384,1024]{1,0:T(8,128)(2,1)S(1)}, u32[]{:S(2)}, u32[]{:S(2)}) collective-permute-start(bf16[384,1024]{1,0:T(8,128)(2,1)S(1)} %broadcast_select_fusion), channel_id=1, source_target_pairs={{0,1},{1,0},{2,3},{3,2},{4,5},{5,4},{6,7},{7,6},{8,9},{9,8},{10,11... | collective-permute-start | bytes 2359304 | tf_op jit(solution)/shard_map/ppermute | solution.py:169
  120.3 15.9 %copy-start.5 = (bf16[384,2048]{1,0:T(8,128)(2,1)}, bf16[384,2048]{1,0:T(8,128)(2,1)S(1)}, u32[]{:S(2)}) copy-start(bf16[384,2048]{1,0:T(8,128)(2,1)S(1)} %multiply_convert_fusion) | copy-start | bytes 4718596
  120.4 12.0 %collective-permute-start.14 = (bf16[192,512]{1,0:T(8,128)(2,1)S(1)}, bf16[192,512]{1,0:T(8,128)(2,1)S(1)}, u32[]{:S(2)}, u32[]{:S(2)}) collective-permute-start(bf16[192,512]{1,0:T(8,128)(2,1)S(1)} %get-tuple-element.51), channel_id=1, source_target_pairs={{0,192},{64,0},{128,64},{192,128},{1,193},{65,1},{129,65},{193,129... | collective-permute-start | bytes 589832 | tf_op jit(solution)/shard_map/ppermute | solution.py:195
  124.2 9.3 %collective-permute-start.15 = (bf16[192,512]{1,0:T(8,128)(2,1)S(1)}, bf16[192,512]{1,0:T(8,128)(2,1)S(1)}, u32[]{:S(2)}, u32[]{:S(2)}) collective-permute-start(bf16[192,512]{1,0:T(8,128)(2,1)S(1)} %get-tuple-element.50), channel_id=1, source_target_pairs={{0,128},{64,192},{128,0},{192,64},{1,129},{65,193},{129,1},{193,65... | collective-permute-start | bytes 589832 | tf_op jit(solution)/shard_map/ppermute | solution.py:196
  124.4 11.4 %collective-permute-start.16 = (bf16[192,512]{1,0:T(8,128)(2,1)S(1)}, bf16[192,512]{1,0:T(8,128)(2,1)S(1)}, u32[]{:S(2)}, u32[]{:S(2)}) collective-permute-start(bf16[192,512]{1,0:T(8,128)(2,1)S(1)} %get-tuple-element.49), channel_id=1, source_target_pairs={{0,64},{64,128},{128,192},{192,0},{1,65},{65,129},{129,193},{193,1... | collective-permute-start | bytes 589832 | tf_op jit(solution)/shard_map/ppermute | solution.py:197
  135.8 2.3 %collective-permute-start.17 = (bf16[576,512]{1,0:T(8,128)(2,1)S(1)}, bf16[576,512]{1,0:T(8,128)(2,1)S(1)}, u32[]{:S(2)}, u32[]{:S(2)}) collective-permute-start(bf16[576,512]{1,0:T(8,128)(2,1)S(1)} %constant_dynamic-update-slice_fusion.5), channel_id=1, source_target_pairs={{0,1},{1,0},{2,3},{3,2},{4,5},{5,4},{6,7},{7,6},{8,9},{9,8},{10,11... | collective-permute-start | bytes 1769480 | tf_op jit(solution)/shard_map/ppermute | solution.py:199
  140.5 5.8 %collective-permute-start.18 = (bf16[64,1024]{1,0:T(8,128)(2,1)S(1)}, bf16[64,1024]{1,0:T(8,128)(2,1)S(1)}, u32[]{:S(2)}, u32[]{:S(2)}) collective-permute-start(bf16[64,1024]{1,0:T(8,128)(2,1)S(1)} %get-tuple-element.58), channel_id=1, source_target_pairs={{0,16},{16,32},{32,48},{48,0},{1,17},{17,33},{33,49},{49,1},{2,18}... | collective-permute-start | bytes 393224 | tf_op jit(solution)/shard_map/ppermute | solution.py:53
  141.0 6.7 %collective-permute-start.20 = (bf16[64,1024]{1,0:T(8,128)(2,1)S(1)}, bf16[64,1024]{1,0:T(8,128)(2,1)S(1)}, u32[]{:S(2)}, u32[]{:S(2)}) collective-permute-start(bf16[64,1024]{1,0:T(8,128)(2,1)S(1)} %get-tuple-element.59), channel_id=1, source_target_pairs={{0,48},{16,0},{32,16},{48,32},{1,49},{17,1},{33,17},{49,33},{2,50}... | collective-permute-start | bytes 393224 | tf_op jit(solution)/shard_map/ppermute | solution.py:54
  148.8 8.7 %collective-permute-start.21 = (bf16[128,1024]{1,0:T(8,128)(2,1)S(1)}, bf16[128,1024]{1,0:T(8,128)(2,1)S(1)}, u32[]{:S(2)}, u32[]{:S(2)}) collective-permute-start(bf16[128,1024]{1,0:T(8,128)(2,1)S(1)} %pad_maximum_fusion.1), channel_id=1, source_target_pairs={{0,48},{16,0},{32,16},{48,32},{1,49},{17,1},{33,17},{49,33},{2,50}... | collective-permute-start | bytes 786440 | tf_op jit(solution)/shard_map/ppermute | solution.py:59
  149.3 8.2 %collective-permute-start.19 = (bf16[128,1024]{1,0:T(8,128)(2,1)S(1)}, bf16[128,1024]{1,0:T(8,128)(2,1)S(1)}, u32[]{:S(2)}, u32[]{:S(2)}) collective-permute-start(bf16[128,1024]{1,0:T(8,128)(2,1)S(1)} %pad_maximum_fusion), channel_id=1, source_target_pairs={{0,16},{16,32},{32,48},{48,0},{1,17},{17,33},{33,49},{49,1},{2,18}... | collective-permute-start | bytes 786440 | tf_op jit(solution)/shard_map/ppermute | solution.py:58
  159.4 14.0 %all-to-all-start.2 = ((bf16[8,16,1024]{2,1,0:T(8,128)(2,1)}), bf16[8,16,1024]{2,1,0:T(8,128)(2,1)S(1)}, u32[]{:S(2)}, u32[]{:S(2)}) async-start(bf16[8,16,1024]{2,1,0:T(8,128)(2,1)} %bitcast.5), calls=%async_computation.2 | async-start | bytes 524288 | tf_op jit(solution)/shard_map/all_to_all | solution.py:131
  (2 other events, 2.1 us)

commit v9 on v6

--- a/solution.py
+++ b/solution.py
@@ -74,14 +74,17 @@
 
 
 def project_kernel(*refs):
-    context_ref, pieces = refs[0], refs[1:6]
-    weight_ref, out_ref = refs[6], refs[7]
-    placed, sems = refs[8], refs[9]
+    context_ref, a_pieces, b_pieces = refs[0], refs[1:6], refs[6:11]
+    weight_ref, out_ref = refs[11], refs[12]
+    placed, sems = refs[13], refs[14]
     ix, iy = lax.axis_index("x"), lax.axis_index("y")
-    for ref, step, low in zip(pieces, (0, 1, 2, 2, 3), (0, 0, 0, 2, 0)):
-        at = lax.rem(iy + step, 4)
+    steps, lows = (0, 1, 2, 2, 3), (0, 0, 0, 2, 0)
+    for ref, step, low in zip(a_pieces, steps, lows):
         for k in range(ref.shape[0]):
-            placed[lax.rem(ix + low + k, 4), at] = ref[k]
+            placed[lax.rem(ix + step, 4), lax.rem(iy + low + k, 4), :, 0:512] = ref[k]
+    for ref, step, low in zip(b_pieces, steps, lows):
+        for k in range(ref.shape[0]):
+            placed[lax.rem(ix + low + k, 4), lax.rem(iy + step, 4), :, 512:1024] = ref[k]
     copies = [
         pltpu.make_async_copy(placed.at[x], weight_ref.at[x], sems.at[x]) for x in range(4)
     ]
@@ -105,7 +108,7 @@
             jax.ShapeDtypeStruct((4, 4, 128, 1024), BF16),
             jax.ShapeDtypeStruct((rows, 2048), F32),
         ),
-        in_specs=[vmem] * 6,
+        in_specs=[vmem] * 11,
         out_specs=(pl.BlockSpec(memory_space=pltpu.HBM), vmem),
         scratch_shapes=[
             pltpu.VMEM((4, 4, 128, 1024), BF16),
@@ -155,13 +158,21 @@
     context_top = lax.ppermute(context_before[:mid], "x", RIGHT)
     context_bottom = lax.ppermute(context_after[mid:], "x", LEFT)
     context_pieces = (context, context_after, context_top, context_bottom, context_before)
-    block = jnp.concatenate(ring_gather(block, "x")).reshape(4, 128, 1024)
-    before = lax.ppermute(block, "y", RIGHT)
-    after = lax.ppermute(block, "y", LEFT)
-    before, after, context_pieces = lax.optimization_barrier((before, after, context_pieces))
-    top = lax.ppermute(before[:2], "y", RIGHT)
-    bottom = lax.ppermute(after[2:], "y", LEFT)
-    pieces = (block, after, top, bottom, before)
+    a_block = jnp.concatenate(ring_gather(block[:, :512], "y")).reshape(4, 128, 512)
+    b_block = jnp.concatenate(ring_gather(block[:, 512:], "x")).reshape(4, 128, 512)
+    a_before = lax.ppermute(a_block, "x", RIGHT)
+    a_after = lax.ppermute(a_block, "x", LEFT)
+    b_before = lax.ppermute(b_block, "y", RIGHT)
+    b_after = lax.ppermute(b_block, "y", LEFT)
+    a_before, a_after, b_before, b_after, context_pieces = lax.optimization_barrier(
+        (a_before, a_after, b_before, b_after, context_pieces)
+    )
+    a_top = lax.ppermute(a_before[:2], "x", RIGHT)
+    a_bottom = lax.ppermute(a_after[2:], "x", LEFT)
+    b_top = lax.ppermute(b_before[:2], "y", RIGHT)
+    b_bottom = lax.ppermute(b_after[2:], "y", LEFT)
+    pieces = (a_block, a_after, a_top, a_bottom, a_before)
+    pieces = pieces + (b_block, b_after, b_top, b_bottom, b_before)
     pieces, returned = lax.optimization_barrier((pieces, returned))
 
     weight_t, partial_proj = project(context, pieces)

time: 173 us -> 192 us (1.11)
  starting transfers between devices: 46.3 us -> 53.9 us
  waiting for transfers between devices: 53.6 us -> 59.7 us
  local copies, waits for them, and re-layouts: 24.2 us -> 30 us
    ppermute x1, waiting for transfers between devices: 1.63 us -> 14.9 us  [shards(): context_bottom = lax.ppermute(context_after[mid:], 'x', LEFT)]
    ppermute x1, waiting for transfers between devices: 10.8 us -> 0.01 us  [shards(): context_top = lax.ppermute(context_before[:mid], 'x', RIGHT)]
    ppermute x1 -> x2, waiting for transfers between devices: 1.41 us -> 11.6 us  [ring_gather(): top = lax.ppermute(before[:mid], axis, RIGHT)]
    ppermute x4 -> x8, starting transfers between devices: 4.05 us -> 11.9 us  [the longest x1 2.95 us: shards(): a_after = lax.ppermute(a_block, 'x', LEFT)]
    ppermute x1 -> x2, waiting for transfers between devices: 4.35 us -> 0.01 us  [ring_gather(): before = lax.ppermute(piece, axis, RIGHT)]
    unnamed x47 -> x57, local copies, waits for them, and re-layouts: 7.39 us -> 11.2 us
    all_to_all x1, starting transfers between devices: 13.9 us -> 11.5 us  [shards(): lax.all_to_all(mine, ('x', 'y', 'z'), split_axis=0, concat_axis=0, tiled=...]
    ppermute x1 -> x2, starting transfers between devices: 0.08 us -> 2.24 us  [ring_gather(): top = lax.ppermute(before[:mid], axis, RIGHT)]
  transfers between devices with their start and end apart: 24 -> 32, of which waited for: 15 -> 12; matrix products, arithmetic and copies ran while one was open for 15% -> 14% of each run, Pallas kernels for 0% -> 0%
where the time goes in v9:
time: 192 us; the launch traced here: 191 us
  waiting for transfers between devices  59.7 us (31%)
  starting transfers between devices  53.9 us (28%)
  local copies, waits for them, and re-layouts  30 us (16%)
  blocking collectives  19.6 us (10%)
  other arithmetic  13.2 us (7%)
  matrix products  7.6 us (4%)
  Pallas kernels  5.52 us (3%)
    all_to_all x1, blocking collectives, spread(): return lax.all_to_all(whole, axis, split_axis=0, concat_axis=0)  19.6 us
    ppermute x1, waiting for transfers between devices, shards(): context_bottom = lax.ppermute(context_after[mid:], 'x', LEFT)  14.9 us
    ppermute x2, waiting for transfers between devices, ring_gather(): top = lax.ppermute(before[:mid], axis, RIGHT)  11.6 us
    all_to_all x1, starting transfers between devices, shards(): lax.all_to_all(mine, ('x', 'y', 'z'), split_axis=0, concat_axis=0, tiled=...  11.5 us
    unnamed x57, local copies, waits for them, and re-layouts  11.2 us
    ppermute x1, waiting for transfers between devices, shards(): lax.ppermute(half_of(3), 'x', LEFT)  7.53 us
    all_to_all x1, starting transfers between devices, collect(): got = lax.all_to_all(share, axis, split_axis=0, concat_axis=0)  6.03 us
    all_to_all x1, waiting for transfers between devices, collect(): got = lax.all_to_all(share, axis, split_axis=0, concat_axis=0)  5.75 us
  transfers between devices with their start and end apart: 32, of which 12 were waited for; matrix products, arithmetic and copies ran while one was open for 14% of the time, Pallas kernels for 0%

profile of v9, /device:TPU:24, one launch (start us, length us, event | category | flops | bytes accessed | tf_op | source)
XLA Modules:
  0.0 191.2 jit_solution(249545881419963817)
XLA Ops:
  2.2 1.7 collective-permute-start.1
  4.8 19.6 %all_to_all.22 = bf16[8,16,1024]{2,1,0:T(8,128)(2,1)S(1)} all-to-all(bf16[8,16,1024]{2,1,0:T(8,128)(2,1)S(1)} %broadcast_in_dim.16), channel_id=1, replica_groups=mesh['x'=4,'y'=4,'z'=8,'core'=2] {'z'}, dimensions={0} | all-to-all | bytes 524288 | tf_op jit(solution)/shard_map/all_to_all | solution.py:128
  25.4 3.0 %collective-permute-start.8 = (bf16[128,512]{1,0:T(8,128)(2,1)}, bf16[128,512]{1,0:T(8,128)(2,1)S(1)}, u32[]{:S(2)}, u32[]{:S(2)}) collective-permute-start(bf16[128,512]{1,0:T(8,128)(2,1)} %get-tuple-element.74), channel_id=1, source_target_pairs={{0,192},{64,0},{128,64},{192,128},{1,193},{65,1},{129,65},{193,129... | collective-permute-start | bytes 393224 | tf_op jit(solution)/shard_map/ppermute | solution.py:31
  28.6 1.8 collective-permute-start.2
  31.7 11.5 %all-to-all-start.1 = ((bf16[128,3,1024]{2,1,0:T(4,128)(2,1)}), bf16[128,3,1024]{2,1,0:T(4,128)(2,1)}, u32[]{:S(2)}, u32[]{:S(2)}) async-start(bf16[128,3,1024]{2,1,0:T(4,128)(2,1)} %all_to_all.15), calls=%async_computation.1 | async-start | bytes 2097152 | tf_op jit(solution)/shard_map/all_to_all | solution.py:150
  44.2 1.8 collective-permute-start.14
  45.9 1.8 collective-permute-start.10
  47.7 1.6 collective-permute-start.11
  49.8 1.7 collective-permute-start.5
  52.2 11.6 %collective-permute-done.10 = bf16[64,512]{1,0:T(8,128)(2,1)S(1)} collective-permute-done((bf16[64,512]{1,0:T(8,128)(2,1)S(1)}, bf16[64,512]{1,0:T(8,128)(2,1)S(1)}, u32[]{:S(2)}, u32[]{:S(2)}) %collective-permute-start.10) | collective-permute-done | bytes 65568 | tf_op jit(solution)/shard_map/ppermute | solution.py:32
  68.9 3.0 %collective-permute-start.7 = (bf16[4,128,512]{2,1,0:T(8,128)(2,1)}, bf16[4,128,512]{2,1,0:T(8,128)(2,1)S(1)}, u32[]{:S(2)}, u32[]{:S(2)}) collective-permute-start(bf16[4,128,512]{2,1,0:T(8,128)(2,1)} %bitcast.16), channel_id=1, source_target_pairs={{0,192},{64,0},{128,64},{192,128},{1,193},{65,1},{129,65},{193,129... | collective-permute-start | bytes 1572872 | tf_op jit(solution)/shard_map/ppermute | solution.py:164
  73.5 14.9 %collective-permute-done.15 = bf16[192,1024]{1,0:T(8,128)(2,1)S(1)} collective-permute-done((bf16[192,1024]{1,0:T(8,128)(2,1)S(1)}, bf16[192,1024]{1,0:T(8,128)(2,1)S(1)}, u32[]{:S(2)}, u32[]{:S(2)}) %collective-permute-start.15) | collective-permute-done | bytes 393248 | tf_op jit(solution)/shard_map/ppermute | solution.py:159
  92.4 2.7 %collective-permute-start.17 = (bf16[2,128,512]{2,1,0:T(8,128)(2,1)}, bf16[2,128,512]{2,1,0:T(8,128)(2,1)}, u32[]{:S(2)}, u32[]{:S(2)}) collective-permute-start(bf16[2,128,512]{2,1,0:T(8,128)(2,1)} %slice.65), channel_id=1, source_target_pairs={{0,192},{64,0},{128,64},{192,128},{1,193},{65,1},{129,65},{193,129... | collective-permute-start | bytes 786440 | tf_op jit(solution)/shard_map/ppermute | solution.py:171
  95.9 2.9 %collective-permute-start.18 = (bf16[2,128,512]{2,1,0:T(8,128)(2,1)}, bf16[2,128,512]{2,1,0:T(8,128)(2,1)}, u32[]{:S(2)}, u32[]{:S(2)}) collective-permute-start(bf16[2,128,512]{2,1,0:T(8,128)(2,1)} %slice.66), channel_id=1, source_target_pairs={{0,16},{16,32},{32,48},{48,0},{1,17},{17,33},{33,49},{49,1},{2,18}... | collective-permute-start | bytes 786440 | tf_op jit(solution)/shard_map/ppermute | solution.py:172
  99.5 3.2 %all_to_all.17 = bf16[384,1024]{1,0:T(8,128)(2,1)} reshape(bf16[128,3,1024]{2,1,0:T(4,128)(2,1)} %all-to-all-done.1) | data formatting | bytes 1572864 | tf_op jit(solution)/shard_map/all_to_all | solution.py:150
  103.0 4.4 %collective-permute-done.19.refs_9_ = bf16[2,128,512]{2,1,0:T(8,128)(2,1)} collective-permute-done((bf16[2,128,512]{2,1,0:T(8,128)(2,1)}, bf16[2,128,512]{2,1,0:T(8,128)(2,1)}, u32[]{:S(2)}, u32[]{:S(2)}) %collective-permute-start.19) | collective-permute-done | bytes 262176 | tf_op jit(solution)/shard_map/ppermute | solution.py:173
  110.6 5.5 %project.1 = (bf16[4,4,128,1024]{3,2,1,0:T(8,128)(2,1)S(1)}, f32[384,2048]{1,0:T(8,128)}) custom-call(bf16[384,1024]{1,0:T(8,128)(2,1)S(1)} %copy-done.1, bf16[4,128,512]{2,1,0:T(8,128)(2,1)S(1)} %bitcast.17, bf16[4,128,512]{2,1,0:T(8,128)(2,1)S(1)} %copy-done.5, bf16[2,128,512]{2,1,0:T(8,128)(2,1)} %collective-permute-done.16.refs_3_, ...), custom_call_target="tpu_custom_call" | custom-call | flops 1610612736 | bytes 16777216 | tf_op jit(solution)/shard_map/project/pallas_call | solution.py:105
  116.1 2.0 %copy-done.8 = bf16[4,4,128,1024]{3,2,1,0:T(8,128)(2,1)} copy-done((bf16[4,4,128,1024]{3,2,1,0:T(8,128)(2,1)}, bf16[4,4,128,1024]{3,2,1,0:T(8,128)(2,1)S(1)}, u32[]{:S(2)}) %copy-start.8) | copy-done | bytes 4194328
  118.9 2.4 %constant_dynamic-slice_fusion = (bf16[192,1024]{1,0:T(8,128)(2,1)S(1)}, bf16[192,1024]{1,0:T(8,128)(2,1)}, bf16[192,1024]{1,0:T(8,128)(2,1)}, bf16[192,1024]{1,0:T(8,128)(2,1)}) fusion(bf16[384,1024]{1,0:T(8,128)(2,1)} %collective-permute-done, s32[]{:T(128)S(6)} %select_n.65, s32[]{:T(128)S(6)} %select_n.61, bf16[384,1024]{1,0:T(8,128)(2,1)} %collective-permute-done.1), kind=kLoop, calls=%fused_computation.53 | loop fusion | bytes 3145736 | tf_op jit(solution)/shard_map/dynamic_slice | solution.py:215
  121.3 2.7 %gather_fusion = bf16[384,1024]{1,0:T(8,128)(2,1)} fusion(bf16[384,1024]{1,0:T(8,128)(2,1)S(1)} %copy-done.9, s32[1024]{0:T(1024)S(1)} %pad_clamp_fusion), kind=kCustom, calls=%fused_computation | custom fusion | bytes 1574400 | tf_op jit(solution)/shard_map/gather | solution.py:180
  126.1 3.6 %fusion.19 = (f32[384]{0:T(512)S(1)}, f32[384,2048]{1,0:T(8,128)S(1)}) fusion(f32[2048]{0:T(1024)S(1)} %copy-done.22, f32[384,2048]{1,0:T(8,128)} %get-tuple-element.48, f32[384,2048]{1,0:T(8,128)} %collective-permute-done.20, bf16[384,2048]{1,0:T(8,128)(2,1)S(1)} %copy-done.14), kind=kLoop, calls=%fused_computation.68 | loop fusion | flops 3931776 | bytes 11019776 | tf_op jit(solution)/shard_map/reduce_sum | solution.py:17
  133.1 2.1 %collective-permute-start.22 = (bf16[192,512]{1,0:T(8,128)(2,1)S(1)}, bf16[192,512]{1,0:T(8,128)(2,1)S(1)}, u32[]{:S(2)}, u32[]{:S(2)}) collective-permute-start(bf16[192,512]{1,0:T(8,128)(2,1)S(1)} %get-tuple-element.65), channel_id=1, source_target_pairs={{0,192},{64,0},{128,64},{192,128},{1,193},{65,1},{129,65},{193,129... | collective-permute-start | bytes 589832 | tf_op jit(solution)/shard_map/ppermute | solution.py:205
  136.4 7.5 %collective-permute-done.22 = bf16[192,512]{1,0:T(8,128)(2,1)S(1)} collective-permute-done((bf16[192,512]{1,0:T(8,128)(2,1)S(1)}, bf16[192,512]{1,0:T(8,128)(2,1)S(1)}, u32[]{:S(2)}, u32[]{:S(2)}) %collective-permute-start.22) | collective-permute-done | bytes 196640 | tf_op jit(solution)/shard_map/ppermute | solution.py:205
  144.7 2.8 %collective-permute-done.24 = bf16[192,512]{1,0:T(8,128)(2,1)S(1)} collective-permute-done((bf16[192,512]{1,0:T(8,128)(2,1)S(1)}, bf16[192,512]{1,0:T(8,128)(2,1)S(1)}, u32[]{:S(2)}, u32[]{:S(2)}) %collective-permute-start.24) | collective-permute-done | bytes 196640 | tf_op jit(solution)/shard_map/ppermute | solution.py:207
  152.8 2.0 %collective-permute-start.28 = (bf16[64,1024]{1,0:T(8,128)(2,1)S(1)}, bf16[64,1024]{1,0:T(8,128)(2,1)S(1)}, u32[]{:S(2)}, u32[]{:S(2)}) collective-permute-start(bf16[64,1024]{1,0:T(8,128)(2,1)S(1)} %get-tuple-element.73), channel_id=1, source_target_pairs={{0,48},{16,0},{32,16},{48,32},{1,49},{17,1},{33,17},{49,33},{2,50}... | collective-permute-start | bytes 393224 | tf_op jit(solution)/shard_map/ppermute | solution.py:54
  155.8 2.9 %collective-permute-done.26 = bf16[64,1024]{1,0:T(8,128)(2,1)S(1)} collective-permute-done((bf16[64,1024]{1,0:T(8,128)(2,1)}, bf16[64,1024]{1,0:T(8,128)(2,1)S(1)}, u32[]{:S(2)}, u32[]{:S(2)}) %collective-permute-start.26) | collective-permute-done | bytes 131104 | tf_op jit(solution)/shard_map/ppermute | solution.py:53
  164.3 5.2 %collective-permute-done.27 = bf16[128,1024]{1,0:T(8,128)(2,1)S(1)} collective-permute-done((bf16[128,1024]{1,0:T(8,128)(2,1)}, bf16[128,1024]{1,0:T(8,128)(2,1)S(1)}, u32[]{:S(2)}, u32[]{:S(2)}) %collective-permute-start.27) | collective-permute-done | bytes 262176 | tf_op jit(solution)/shard_map/ppermute | solution.py:58
  169.5 2.5 %collective-permute-done.29 = bf16[128,1024]{1,0:T(8,128)(2,1)} collective-permute-done((bf16[128,1024]{1,0:T(8,128)(2,1)}, bf16[128,1024]{1,0:T(8,128)(2,1)}, u32[]{:S(2)}, u32[]{:S(2)}) %collective-permute-start.29) | collective-permute-done | bytes 262176 | tf_op jit(solution)/shard_map/ppermute | solution.py:59
  172.0 1.9 %add_convert_fusion = bf16[128,1024]{1,0:T(8,128)(2,1)} fusion(bf16[128,1024]{1,0:T(8,128)(2,1)} %collective-permute-done.29, bf16[128,1024]{1,0:T(8,128)(2,1)S(1)} %collective-permute-done.27, f32[512,1024]{1,0:T(8,128)} %copy-done.10, s32[]{:T(128)S(6)} %select_n.66), kind=kLoop, calls=%fused_computation.23 | loop fusion | flops 655360 | bytes 1310724 | tf_op jit(solution)/shard_map/convert_element_type | solution.py:133
  173.9 6.0 %all-to-all-start.2 = ((bf16[8,16,1024]{2,1,0:T(8,128)(2,1)}), bf16[8,16,1024]{2,1,0:T(8,128)(2,1)S(1)}, u32[]{:S(2)}, u32[]{:S(2)}) async-start(bf16[8,16,1024]{2,1,0:T(8,128)(2,1)} %bitcast.6), calls=%async_computation.2 | async-start | bytes 524288 | tf_op jit(solution)/shard_map/all_to_all | solution.py:134
  179.9 4.9 %convolution_convert_fusion = bf16[384,1024]{1,0:T(8,128)(2,1)} fusion(bf16[384,2048]{1,0:T(8,128)(2,1)S(1)} %copy-done.12, bf16[2048,1024]{1,0:T(8,128)(2,1)} %bitcast.18), kind=kOutput, calls=%fused_computation.9 | convolution fusion | flops 1611005952 | bytes 6553600 | tf_op jit(solution)/shard_map/dot_general | solution.py:228
  184.8 5.8 %all-to-all-done.2 = bf16[8,16,1024]{2,1,0:T(8,128)(2,1)S(1)} async-done(((bf16[8,16,1024]{2,1,0:T(8,128)(2,1)}), bf16[8,16,1024]{2,1,0:T(8,128)(2,1)S(1)}, u32[]{:S(2)}, u32[]{:S(2)}) %all-to-all-start.2) | async-done | bytes 262176 | tf_op jit(solution)/shard_map/all_to_all | solution.py:134
  (138 shorter events, 42.6 us)
Async XLA Ops:
  0.6 23.8 %collective-permute-start = (bf16[384,1024]{1,0:T(8,128)(2,1)}, bf16[384,1024]{1,0:T(8,128)(2,1)}, u32[]{:S(2)}, u32[]{:S(2)}) collective-permute-start(bf16[384,1024]{1,0:T(8,128)(2,1)} %refs_0_.1), channel_id=1, source_target_pairs={{0,64},{64,128},{128,192},{192,0},{1,65},{65,129},{129,193},{193,1... | collective-permute-start | bytes 2359304 | tf_op jit(solution)/shard_map/ppermute | solution.py:152
  2.2 22.2 %collective-permute-start.1 = (bf16[384,1024]{1,0:T(8,128)(2,1)}, bf16[384,1024]{1,0:T(8,128)(2,1)}, u32[]{:S(2)}, u32[]{:S(2)}) collective-permute-start(bf16[384,1024]{1,0:T(8,128)(2,1)} %refs_0_.1), channel_id=1, source_target_pairs={{0,192},{64,0},{128,64},{192,128},{1,193},{65,1},{129,65},{193,129... | collective-permute-start | bytes 2359304 | tf_op jit(solution)/shard_map/ppermute | solution.py:153
  25.1 20.8 %collective-permute-start.9 = (bf16[128,512]{1,0:T(8,128)(2,1)}, bf16[128,512]{1,0:T(8,128)(2,1)S(1)}, u32[]{:S(2)}, u32[]{:S(2)}) collective-permute-start(bf16[128,512]{1,0:T(8,128)(2,1)} %get-tuple-element.74), channel_id=1, source_target_pairs={{0,64},{64,128},{128,192},{192,0},{1,65},{65,129},{129,193},{193,1... | collective-permute-start | bytes 393224 | tf_op jit(solution)/shard_map/ppermute | solution.py:30
  25.4 22.3 %collective-permute-start.8 = (bf16[128,512]{1,0:T(8,128)(2,1)}, bf16[128,512]{1,0:T(8,128)(2,1)S(1)}, u32[]{:S(2)}, u32[]{:S(2)}) collective-permute-start(bf16[128,512]{1,0:T(8,128)(2,1)} %get-tuple-element.74), channel_id=1, source_target_pairs={{0,192},{64,0},{128,64},{192,128},{1,193},{65,1},{129,65},{193,129... | collective-permute-start | bytes 393224 | tf_op jit(solution)/shard_map/ppermute | solution.py:31
  28.4 21.0 %collective-permute-start.3 = (bf16[128,512]{1,0:T(8,128)(2,1)S(1)}, bf16[128,512]{1,0:T(8,128)(2,1)S(1)}, u32[]{:S(2)}, u32[]{:S(2)}) collective-permute-start(bf16[128,512]{1,0:T(8,128)(2,1)S(1)} %get-tuple-element.77), channel_id=1, source_target_pairs={{0,16},{16,32},{32,48},{48,0},{1,17},{17,33},{33,49},{49,1},{2,18}... | collective-permute-start | bytes 393224 | tf_op jit(solution)/shard_map/ppermute | solution.py:30
  28.6 21.2 %collective-permute-start.2 = (bf16[128,512]{1,0:T(8,128)(2,1)S(1)}, bf16[128,512]{1,0:T(8,128)(2,1)S(1)}, u32[]{:S(2)}, u32[]{:S(2)}) collective-permute-start(bf16[128,512]{1,0:T(8,128)(2,1)S(1)} %get-tuple-element.77), channel_id=1, source_target_pairs={{0,48},{16,0},{32,16},{48,32},{1,49},{17,1},{33,17},{49,33},{2,50}... | collective-permute-start | bytes 393224 | tf_op jit(solution)/shard_map/ppermute | solution.py:31
  31.7 67.9 %all-to-all-start.1 = ((bf16[128,3,1024]{2,1,0:T(4,128)(2,1)}), bf16[128,3,1024]{2,1,0:T(4,128)(2,1)}, u32[]{:S(2)}, u32[]{:S(2)}) async-start(bf16[128,3,1024]{2,1,0:T(4,128)(2,1)} %all_to_all.15), calls=%async_computation.1 | async-start | bytes 2097152 | tf_op jit(solution)/shard_map/all_to_all | solution.py:150
  44.2 28.7 %collective-permute-start.14 = (bf16[192,1024]{1,0:T(8,128)(2,1)S(1)}, bf16[192,1024]{1,0:T(8,128)(2,1)S(1)}, u32[]{:S(2)}, u32[]{:S(2)}) collective-permute-start(bf16[192,1024]{1,0:T(8,128)(2,1)S(1)} %slice.62), channel_id=1, source_target_pairs={{0,64},{64,128},{128,192},{192,0},{1,65},{65,129},{129,193},{193,1... | collective-permute-start | bytes 1179656 | tf_op jit(solution)/shard_map/ppermute | solution.py:158
  45.9 17.9 %collective-permute-start.10 = (bf16[64,512]{1,0:T(8,128)(2,1)S(1)}, bf16[64,512]{1,0:T(8,128)(2,1)S(1)}, u32[]{:S(2)}, u32[]{:S(2)}) collective-permute-start(bf16[64,512]{1,0:T(8,128)(2,1)S(1)} %slice.78), channel_id=1, source_target_pairs={{0,64},{64,128},{128,192},{192,0},{1,65},{65,129},{129,193},{193,1... | collective-permute-start | bytes 196616 | tf_op jit(solution)/shard_map/ppermute | solution.py:32
  47.7 16.8 %collective-permute-start.11 = (bf16[64,512]{1,0:T(8,128)(2,1)S(1)}, bf16[64,512]{1,0:T(8,128)(2,1)S(1)}, u32[]{:S(2)}, u32[]{:S(2)}) collective-permute-start(bf16[64,512]{1,0:T(8,128)(2,1)S(1)} %slice.79), channel_id=1, source_target_pairs={{0,192},{64,0},{128,64},{192,128},{1,193},{65,1},{129,65},{193,129... | collective-permute-start | bytes 196616 | tf_op jit(solution)/shard_map/ppermute | solution.py:33
  49.4 18.4 %collective-permute-start.4 = (bf16[64,512]{1,0:T(8,128)(2,1)S(1)}, bf16[64,512]{1,0:T(8,128)(2,1)S(1)}, u32[]{:S(2)}, u32[]{:S(2)}) collective-permute-start(bf16[64,512]{1,0:T(8,128)(2,1)S(1)} %slice.76), channel_id=1, source_target_pairs={{0,16},{16,32},{32,48},{48,0},{1,17},{17,33},{33,49},{49,1},{2,18}... | collective-permute-start | bytes 196616 | tf_op jit(solution)/shard_map/ppermute | solution.py:32
  49.8 17.9 %collective-permute-start.5 = (bf16[64,512]{1,0:T(8,128)(2,1)S(1)}, bf16[64,512]{1,0:T(8,128)(2,1)S(1)}, u32[]{:S(2)}, u32[]{:S(2)}) collective-permute-start(bf16[64,512]{1,0:T(8,128)(2,1)S(1)} %slice.77), channel_id=1, source_target_pairs={{0,48},{16,0},{32,16},{48,32},{1,49},{17,1},{33,17},{49,33},{2,50}... | collective-permute-start | bytes 196616 | tf_op jit(solution)/shard_map/ppermute | solution.py:33
  65.7 22.6 %collective-permute-start.12 = (bf16[4,128,512]{2,1,0:T(8,128)(2,1)}, bf16[4,128,512]{2,1,0:T(8,128)(2,1)S(1)}, u32[]{:S(2)}, u32[]{:S(2)}) collective-permute-start(bf16[4,128,512]{2,1,0:T(8,128)(2,1)} %bitcast.3.refs_6_), channel_id=1, source_target_pairs={{0,16},{16,32},{32,48},{48,0},{1,17},{17,33},{33,49},{49,1},{2,18}... | collective-permute-start | bytes 1572872 | tf_op jit(solution)/shard_map/ppermute | solution.py:165
  67.0 21.4 %collective-permute-start.13 = (bf16[4,128,512]{2,1,0:T(8,128)(2,1)}, bf16[4,128,512]{2,1,0:T(8,128)(2,1)S(1)}, u32[]{:S(2)}, u32[]{:S(2)}) collective-permute-start(bf16[4,128,512]{2,1,0:T(8,128)(2,1)} %bitcast.3.refs_6_), channel_id=1, source_target_pairs={{0,48},{16,0},{32,16},{48,32},{1,49},{17,1},{33,17},{49,33},{2,50}... | collective-permute-start | bytes 1572872 | tf_op jit(solution)/shard_map/ppermute | solution.py:166
  68.6 19.7 %collective-permute-start.6 = (bf16[4,128,512]{2,1,0:T(8,128)(2,1)}, bf16[4,128,512]{2,1,0:T(8,128)(2,1)S(1)}, u32[]{:S(2)}, u32[]{:S(2)}) collective-permute-start(bf16[4,128,512]{2,1,0:T(8,128)(2,1)} %bitcast.15), channel_id=1, source_target_pairs={{0,64},{64,128},{128,192},{192,0},{1,65},{65,129},{129,193},{193,1... | collective-permute-start | bytes 1572872 | tf_op jit(solution)/shard_map/ppermute | solution.py:163
  68.9 20.2 %collective-permute-start.7 = (bf16[4,128,512]{2,1,0:T(8,128)(2,1)}, bf16[4,128,512]{2,1,0:T(8,128)(2,1)S(1)}, u32[]{:S(2)}, u32[]{:S(2)}) collective-permute-start(bf16[4,128,512]{2,1,0:T(8,128)(2,1)} %bitcast.16), channel_id=1, source_target_pairs={{0,192},{64,0},{128,64},{192,128},{1,193},{65,1},{129,65},{193,129... | collective-permute-start | bytes 1572872 | tf_op jit(solution)/shard_map/ppermute | solution.py:164
  72.9 15.4 %collective-permute-start.15 = (bf16[192,1024]{1,0:T(8,128)(2,1)S(1)}, bf16[192,1024]{1,0:T(8,128)(2,1)S(1)}, u32[]{:S(2)}, u32[]{:S(2)}) collective-permute-start(bf16[192,1024]{1,0:T(8,128)(2,1)S(1)} %slice.63), channel_id=1, source_target_pairs={{0,192},{64,0},{128,64},{192,128},{1,193},{65,1},{129,65},{193,129... | collective-permute-start | bytes 1179656 | tf_op jit(solution)/shard_map/ppermute | solution.py:159
  90.7 12.0 %collective-permute-start.16 = (bf16[2,128,512]{2,1,0:T(8,128)(2,1)}, bf16[2,128,512]{2,1,0:T(8,128)(2,1)}, u32[]{:S(2)}, u32[]{:S(2)}) collective-permute-start(bf16[2,128,512]{2,1,0:T(8,128)(2,1)} %slice.64), channel_id=1, source_target_pairs={{0,64},{64,128},{128,192},{192,0},{1,65},{65,129},{129,193},{193,1... | collective-permute-start | bytes 786440 | tf_op jit(solution)/shard_map/ppermute | solution.py:170
  92.4 10.3 %collective-permute-start.17 = (bf16[2,128,512]{2,1,0:T(8,128)(2,1)}, bf16[2,128,512]{2,1,0:T(8,128)(2,1)}, u32[]{:S(2)}, u32[]{:S(2)}) collective-permute-start(bf16[2,128,512]{2,1,0:T(8,128)(2,1)} %slice.65), channel_id=1, source_target_pairs={{0,192},{64,0},{128,64},{192,128},{1,193},{65,1},{129,65},{193,129... | collective-permute-start | bytes 786440 | tf_op jit(solution)/shard_map/ppermute | solution.py:171
  95.9 7.2 %collective-permute-start.18 = (bf16[2,128,512]{2,1,0:T(8,128)(2,1)}, bf16[2,128,512]{2,1,0:T(8,128)(2,1)}, u32[]{:S(2)}, u32[]{:S(2)}) collective-permute-start(bf16[2,128,512]{2,1,0:T(8,128)(2,1)} %slice.66), channel_id=1, source_target_pairs={{0,16},{16,32},{32,48},{48,0},{1,17},{17,33},{33,49},{49,1},{2,18}... | collective-permute-start | bytes 786440 | tf_op jit(solution)/shard_map/ppermute | solution.py:172
  99.5 7.9 %collective-permute-start.19 = (bf16[2,128,512]{2,1,0:T(8,128)(2,1)}, bf16[2,128,512]{2,1,0:T(8,128)(2,1)}, u32[]{:S(2)}, u32[]{:S(2)}) collective-permute-start(bf16[2,128,512]{2,1,0:T(8,128)(2,1)} %slice.67), channel_id=1, source_target_pairs={{0,48},{16,0},{32,16},{48,32},{1,49},{17,1},{33,17},{49,33},{2,50}... | collective-permute-start | bytes 786440 | tf_op jit(solution)/shard_map/ppermute | solution.py:173
  118.1 8.0 %collective-permute-start.20 = (f32[384,2048]{1,0:T(8,128)}, f32[384,2048]{1,0:T(8,128)}, u32[]{:S(2)}, u32[]{:S(2)}) collective-permute-start(f32[384,2048]{1,0:T(8,128)} %get-tuple-element.48), channel_id=1, source_target_pairs={{0,1},{1,0},{2,3},{3,2},{4,5},{5,4},{6,7},{7,6},{8,9},{9,8},{10,11... | collective-permute-start | bytes 9437192 | tf_op jit(solution)/shard_map/ppermute | solution.py:188
  125.4 4.8 %collective-permute-start.21 = (bf16[384,1024]{1,0:T(8,128)(2,1)S(1)}, bf16[384,1024]{1,0:T(8,128)(2,1)S(1)}, u32[]{:S(2)}, u32[]{:S(2)}) collective-permute-start(bf16[384,1024]{1,0:T(8,128)(2,1)S(1)} %broadcast_select_fusion), channel_id=1, source_target_pairs={{0,1},{1,0},{2,3},{3,2},{4,5},{5,4},{6,7},{7,6},{8,9},{9,8},{10,11... | collective-permute-start | bytes 2359304 | tf_op jit(solution)/shard_map/ppermute | solution.py:182
  133.1 10.7 %collective-permute-start.22 = (bf16[192,512]{1,0:T(8,128)(2,1)S(1)}, bf16[192,512]{1,0:T(8,128)(2,1)S(1)}, u32[]{:S(2)}, u32[]{:S(2)}) collective-permute-start(bf16[192,512]{1,0:T(8,128)(2,1)S(1)} %get-tuple-element.65), channel_id=1, source_target_pairs={{0,192},{64,0},{128,64},{192,128},{1,193},{65,1},{129,65},{193,129... | collective-permute-start | bytes 589832 | tf_op jit(solution)/shard_map/ppermute | solution.py:205
  135.3 9.4 %collective-permute-start.23 = (bf16[192,512]{1,0:T(8,128)(2,1)S(1)}, bf16[192,512]{1,0:T(8,128)(2,1)S(1)}, u32[]{:S(2)}, u32[]{:S(2)}) collective-permute-start(bf16[192,512]{1,0:T(8,128)(2,1)S(1)} %get-tuple-element.64), channel_id=1, source_target_pairs={{0,128},{64,192},{128,0},{192,64},{1,129},{65,193},{129,1},{193,65... | collective-permute-start | bytes 589832 | tf_op jit(solution)/shard_map/ppermute | solution.py:206
  135.4 12.1 %collective-permute-start.24 = (bf16[192,512]{1,0:T(8,128)(2,1)S(1)}, bf16[192,512]{1,0:T(8,128)(2,1)S(1)}, u32[]{:S(2)}, u32[]{:S(2)}) collective-permute-start(bf16[192,512]{1,0:T(8,128)(2,1)S(1)} %get-tuple-element.63), channel_id=1, source_target_pairs={{0,64},{64,128},{128,192},{192,0},{1,65},{65,129},{129,193},{193,1... | collective-permute-start | bytes 589832 | tf_op jit(solution)/shard_map/ppermute | solution.py:207
  147.6 2.1 %collective-permute-start.25 = (bf16[576,512]{1,0:T(8,128)(2,1)S(1)}, bf16[576,512]{1,0:T(8,128)(2,1)S(1)}, u32[]{:S(2)}, u32[]{:S(2)}) collective-permute-start(bf16[576,512]{1,0:T(8,128)(2,1)S(1)} %constant_dynamic-update-slice_fusion.10), channel_id=1, source_target_pairs={{0,1},{1,0},{2,3},{3,2},{4,5},{5,4},{6,7},{7,6},{8,9},{9,8},{10,11... | collective-permute-start | bytes 1769480 | tf_op jit(solution)/shard_map/ppermute | solution.py:209
  152.8 6.0 %collective-permute-start.26 = (bf16[64,1024]{1,0:T(8,128)(2,1)}, bf16[64,1024]{1,0:T(8,128)(2,1)S(1)}, u32[]{:S(2)}, u32[]{:S(2)}) collective-permute-start(bf16[64,1024]{1,0:T(8,128)(2,1)} %get-tuple-element.72), channel_id=1, source_target_pairs={{0,16},{16,32},{32,48},{48,0},{1,17},{17,33},{33,49},{49,1},{2,18}... | collective-permute-start | bytes 393224 | tf_op jit(solution)/shard_map/ppermute | solution.py:53
  152.8 7.0 %collective-permute-start.28 = (bf16[64,1024]{1,0:T(8,128)(2,1)S(1)}, bf16[64,1024]{1,0:T(8,128)(2,1)S(1)}, u32[]{:S(2)}, u32[]{:S(2)}) collective-permute-start(bf16[64,1024]{1,0:T(8,128)(2,1)S(1)} %get-tuple-element.73), channel_id=1, source_target_pairs={{0,48},{16,0},{32,16},{48,32},{1,49},{17,1},{33,17},{49,33},{2,50}... | collective-permute-start | bytes 393224 | tf_op jit(solution)/shard_map/ppermute | solution.py:54
  161.5 8.0 %collective-permute-start.27 = (bf16[128,1024]{1,0:T(8,128)(2,1)}, bf16[128,1024]{1,0:T(8,128)(2,1)S(1)}, u32[]{:S(2)}, u32[]{:S(2)}) collective-permute-start(bf16[128,1024]{1,0:T(8,128)(2,1)} %pad_maximum_fusion), channel_id=1, source_target_pairs={{0,16},{16,32},{32,48},{48,0},{1,17},{17,33},{33,49},{49,1},{2,18}... | collective-permute-start | bytes 786440 | tf_op jit(solution)/shard_map/ppermute | solution.py:58
  162.7 9.2 %collective-permute-start.29 = (bf16[128,1024]{1,0:T(8,128)(2,1)}, bf16[128,1024]{1,0:T(8,128)(2,1)}, u32[]{:S(2)}, u32[]{:S(2)}) collective-permute-start(bf16[128,1024]{1,0:T(8,128)(2,1)} %pad_maximum_fusion.1), channel_id=1, source_target_pairs={{0,48},{16,0},{32,16},{48,32},{1,49},{17,1},{33,17},{49,33},{2,50}... | collective-permute-start | bytes 786440 | tf_op jit(solution)/shard_map/ppermute | solution.py:59
  173.9 16.6 %all-to-all-start.2 = ((bf16[8,16,1024]{2,1,0:T(8,128)(2,1)}), bf16[8,16,1024]{2,1,0:T(8,128)(2,1)S(1)}, u32[]{:S(2)}, u32[]{:S(2)}) async-start(bf16[8,16,1024]{2,1,0:T(8,128)(2,1)} %bitcast.6), calls=%async_computation.2 | async-start | bytes 524288 | tf_op jit(solution)/shard_map/all_to_all | solution.py:134
  (24 other events, 155.9 us)

commit v10 on v6

--- a/solution.py
+++ b/solution.py
@@ -35,42 +35,10 @@
 
 
 def ring_reduce(chunk_of, axis):
-    far = chunk_of(2).astype(BF16)
-    mid = far.shape[0] // 2
-    top = lax.ppermute(far[:mid], axis, RIGHT)
-    bottom = lax.ppermute(far[mid:], axis, LEFT)
-    ahead, behind = chunk_of(1), chunk_of(3)
-    ahead = jnp.concatenate([ahead[:mid] + top.astype(F32), ahead[mid:]]).astype(BF16)
-    behind = jnp.concatenate([behind[:mid], behind[mid:] + bottom.astype(F32)]).astype(BF16)
-    from_before = lax.ppermute(ahead, axis, RIGHT)
-    from_after = lax.ppermute(behind, axis, LEFT)
-    return chunk_of(0) + from_before.astype(F32) + from_after.astype(F32)
-
-
-def ring_reduce(chunk_of, axis):
-    far = chunk_of(2).astype(BF16)
-    mid = far.shape[0] // 2
-    top = lax.ppermute(far[:mid], axis, RIGHT)
-    bottom = lax.ppermute(far[mid:], axis, LEFT)
-    ahead, behind = chunk_of(1), chunk_of(3)
-    ahead = jnp.concatenate([ahead[:mid] + top.astype(F32), ahead[mid:]]).astype(BF16)
-    behind = jnp.concatenate([behind[:mid], behind[mid:] + bottom.astype(F32)]).astype(BF16)
-    from_before = lax.ppermute(ahead, axis, RIGHT)
-    from_after = lax.ppermute(behind, axis, LEFT)
-    return chunk_of(0) + from_before.astype(F32) + from_after.astype(F32)
-
-
-def ring_columns(columns_of, axis):
-    far = columns_of(2)
-    rows = far.shape[0]
-    mid = rows // 2
-    right = jnp.concatenate([columns_of(1), far[:mid]])
-    left = jnp.concatenate([columns_of(3), far[mid:]])
-    before = lax.ppermute(right, axis, RIGHT)
-    after = lax.ppermute(left, axis, LEFT)
-    top = lax.ppermute(before[rows:], axis, RIGHT)
-    bottom = lax.ppermute(after[rows:], axis, LEFT)
-    return columns_of(0), after[:rows], top, bottom, before[:rows]
+    far = lax.ppermute(chunk_of(2).astype(BF16), axis, ACROSS)
+    from_before = lax.ppermute(chunk_of(1).astype(BF16), axis, RIGHT)
+    from_after = lax.ppermute(chunk_of(3).astype(BF16), axis, LEFT)
+    return chunk_of(0) + from_before.astype(F32) + far.astype(F32) + from_after.astype(F32)
 
 
 def project_kernel(*refs):

time: 173 us -> 171 us (0.988)
  waiting for transfers between devices: 53.6 us -> 56.9 us
  other arithmetic: 13.2 us -> 10.6 us
  local copies, waits for them, and re-layouts: 24.2 us -> 22.4 us
  starting transfers between devices: 46.3 us -> 44.5 us
    ppermute x4 -> x3, waiting for transfers between devices: 11.6 us -> 13.8 us  [the longest x1 7.09 us: ring_reduce(): from_before = lax.ppermute(chunk_of(1).astype(BF16), axis, RIGHT)]
    ppermute x4 -> x3, starting transfers between devices: 4.05 us -> 2.11 us  [the longest x1 1.86 us: ring_reduce(): far = lax.ppermute(chunk_of(2).astype(BF16), axis, ACROSS)]
    unnamed x47 -> x45, local copies, waits for them, and re-layouts: 7.39 us -> 7.24 us
  transfers between devices with their start and end apart: 24 -> 23, of which waited for: 15 -> 15; matrix products, arithmetic and copies ran while one was open for 15% -> 14% of each run, Pallas kernels for 0% -> 0%
where the time goes in v10:
time: 171 us; the launch traced here: 170 us
  waiting for transfers between devices  56.9 us (33%)
  starting transfers between devices  44.5 us (26%)
  local copies, waits for them, and re-layouts  22.4 us (13%)
  blocking collectives  19.6 us (11%)
  other arithmetic  10.6 us (6%)
  matrix products  8.08 us (5%)
  Pallas kernels  5.93 us (3%)
  between operations  1.75 us (1%)
    all_to_all x1, blocking collectives, spread(): return lax.all_to_all(whole, axis, split_axis=0, concat_axis=0)  19.6 us
    all_to_all x1, starting transfers between devices, shards(): lax.all_to_all(mine, ('x', 'y', 'z'), split_axis=0, concat_axis=0, tiled=...  13.9 us
    ppermute x1, waiting for transfers between devices, shards(): context_top = lax.ppermute(context_before[:mid], 'x', RIGHT)  10.8 us
    ppermute x1, waiting for transfers between devices, shards(): lax.ppermute(half_of(3), 'x', LEFT)  7.58 us
    unnamed x45, local copies, waits for them, and re-layouts  7.24 us
    ppermute x1, waiting for transfers between devices, ring_reduce(): from_before = lax.ppermute(chunk_of(1).astype(BF16), axis, RIGHT)  7.09 us
    all_to_all x1, waiting for transfers between devices, collect(): got = lax.all_to_all(share, axis, split_axis=0, concat_axis=0)  6.72 us
    pallas_call x1, Pallas kernels, project(): pl.pallas_call(project_kernel, out_shape=(jax.ShapeDtypeStruct((4, 4, 128...  5.93 us
  transfers between devices with their start and end apart: 23, of which 15 were waited for; matrix products, arithmetic and copies ran while one was open for 14% of the time, Pallas kernels for 0%

profile of v10, /device:TPU:24, one launch (start us, length us, event | category | flops | bytes accessed | tf_op | source)
XLA Modules:
  0.0 169.7 jit_solution(11224767562330060453)
XLA Ops:
  2.2 1.7 %collective-permute-start.1 = (bf16[384,1024]{1,0:T(8,128)(2,1)}, bf16[384,1024]{1,0:T(8,128)(2,1)}, u32[]{:S(2)}, u32[]{:S(2)}) collective-permute-start(bf16[384,1024]{1,0:T(8,128)(2,1)} %refs_0_.1), channel_id=1, source_target_pairs={{0,192},{64,0},{128,64},{192,128},{1,193},{65,1},{129,65},{193,129... | collective-permute-start | bytes 2359304 | tf_op jit(solution)/shard_map/ppermute | solution.py:118
  4.8 19.6 %all_to_all.22 = bf16[8,16,1024]{2,1,0:T(8,128)(2,1)S(1)} all-to-all(bf16[8,16,1024]{2,1,0:T(8,128)(2,1)S(1)} %broadcast_in_dim.16), channel_id=1, replica_groups=mesh['x'=4,'y'=4,'z'=8,'core'=2] {'z'}, dimensions={0} | all-to-all | bytes 524288 | tf_op jit(solution)/shard_map/all_to_all | solution.py:93
  24.8 3.0 %collective-permute-start.2 = (bf16[128,1024]{1,0:T(8,128)(2,1)S(1)}, bf16[128,1024]{1,0:T(8,128)(2,1)S(1)}, u32[]{:S(2)}, u32[]{:S(2)}) collective-permute-start(bf16[128,1024]{1,0:T(8,128)(2,1)S(1)} %bitcast.16), channel_id=1, source_target_pairs={{0,192},{64,0},{128,64},{192,128},{1,193},{65,1},{129,65},{193,129... | collective-permute-start | bytes 786440 | tf_op jit(solution)/shard_map/ppermute | solution.py:31
  27.7 4.3 %collective-permute-done.3 = bf16[128,1024]{1,0:T(8,128)(2,1)S(1)} collective-permute-done((bf16[128,1024]{1,0:T(8,128)(2,1)S(1)}, bf16[128,1024]{1,0:T(8,128)(2,1)S(1)}, u32[]{:S(2)}, u32[]{:S(2)}) %collective-permute-start.3) | collective-permute-done | bytes 262176 | tf_op jit(solution)/shard_map/ppermute | solution.py:30
  32.9 3.3 %collective-permute-start.5 = (bf16[64,1024]{1,0:T(8,128)(2,1)S(1)}, bf16[64,1024]{1,0:T(8,128)(2,1)S(1)}, u32[]{:S(2)}, u32[]{:S(2)}) collective-permute-start(bf16[64,1024]{1,0:T(8,128)(2,1)S(1)} %slice.27), channel_id=1, source_target_pairs={{0,192},{64,0},{128,64},{192,128},{1,193},{65,1},{129,65},{193,129... | collective-permute-start | bytes 393224 | tf_op jit(solution)/shard_map/ppermute | solution.py:33
  40.6 1.8 %collective-permute-start.7 = (bf16[4,128,1024]{2,1,0:T(8,128)(2,1)}, bf16[4,128,1024]{2,1,0:T(8,128)(2,1)}, u32[]{:S(2)}, u32[]{:S(2)}) collective-permute-start(bf16[4,128,1024]{2,1,0:T(8,128)(2,1)} %bitcast.2.refs_1_), channel_id=1, source_target_pairs={{0,48},{16,0},{32,16},{48,32},{1,49},{17,1},{33,17},{49,33},{2,50}... | collective-permute-start | bytes 3145736 | tf_op jit(solution)/shard_map/ppermute | solution.py:128
  43.7 13.9 %all-to-all-start.1 = ((bf16[128,3,1024]{2,1,0:T(4,128)(2,1)}), bf16[128,3,1024]{2,1,0:T(4,128)(2,1)}, u32[]{:S(2)}, u32[]{:S(2)}) async-start(bf16[128,3,1024]{2,1,0:T(4,128)(2,1)} %all_to_all.15), calls=%async_computation.1 | async-start | bytes 2097152 | tf_op jit(solution)/shard_map/all_to_all | solution.py:115
  57.6 1.8 %collective-permute-start.8 = (bf16[192,1024]{1,0:T(8,128)(2,1)S(1)}, bf16[192,1024]{1,0:T(8,128)(2,1)S(1)}, u32[]{:S(2)}, u32[]{:S(2)}) collective-permute-start(bf16[192,1024]{1,0:T(8,128)(2,1)S(1)} %slice.20), channel_id=1, source_target_pairs={{0,64},{64,128},{128,192},{192,0},{1,65},{65,129},{129,193},{193,1... | collective-permute-start | bytes 1179656 | tf_op jit(solution)/shard_map/ppermute | solution.py:123
  60.4 1.8 %collective-permute-start.9 = (bf16[192,1024]{1,0:T(8,128)(2,1)S(1)}, bf16[192,1024]{1,0:T(8,128)(2,1)S(1)}, u32[]{:S(2)}, u32[]{:S(2)}) collective-permute-start(bf16[192,1024]{1,0:T(8,128)(2,1)S(1)} %slice.21), channel_id=1, source_target_pairs={{0,192},{64,0},{128,64},{192,128},{1,193},{65,1},{129,65},{193,129... | collective-permute-start | bytes 1179656 | tf_op jit(solution)/shard_map/ppermute | solution.py:124
  62.2 10.8 %collective-permute-done.8 = bf16[192,1024]{1,0:T(8,128)(2,1)S(1)} collective-permute-done((bf16[192,1024]{1,0:T(8,128)(2,1)S(1)}, bf16[192,1024]{1,0:T(8,128)(2,1)S(1)}, u32[]{:S(2)}, u32[]{:S(2)}) %collective-permute-start.8) | collective-permute-done | bytes 393248 | tf_op jit(solution)/shard_map/ppermute | solution.py:123
  73.1 1.6 collective-permute-done.9
  76.8 1.9 %slice.23 = bf16[2,128,1024]{2,1,0:T(8,128)(2,1)} slice(bf16[4,128,1024]{2,1,0:T(8,128)(2,1)} %collective-permute-done.7.refs_2_), slice={[2:4], [0:128], [0:1024]} | slice | bytes 1048576 | tf_op jit(solution)/shard_map/slice | solution.py:131
  80.2 1.8 %all-to-all-done.1 = bf16[128,3,1024]{2,1,0:T(4,128)(2,1)} async-done(((bf16[128,3,1024]{2,1,0:T(4,128)(2,1)}), bf16[128,3,1024]{2,1,0:T(4,128)(2,1)}, u32[]{:S(2)}, u32[]{:S(2)}) %all-to-all-start.1) | async-done | bytes 786464 | tf_op jit(solution)/shard_map/all_to_all | solution.py:115
  82.0 3.2 %all_to_all.17 = bf16[384,1024]{1,0:T(8,128)(2,1)} reshape(bf16[128,3,1024]{2,1,0:T(4,128)(2,1)} %all-to-all-done.1) | data formatting | bytes 1572864 | tf_op jit(solution)/shard_map/all_to_all | solution.py:115
  85.2 3.2 %collective-permute-done.10.refs_3_ = bf16[2,128,1024]{2,1,0:T(8,128)(2,1)} collective-permute-done((bf16[2,128,1024]{2,1,0:T(8,128)(2,1)}, bf16[2,128,1024]{2,1,0:T(8,128)(2,1)}, u32[]{:S(2)}, u32[]{:S(2)}) %collective-permute-start.10) | collective-permute-done | bytes 524320 | tf_op jit(solution)/shard_map/ppermute | solution.py:130
  88.4 1.8 %collective-permute-done.11.refs_4_ = bf16[2,128,1024]{2,1,0:T(8,128)(2,1)} collective-permute-done((bf16[2,128,1024]{2,1,0:T(8,128)(2,1)}, bf16[2,128,1024]{2,1,0:T(8,128)(2,1)}, u32[]{:S(2)}, u32[]{:S(2)}) %collective-permute-start.11) | collective-permute-done | bytes 524320 | tf_op jit(solution)/shard_map/ppermute | solution.py:131
  90.2 5.9 %project.1 = (bf16[4,4,128,1024]{3,2,1,0:T(8,128)(2,1)S(1)}, f32[384,2048]{1,0:T(8,128)}) custom-call(bf16[384,1024]{1,0:T(8,128)(2,1)S(1)} %copy-done.1, bf16[4,128,1024]{2,1,0:T(8,128)(2,1)} %bitcast.2.refs_1_, bf16[4,128,1024]{2,1,0:T(8,128)(2,1)} %collective-permute-done.7.refs_2_, bf16[2,128,1024]{2,1,0:T(8,128)(2,1)} %collective-permute-done.10.refs_3_, ...), custom_call_target="tpu_custom_call" | custom-call | flops 1610612736 | bytes 16777216 | tf_op jit(solution)/shard_map/project/pallas_call | solution.py:70
  96.2 2.0 %copy-done.2 = bf16[4,4,128,1024]{3,2,1,0:T(8,128)(2,1)} copy-done((bf16[4,4,128,1024]{3,2,1,0:T(8,128)(2,1)}, bf16[4,4,128,1024]{3,2,1,0:T(8,128)(2,1)S(1)}, u32[]{:S(2)}) %copy-start.2) | copy-done | bytes 4194328
  98.9 2.4 %constant_dynamic-slice_fusion = (bf16[192,1024]{1,0:T(8,128)(2,1)S(1)}, bf16[192,1024]{1,0:T(8,128)(2,1)}, bf16[192,1024]{1,0:T(8,128)(2,1)}, bf16[192,1024]{1,0:T(8,128)(2,1)}) fusion(bf16[384,1024]{1,0:T(8,128)(2,1)} %copy-done.6, s32[]{:T(128)S(6)} %select_n.65, s32[]{:T(128)S(6)} %select_n.61, bf16[384,1024]{1,0:T(8,128)(2,1)} %collective-permute-done.1), kind=kLoop, calls=%fused_computation.42 | loop fusion | bytes 3145736 | tf_op jit(solution)/shard_map/dynamic_slice | solution.py:172
  101.3 2.7 %gather_fusion = bf16[384,1024]{1,0:T(8,128)(2,1)} fusion(bf16[384,1024]{1,0:T(8,128)(2,1)S(1)} %copy-done.3, s32[1024]{0:T(1024)S(1)} %pad_clamp_fusion), kind=kCustom, calls=%fused_computation | custom fusion | bytes 1574400 | tf_op jit(solution)/shard_map/gather | solution.py:137
  105.9 3.6 %fusion.17 = (f32[384]{0:T(512)S(1)}, f32[384,2048]{1,0:T(8,128)S(1)}) fusion(f32[2048]{0:T(1024)S(1)} %copy-done.17, f32[384,2048]{1,0:T(8,128)} %get-tuple-element.34, f32[384,2048]{1,0:T(8,128)} %collective-permute-done.12, bf16[384,2048]{1,0:T(8,128)(2,1)S(1)} %copy-done.9), kind=kLoop, calls=%fused_computation.57 | loop fusion | flops 3931776 | bytes 11019776 | tf_op jit(solution)/shard_map/reduce_sum | solution.py:17
  112.9 3.6 %collective-permute-start.14 = (bf16[192,512]{1,0:T(8,128)(2,1)S(1)}, bf16[192,512]{1,0:T(8,128)(2,1)S(1)}, u32[]{:S(2)}, u32[]{:S(2)}) collective-permute-start(bf16[192,512]{1,0:T(8,128)(2,1)S(1)} %get-tuple-element.50), channel_id=1, source_target_pairs={{0,192},{64,0},{128,64},{192,128},{1,193},{65,1},{129,65},{193,129... | collective-permute-start | bytes 589832 | tf_op jit(solution)/shard_map/ppermute | solution.py:162
  117.6 7.6 %collective-permute-done.14 = bf16[192,512]{1,0:T(8,128)(2,1)S(1)} collective-permute-done((bf16[192,512]{1,0:T(8,128)(2,1)S(1)}, bf16[192,512]{1,0:T(8,128)(2,1)S(1)}, u32[]{:S(2)}, u32[]{:S(2)}) %collective-permute-start.14) | collective-permute-done | bytes 196640 | tf_op jit(solution)/shard_map/ppermute | solution.py:162
  126.0 2.9 %collective-permute-done.16 = bf16[192,512]{1,0:T(8,128)(2,1)S(1)} collective-permute-done((bf16[192,512]{1,0:T(8,128)(2,1)S(1)}, bf16[192,512]{1,0:T(8,128)(2,1)S(1)}, u32[]{:S(2)}, u32[]{:S(2)}) %collective-permute-start.16) | collective-permute-done | bytes 196640 | tf_op jit(solution)/shard_map/ppermute | solution.py:164
  133.8 1.9 %collective-permute-start.19 = (bf16[128,1024]{1,0:T(8,128)(2,1)S(1)}, bf16[128,1024]{1,0:T(8,128)(2,1)S(1)}, u32[]{:S(2)}, u32[]{:S(2)}) collective-permute-start(bf16[128,1024]{1,0:T(8,128)(2,1)S(1)} %get-tuple-element.47), channel_id=1, source_target_pairs={{0,32},{16,48},{32,0},{48,16},{1,33},{17,49},{33,1},{49,17},{2,34}... | collective-permute-start | bytes 786440 | tf_op jit(solution)/shard_map/ppermute | solution.py:38
  135.9 7.1 %collective-permute-done.18 = bf16[128,1024]{1,0:T(8,128)(2,1)S(1)} collective-permute-done((bf16[128,1024]{1,0:T(8,128)(2,1)S(1)}, bf16[128,1024]{1,0:T(8,128)(2,1)S(1)}, u32[]{:S(2)}, u32[]{:S(2)}) %collective-permute-start.18) | collective-permute-done | bytes 262176 | tf_op jit(solution)/shard_map/ppermute | solution.py:39
  143.0 1.6 collective-permute-done.19
  144.6 5.0 %collective-permute-done.20 = bf16[128,1024]{1,0:T(8,128)(2,1)S(1)} collective-permute-done((bf16[128,1024]{1,0:T(8,128)(2,1)S(1)}, bf16[128,1024]{1,0:T(8,128)(2,1)S(1)}, u32[]{:S(2)}, u32[]{:S(2)}) %collective-permute-start.20) | collective-permute-done | bytes 262176 | tf_op jit(solution)/shard_map/ppermute | solution.py:40
  149.6 1.9 %add_convert_fusion = bf16[128,1024]{1,0:T(8,128)(2,1)} fusion(bf16[128,1024]{1,0:T(8,128)(2,1)S(1)} %collective-permute-done.20, bf16[128,1024]{1,0:T(8,128)(2,1)S(1)} %collective-permute-done.19, bf16[128,1024]{1,0:T(8,128)(2,1)S(1)} %collective-permute-done.18, f32[512,1024]{1,0:T(8,128)} %copy-done.4, s32[]{:T(128)S(6)} %select_n.66), kind=kLoop, calls=%fused_computation.23 | loop fusion | flops 917504 | bytes 1572868 | tf_op jit(solution)/shard_map/convert_element_type | solution.py:98
  151.5 5.5 %all-to-all-start.2 = ((bf16[8,16,1024]{2,1,0:T(8,128)(2,1)}), bf16[8,16,1024]{2,1,0:T(8,128)(2,1)S(1)}, u32[]{:S(2)}, u32[]{:S(2)}) async-start(bf16[8,16,1024]{2,1,0:T(8,128)(2,1)} %bitcast.5), calls=%async_computation.2 | async-start | bytes 524288 | tf_op jit(solution)/shard_map/all_to_all | solution.py:99
  157.0 5.3 %convolution_convert_fusion = bf16[384,1024]{1,0:T(8,128)(2,1)} fusion(bf16[384,2048]{1,0:T(8,128)(2,1)} %copy-done.5, bf16[2048,1024]{1,0:T(8,128)(2,1)} %bitcast.14), kind=kOutput, calls=%fused_computation.9 | convolution fusion | flops 1611005952 | bytes 6553600 | tf_op jit(solution)/shard_map/dot_general | solution.py:185
  162.3 6.7 %all-to-all-done.2 = bf16[8,16,1024]{2,1,0:T(8,128)(2,1)S(1)} async-done(((bf16[8,16,1024]{2,1,0:T(8,128)(2,1)}), bf16[8,16,1024]{2,1,0:T(8,128)(2,1)S(1)}, u32[]{:S(2)}, u32[]{:S(2)}) %all-to-all-start.2) | async-done | bytes 262176 | tf_op jit(solution)/shard_map/all_to_all | solution.py:99
  (97 shorter events, 26.8 us)
Async XLA Ops:
  0.6 3.3 %copy-start = (bf16[384,2048]{1,0:T(8,128)(2,1)S(1)}, bf16[384,2048]{1,0:T(8,128)(2,1)}, u32[]{:S(2)}) copy-start(bf16[384,2048]{1,0:T(8,128)(2,1)} %param.13) | copy-start | bytes 4718596
  0.6 23.8 %collective-permute-start = (bf16[384,1024]{1,0:T(8,128)(2,1)}, bf16[384,1024]{1,0:T(8,128)(2,1)S(1)}, u32[]{:S(2)}, u32[]{:S(2)}) collective-permute-start(bf16[384,1024]{1,0:T(8,128)(2,1)} %refs_0_.1), channel_id=1, source_target_pairs={{0,64},{64,128},{128,192},{192,0},{1,65},{65,129},{129,193},{193,1... | collective-permute-start | bytes 2359304 | tf_op jit(solution)/shard_map/ppermute | solution.py:117
  2.2 22.2 %collective-permute-start.1 = (bf16[384,1024]{1,0:T(8,128)(2,1)}, bf16[384,1024]{1,0:T(8,128)(2,1)}, u32[]{:S(2)}, u32[]{:S(2)}) collective-permute-start(bf16[384,1024]{1,0:T(8,128)(2,1)} %refs_0_.1), channel_id=1, source_target_pairs={{0,192},{64,0},{128,64},{192,128},{1,193},{65,1},{129,65},{193,129... | collective-permute-start | bytes 2359304 | tf_op jit(solution)/shard_map/ppermute | solution.py:118
  24.4 16.0 %copy-start.6 = (bf16[384,1024]{1,0:T(8,128)(2,1)}, bf16[384,1024]{1,0:T(8,128)(2,1)S(1)}, u32[]{:S(2)}) copy-start(bf16[384,1024]{1,0:T(8,128)(2,1)S(1)} %collective-permute-done) | copy-start | bytes 2359300
  24.4 7.7 %collective-permute-start.3 = (bf16[128,1024]{1,0:T(8,128)(2,1)S(1)}, bf16[128,1024]{1,0:T(8,128)(2,1)S(1)}, u32[]{:S(2)}, u32[]{:S(2)}) collective-permute-start(bf16[128,1024]{1,0:T(8,128)(2,1)S(1)} %bitcast.15), channel_id=1, source_target_pairs={{0,64},{64,128},{128,192},{192,0},{1,65},{65,129},{129,193},{193,1... | collective-permute-start | bytes 786440 | tf_op jit(solution)/shard_map/ppermute | solution.py:30
  24.8 8.1 %collective-permute-start.2 = (bf16[128,1024]{1,0:T(8,128)(2,1)S(1)}, bf16[128,1024]{1,0:T(8,128)(2,1)S(1)}, u32[]{:S(2)}, u32[]{:S(2)}) collective-permute-start(bf16[128,1024]{1,0:T(8,128)(2,1)S(1)} %bitcast.16), channel_id=1, source_target_pairs={{0,192},{64,0},{128,64},{192,128},{1,193},{65,1},{129,65},{193,129... | collective-permute-start | bytes 786440 | tf_op jit(solution)/shard_map/ppermute | solution.py:31
  32.1 6.3 %collective-permute-start.4 = (bf16[64,1024]{1,0:T(8,128)(2,1)S(1)}, bf16[64,1024]{1,0:T(8,128)(2,1)S(1)}, u32[]{:S(2)}, u32[]{:S(2)}) collective-permute-start(bf16[64,1024]{1,0:T(8,128)(2,1)S(1)} %slice.26), channel_id=1, source_target_pairs={{0,64},{64,128},{128,192},{192,0},{1,65},{65,129},{129,193},{193,1... | collective-permute-start | bytes 393224 | tf_op jit(solution)/shard_map/ppermute | solution.py:32
  32.9 6.1 %collective-permute-start.5 = (bf16[64,1024]{1,0:T(8,128)(2,1)S(1)}, bf16[64,1024]{1,0:T(8,128)(2,1)S(1)}, u32[]{:S(2)}, u32[]{:S(2)}) collective-permute-start(bf16[64,1024]{1,0:T(8,128)(2,1)S(1)} %slice.27), channel_id=1, source_target_pairs={{0,192},{64,0},{128,64},{192,128},{1,193},{65,1},{129,65},{193,129... | collective-permute-start | bytes 393224 | tf_op jit(solution)/shard_map/ppermute | solution.py:33
  40.4 34.3 %collective-permute-start.6 = (bf16[4,128,1024]{2,1,0:T(8,128)(2,1)}, bf16[4,128,1024]{2,1,0:T(8,128)(2,1)S(1)}, u32[]{:S(2)}, u32[]{:S(2)}) collective-permute-start(bf16[4,128,1024]{2,1,0:T(8,128)(2,1)} %bitcast.2.refs_1_), channel_id=1, source_target_pairs={{0,16},{16,32},{32,48},{48,0},{1,17},{17,33},{33,49},{49,1},{2,18}... | collective-permute-start | bytes 3145736 | tf_op jit(solution)/shard_map/ppermute | solution.py:127
  40.6 34.9 %collective-permute-start.7 = (bf16[4,128,1024]{2,1,0:T(8,128)(2,1)}, bf16[4,128,1024]{2,1,0:T(8,128)(2,1)}, u32[]{:S(2)}, u32[]{:S(2)}) collective-permute-start(bf16[4,128,1024]{2,1,0:T(8,128)(2,1)} %bitcast.2.refs_1_), channel_id=1, source_target_pairs={{0,48},{16,0},{32,16},{48,32},{1,49},{17,1},{33,17},{49,33},{2,50}... | collective-permute-start | bytes 3145736 | tf_op jit(solution)/shard_map/ppermute | solution.py:128
  43.7 13.9 %copy-start.7 = (bf16[384,1024]{1,0:T(8,128)(2,1)S(1)}, bf16[384,1024]{1,0:T(8,128)(2,1)}, u32[]{:S(2)}) copy-start(bf16[384,1024]{1,0:T(8,128)(2,1)} %copy-done.6) | copy-start | bytes 2359300
  43.7 38.3 %all-to-all-start.1 = ((bf16[128,3,1024]{2,1,0:T(4,128)(2,1)}), bf16[128,3,1024]{2,1,0:T(4,128)(2,1)}, u32[]{:S(2)}, u32[]{:S(2)}) async-start(bf16[128,3,1024]{2,1,0:T(4,128)(2,1)} %all_to_all.15), calls=%async_computation.1 | async-start | bytes 2097152 | tf_op jit(solution)/shard_map/all_to_all | solution.py:115
  57.6 32.6 %copy-start.1 = (bf16[384,1024]{1,0:T(8,128)(2,1)S(1)}, bf16[384,1024]{1,0:T(8,128)(2,1)}, u32[]{:S(2)}) copy-start(bf16[384,1024]{1,0:T(8,128)(2,1)} %refs_0_.1) | copy-start | bytes 2359300
  57.6 15.4 %collective-permute-start.8 = (bf16[192,1024]{1,0:T(8,128)(2,1)S(1)}, bf16[192,1024]{1,0:T(8,128)(2,1)S(1)}, u32[]{:S(2)}, u32[]{:S(2)}) collective-permute-start(bf16[192,1024]{1,0:T(8,128)(2,1)S(1)} %slice.20), channel_id=1, source_target_pairs={{0,64},{64,128},{128,192},{192,0},{1,65},{65,129},{129,193},{193,1... | collective-permute-start | bytes 1179656 | tf_op jit(solution)/shard_map/ppermute | solution.py:123
  60.4 14.3 %collective-permute-start.9 = (bf16[192,1024]{1,0:T(8,128)(2,1)S(1)}, bf16[192,1024]{1,0:T(8,128)(2,1)S(1)}, u32[]{:S(2)}, u32[]{:S(2)}) collective-permute-start(bf16[192,1024]{1,0:T(8,128)(2,1)S(1)} %slice.21), channel_id=1, source_target_pairs={{0,192},{64,0},{128,64},{192,128},{1,193},{65,1},{129,65},{193,129... | collective-permute-start | bytes 1179656 | tf_op jit(solution)/shard_map/ppermute | solution.py:124
  76.3 12.1 %collective-permute-start.10 = (bf16[2,128,1024]{2,1,0:T(8,128)(2,1)}, bf16[2,128,1024]{2,1,0:T(8,128)(2,1)}, u32[]{:S(2)}, u32[]{:S(2)}) collective-permute-start(bf16[2,128,1024]{2,1,0:T(8,128)(2,1)} %slice.22), channel_id=1, source_target_pairs={{0,16},{16,32},{32,48},{48,0},{1,17},{17,33},{33,49},{49,1},{2,18}... | collective-permute-start | bytes 1572872 | tf_op jit(solution)/shard_map/ppermute | solution.py:130
  78.6 11.6 %collective-permute-start.11 = (bf16[2,128,1024]{2,1,0:T(8,128)(2,1)}, bf16[2,128,1024]{2,1,0:T(8,128)(2,1)}, u32[]{:S(2)}, u32[]{:S(2)}) collective-permute-start(bf16[2,128,1024]{2,1,0:T(8,128)(2,1)} %slice.23), channel_id=1, source_target_pairs={{0,48},{16,0},{32,16},{48,32},{1,49},{17,1},{33,17},{49,33},{2,50}... | collective-permute-start | bytes 1572872 | tf_op jit(solution)/shard_map/ppermute | solution.py:131
  85.2 13.7 %copy-start.18 = (s32[384]{0:T(512)S(1)}, s32[384]{0:T(512)}, u32[]{:S(2)}) copy-start(s32[384]{0:T(512)} %param.15) | copy-start | bytes 4612
  98.1 7.8 %collective-permute-start.12 = (f32[384,2048]{1,0:T(8,128)}, f32[384,2048]{1,0:T(8,128)}, u32[]{:S(2)}, u32[]{:S(2)}) collective-permute-start(f32[384,2048]{1,0:T(8,128)} %get-tuple-element.34), channel_id=1, source_target_pairs={{0,1},{1,0},{2,3},{3,2},{4,5},{5,4},{6,7},{7,6},{8,9},{9,8},{10,11... | collective-permute-start | bytes 9437192 | tf_op jit(solution)/shard_map/ppermute | solution.py:145
  101.3 4.6 %copy-start.17 = (f32[2048]{0:T(1024)S(1)}, f32[2048]{0:T(1024)}, u32[]{:S(2)}) copy-start(f32[2048]{0:T(1024)} %param.10) | copy-start | bytes 24580
  105.4 4.6 %collective-permute-start.13 = (bf16[384,1024]{1,0:T(8,128)(2,1)S(1)}, bf16[384,1024]{1,0:T(8,128)(2,1)S(1)}, u32[]{:S(2)}, u32[]{:S(2)}) collective-permute-start(bf16[384,1024]{1,0:T(8,128)(2,1)S(1)} %broadcast_select_fusion), channel_id=1, source_target_pairs={{0,1},{1,0},{2,3},{3,2},{4,5},{5,4},{6,7},{7,6},{8,9},{9,8},{10,11... | collective-permute-start | bytes 2359304 | tf_op jit(solution)/shard_map/ppermute | solution.py:139
  111.2 5.3 %copy-start.13 = (bf16[192,1024]{1,0:T(8,128)(2,1)S(1)}, bf16[192,1024]{1,0:T(8,128)(2,1)}, u32[]{:S(2)}) copy-start(bf16[192,1024]{1,0:T(8,128)(2,1)} %copy-done.12) | copy-start | bytes 1179652
  111.2 5.4 %copy-start.11 = (bf16[192,1024]{1,0:T(8,128)(2,1)S(1)}, bf16[192,1024]{1,0:T(8,128)(2,1)}, u32[]{:S(2)}) copy-start(bf16[192,1024]{1,0:T(8,128)(2,1)} %copy-done.10) | copy-start | bytes 1179652
  112.9 16.5 %copy-start.5 = (bf16[384,2048]{1,0:T(8,128)(2,1)}, bf16[384,2048]{1,0:T(8,128)(2,1)S(1)}, u32[]{:S(2)}) copy-start(bf16[384,2048]{1,0:T(8,128)(2,1)S(1)} %multiply_convert_fusion) | copy-start | bytes 4718596
  112.9 12.3 %collective-permute-start.14 = (bf16[192,512]{1,0:T(8,128)(2,1)S(1)}, bf16[192,512]{1,0:T(8,128)(2,1)S(1)}, u32[]{:S(2)}, u32[]{:S(2)}) collective-permute-start(bf16[192,512]{1,0:T(8,128)(2,1)S(1)} %get-tuple-element.50), channel_id=1, source_target_pairs={{0,192},{64,0},{128,64},{192,128},{1,193},{65,1},{129,65},{193,129... | collective-permute-start | bytes 589832 | tf_op jit(solution)/shard_map/ppermute | solution.py:162
  116.6 9.4 %collective-permute-start.15 = (bf16[192,512]{1,0:T(8,128)(2,1)S(1)}, bf16[192,512]{1,0:T(8,128)(2,1)S(1)}, u32[]{:S(2)}, u32[]{:S(2)}) collective-permute-start(bf16[192,512]{1,0:T(8,128)(2,1)S(1)} %get-tuple-element.49), channel_id=1, source_target_pairs={{0,128},{64,192},{128,0},{192,64},{1,129},{65,193},{129,1},{193,65... | collective-permute-start | bytes 589832 | tf_op jit(solution)/shard_map/ppermute | solution.py:163
  116.7 12.2 %collective-permute-start.16 = (bf16[192,512]{1,0:T(8,128)(2,1)S(1)}, bf16[192,512]{1,0:T(8,128)(2,1)S(1)}, u32[]{:S(2)}, u32[]{:S(2)}) collective-permute-start(bf16[192,512]{1,0:T(8,128)(2,1)S(1)} %get-tuple-element.48), channel_id=1, source_target_pairs={{0,64},{64,128},{128,192},{192,0},{1,65},{65,129},{129,193},{193,1... | collective-permute-start | bytes 589832 | tf_op jit(solution)/shard_map/ppermute | solution.py:164
  128.9 2.3 %collective-permute-start.17 = (bf16[576,512]{1,0:T(8,128)(2,1)S(1)}, bf16[576,512]{1,0:T(8,128)(2,1)S(1)}, u32[]{:S(2)}, u32[]{:S(2)}) collective-permute-start(bf16[576,512]{1,0:T(8,128)(2,1)S(1)} %constant_dynamic-update-slice_fusion.5), channel_id=1, source_target_pairs={{0,1},{1,0},{2,3},{3,2},{4,5},{5,4},{6,7},{7,6},{8,9},{9,8},{10,11... | collective-permute-start | bytes 1769480 | tf_op jit(solution)/shard_map/ppermute | solution.py:166
  133.7 9.2 %collective-permute-start.18 = (bf16[128,1024]{1,0:T(8,128)(2,1)S(1)}, bf16[128,1024]{1,0:T(8,128)(2,1)S(1)}, u32[]{:S(2)}, u32[]{:S(2)}) collective-permute-start(bf16[128,1024]{1,0:T(8,128)(2,1)S(1)} %get-tuple-element.45), channel_id=1, source_target_pairs={{0,16},{16,32},{32,48},{48,0},{1,17},{17,33},{33,49},{49,1},{2,18}... | collective-permute-start | bytes 786440 | tf_op jit(solution)/shard_map/ppermute | solution.py:39
  133.8 10.8 %collective-permute-start.19 = (bf16[128,1024]{1,0:T(8,128)(2,1)S(1)}, bf16[128,1024]{1,0:T(8,128)(2,1)S(1)}, u32[]{:S(2)}, u32[]{:S(2)}) collective-permute-start(bf16[128,1024]{1,0:T(8,128)(2,1)S(1)} %get-tuple-element.47), channel_id=1, source_target_pairs={{0,32},{16,48},{32,0},{48,16},{1,33},{17,49},{33,1},{49,17},{2,34}... | collective-permute-start | bytes 786440 | tf_op jit(solution)/shard_map/ppermute | solution.py:38
  135.7 13.9 %collective-permute-start.20 = (bf16[128,1024]{1,0:T(8,128)(2,1)S(1)}, bf16[128,1024]{1,0:T(8,128)(2,1)S(1)}, u32[]{:S(2)}, u32[]{:S(2)}) collective-permute-start(bf16[128,1024]{1,0:T(8,128)(2,1)S(1)} %get-tuple-element.46), channel_id=1, source_target_pairs={{0,48},{16,0},{32,16},{48,32},{1,49},{17,1},{33,17},{49,33},{2,50}... | collective-permute-start | bytes 786440 | tf_op jit(solution)/shard_map/ppermute | solution.py:40
  151.5 17.5 %all-to-all-start.2 = ((bf16[8,16,1024]{2,1,0:T(8,128)(2,1)}), bf16[8,16,1024]{2,1,0:T(8,128)(2,1)S(1)}, u32[]{:S(2)}, u32[]{:S(2)}) async-start(bf16[8,16,1024]{2,1,0:T(8,128)(2,1)} %bitcast.5), calls=%async_computation.2 | async-start | bytes 524288 | tf_op jit(solution)/shard_map/all_to_all | solution.py:99
  (10 other events, 15.9 us)
